TPU v7x, 32 devices: a whole 2x2x4 slice. The times are simulated.
32 devices in a mesh: groups: 2 (over y), seq: 4 (over z), head: 2 (over x), mp: 2 (over core).
Axes of the slice: x: 2, y: 2, z: 4, core: 2. Of those that a mesh axis runs over, the one named last changes fastest.
Arguments:
- span_order: int32 [16], P('groups'), parts along dimension 0, may hold values from 0 to 7, as said below
- queries: bfloat16 [2048, 1024], P(('groups', 'seq'), ('head', 'mp')), parts along dimension 0, may hold values from -22 to 22
- keys: bfloat16 [2048, 1024], P(('groups', 'seq'), ('head', 'mp')), parts along dimension 0, may hold values from -22 to 22
- values: bfloat16 [2048, 1024], P(('groups', 'seq'), ('head', 'mp')), parts along dimension 0, may hold values from -6 to 6
- grad_out: bfloat16 [2048, 1024], P(('groups', 'seq'), ('head', 'mp')), parts along dimension 0, may hold values from -6 to 6
Outputs:
- attended: bfloat16 [2048, 1024], P(('groups', 'seq'), ('head', 'mp')), parts along dimension 0
- grad_queries: bfloat16 [2048, 1024], P(('groups', 'seq'), ('head', 'mp')), parts along dimension 0
- grad_keys: bfloat16 [2048, 1024], P(('groups', 'seq'), ('head', 'mp')), parts along dimension 0
- grad_values: bfloat16 [2048, 1024], P(('groups', 'seq'), ('head', 'mp')), parts along dimension 0
There are 2 independent parts, one for each index of `groups`. A program takes and returns all parts, laid end to end along the dimension named above; each array names one. Nothing has to cross between parts.
Inputs may be any that keep to these rules, and one draw needn't show every extreme that they name: span_order is a permutation; stored spans 2 s and 2 s + 1 have places p and 7 - p with p < 4.
All inputs are finite; a program needn't handle non-finite values.
Results may differ from a plain program's by a relative error of at most 0.023.
Values may be sent and summed in bfloat16 or wider, within the bound.
No kernel may reach another device: no remote copies, remote signals or barrier semaphores. Data moves between devices by JAX's collectives and lax.ppermute only.
A program may use at most 64 MiB of HBM per device.

v0:
```python
import jax
import jax.numpy as jnp
from jax import lax
from jax.sharding import PartitionSpec as P

HEAD_DIM = 128
SPAN = 128


def settle(values_in):
    return lax.optimization_barrier(values_in.astype(jnp.bfloat16)).astype(jnp.float32)


def masked_scores(query_block, key_block, query_pos, key_positions, factor):
    raw = (
        jnp.einsum("qhd,khd->hqk", query_block, key_block, preferred_element_type=jnp.float32)
        * factor
    )
    return jnp.where(key_positions[None, None, :] <= query_pos[None, :, None], raw, -jnp.inf)


def split_blocks(arrays, block_rows):
    count_blocks = arrays[0].shape[0] // block_rows
    stacked = tuple(
        (member.reshape((count_blocks, block_rows) + member.shape[1:]) for member in arrays)
    )
    starts = jnp.arange(count_blocks, dtype=jnp.int32) * block_rows
    return (stacked, starts)


def per_device(span_order, queries, keys, values, grad_out):
    q_rows, k_rows, v_rows, g_rows = (queries, keys, values, grad_out)
    my_rows = q_rows.shape[0]
    heads_here = q_rows.shape[1] // HEAD_DIM
    factor = HEAD_DIM ** (-0.5)
    total_rows = span_order.shape[0] * SPAN
    offsets = jnp.arange(total_rows, dtype=jnp.int32)
    all_pos = jnp.repeat(span_order, SPAN, total_repeat_length=total_rows) * SPAN + offsets % SPAN
    my_start = lax.axis_index("seq") * my_rows
    my_pos = lax.dynamic_slice_in_dim(all_pos, my_start, my_rows)
    my_q = q_rows.reshape(my_rows, heads_here, HEAD_DIM)
    my_k = k_rows.reshape(my_rows, heads_here, HEAD_DIM)
    my_v = v_rows.reshape(my_rows, heads_here, HEAD_DIM)
    my_g = g_rows.reshape(my_rows, heads_here, HEAD_DIM)

    def key_block_rows():
        return 512

    start_state = (
        jnp.full((heads_here, my_rows), -jnp.inf, jnp.float32),
        jnp.zeros((heads_here, my_rows), jnp.float32),
        jnp.zeros((heads_here, my_rows, HEAD_DIM), jnp.float32),
    )
    carry = start_state
    block_rows = key_block_rows()
    stacked, starts = split_blocks(
        (
            lax.all_gather(k_rows, "seq", axis=0, tiled=True),
            lax.all_gather(v_rows, "seq", axis=0, tiled=True),
        ),
        block_rows,
    )

    def forward_one_block(state, item):
        key_block, value_block, block_start = item
        key3 = key_block.reshape(block_rows, heads_here, HEAD_DIM)
        value3 = value_block.reshape(block_rows, heads_here, HEAD_DIM)
        positions = lax.dynamic_slice_in_dim(all_pos, block_start, block_rows)
        row_max, weight_sum, accum = state
        scores = masked_scores(my_q, key3, my_pos, positions, factor)
        new_max = jnp.maximum(row_max, jnp.max(scores, axis=2))
        safe_max = jnp.where(jnp.isfinite(new_max), new_max, 0.0)
        weights = jnp.exp(scores - safe_max[:, :, None])
        shrink = jnp.exp(row_max - safe_max)
        weight_sum = weight_sum * shrink + jnp.sum(weights, axis=2)
        accum = accum * shrink[:, :, None] + jnp.einsum(
            "hqk,khd->hqd", weights, value3.astype(jnp.float32)
        )
        return ((new_max, weight_sum, accum), None)

    carry, unused = lax.scan(forward_one_block, carry, stacked + (starts,))
    row_max, weight_sum, accum = carry
    lse_rows = (row_max + jnp.log(weight_sum)).T
    attended3 = jnp.transpose(accum / weight_sum[:, :, None], (1, 0, 2)).astype(jnp.bfloat16)
    delta_rows = jnp.sum(my_g.astype(jnp.float32) * attended3.astype(jnp.float32), axis=2)
    lse_all, delta_all = (
        lax.all_gather(lse_rows, "seq", axis=0, tiled=True),
        lax.all_gather(delta_rows, "seq", axis=0, tiled=True),
    )

    def pair_terms(
        q_block, g_block, lse_block, delta_block, q_pos, key_block, value_block, key_positions
    ):
        scores = masked_scores(q_block, key_block, q_pos, key_positions, factor)
        probs = jnp.exp(scores - lse_block.T[:, :, None])
        dprobs = jnp.einsum(
            "qhd,khd->hqk", g_block, value_block, preferred_element_type=jnp.float32
        )
        dscores = (probs * (dprobs - delta_block.T[:, :, None])).astype(jnp.bfloat16)
        return (probs.astype(jnp.bfloat16), dscores)

    def query_part(acc_q, key3, value3, positions):
        unused, dscores = pair_terms(
            my_q, my_g, lse_rows, delta_rows, my_pos, key3, value3, positions
        )
        return acc_q + jnp.einsum("hqk,khd->hqd", dscores, key3, preferred_element_type=jnp.float32)

    def key_part(acc_kv, q3, g3, block_start):
        positions = lax.dynamic_slice_in_dim(all_pos, block_start, my_rows)
        lse_block = lax.dynamic_slice_in_dim(lse_all, block_start, my_rows, 0)
        delta_block = lax.dynamic_slice_in_dim(delta_all, block_start, my_rows, 0)
        grad_k, grad_v = acc_kv
        probs_half, dscores = pair_terms(
            q3, g3, lse_block, delta_block, positions, my_k, my_v, my_pos
        )
        grad_k = grad_k + settle(
            jnp.einsum("hqk,qhd->khd", dscores, q3, preferred_element_type=jnp.float32) * factor
        )
        grad_v = grad_v + settle(
            jnp.einsum("hqk,qhd->khd", probs_half, g3, preferred_element_type=jnp.float32)
        )
        return (grad_k, grad_v)

    zeros_q = jnp.zeros((heads_here, my_rows, HEAD_DIM), jnp.float32)
    zeros_k = jnp.zeros((my_rows, heads_here, HEAD_DIM), jnp.float32)
    carry = zeros_q
    query_block_rows = key_block_rows()
    stacked, starts = split_blocks(
        (
            lax.all_gather(k_rows, "seq", axis=0, tiled=True),
            lax.all_gather(v_rows, "seq", axis=0, tiled=True),
        ),
        query_block_rows,
    )

    def query_one_block(state, item):
        key_block, value_block, block_start = item
        positions = lax.dynamic_slice_in_dim(all_pos, block_start, query_block_rows)
        key3 = key_block.reshape(query_block_rows, heads_here, HEAD_DIM)
        value3 = value_block.reshape(query_block_rows, heads_here, HEAD_DIM)
        return (query_part(state, key3, value3, positions), None)

    carry, unused = lax.scan(query_one_block, carry, stacked + (starts,))
    grad_q_acc = carry
    carry = (zeros_k, zeros_k)
    stacked, starts = split_blocks(
        (
            lax.all_gather(q_rows, "seq", axis=0, tiled=True),
            lax.all_gather(g_rows, "seq", axis=0, tiled=True),
        ),
        my_rows,
    )

    def key_one_block(state, item):
        query_block, cotangent_block, block_start = item
        q3 = query_block.reshape(my_rows, heads_here, HEAD_DIM)
        g3 = cotangent_block.reshape(my_rows, heads_here, HEAD_DIM)
        return (key_part(state, q3, g3, block_start), None)

    carry, unused = lax.scan(key_one_block, carry, stacked + (starts,))
    grad_k_acc, grad_v_acc = carry
    attended_rows = attended3.reshape(my_rows, heads_here * HEAD_DIM)
    grad_q_rows = (
        (jnp.transpose(grad_q_acc, (1, 0, 2)) * factor)
        .astype(jnp.bfloat16)
        .reshape(my_rows, heads_here * HEAD_DIM)
    )
    grad_k_rows = grad_k_acc.astype(jnp.bfloat16).reshape(my_rows, heads_here * HEAD_DIM)
    grad_v_rows = grad_v_acc.astype(jnp.bfloat16).reshape(my_rows, heads_here * HEAD_DIM)
    return (attended_rows, grad_q_rows, grad_k_rows, grad_v_rows)


def solution(mesh):
    placed = (
        P("groups"),
        P(("groups", "seq"), ("head", "mp")),
        P(("groups", "seq"), ("head", "mp")),
        P(("groups", "seq"), ("head", "mp")),
        P(("groups", "seq"), ("head", "mp")),
    )
    return jax.shard_map(
        per_device,
        mesh=mesh,
        in_specs=placed,
        out_specs=(
            P(("groups", "seq"), ("head", "mp")),
            P(("groups", "seq"), ("head", "mp")),
            P(("groups", "seq"), ("head", "mp")),
            P(("groups", "seq"), ("head", "mp")),
        ),
        check_vma=False,
    )
```

profile of v0, /device:TPU:0, one launch (start us, length us, event | category | flops | bytes accessed | tf_op | source)
XLA Modules:
  0.0 140.2 jit_solution(13896386660994476989)
XLA Ops:
  0.6 1.0 copy.91
  1.8 0.6 copy-done.6
  2.4 0.7 fusion.36
  3.1 4.4 %compare_select_fusion.1 = s32[1024,1]{0,1:T(1,128)S(1)} fusion(s32[]{:T(128)} %bitcast.5, s32[]{:T(128)} %bitcast.6, s32[]{:T(128)} %bitcast.7, s32[]{:T(128)} %bitcast.8, s32[]{:T(128)} %bitcast.9, s32[]{:T(128)} %bitcast.11, s32[]{:T(128)} %bitcast.10, s32[1024,1]{0,1:T(1,128)S(1)} %bitcast.177, s32[1024,1]{0,1:T(1,128)S(1)} %bitcast.179), kind=kLoop, calls=%fused_computation.60 | loop fusion | flops 14336 | bytes 12316 | tf_op jit(solution)/shard_map/jit(_take)/gather | solution.py:38
  7.5 0.7 fusion.27
  8.2 17.3 %all_gather.20 = bf16[1024,256]{1,0:T(8,128)(2,1)S(1)} all-gather(bf16[256,256]{1,0:T(8,128)(2,1)S(1)} %copy-done.1), channel_id=1, replica_groups=mesh['groups'=2,'seq'=4,'head'=2,'mp'=2] {'seq'}, dimensions={0}, use_global_device_ids=true | all-gather | bytes 655360 | tf_op jit(solution)/shard_map/all_gather | solution.py:58
  25.8 0.7 copy-done
  26.7 0.8 copy-done.3
  27.5 16.3 %all_gather.21 = bf16[1024,256]{1,0:T(8,128)(2,1)S(1)} all-gather(bf16[256,256]{1,0:T(8,128)(2,1)S(1)} %copy-done.3), channel_id=1, replica_groups=mesh['groups'=2,'seq'=4,'head'=2,'mp'=2] {'seq'}, dimensions={0}, use_global_device_ids=true | all-gather | bytes 655360 | tf_op jit(solution)/shard_map/all_gather | solution.py:59
  44.0 7.7 %while.40 = (s32[]{:T(128)}, f32[2,256]{1,0:T(2,128)S(1)}, f32[2,256]{1,0:T(2,128)S(1)}, f32[2,256,128]{2,1,0:T(8,128)S(1)}, s32[2]{0:T(128)S(1)}, /*index=5*/s3...) while((s32[]{:T(128)}, f32[2,256]{1,0:T(2,128)S(1)}, ...), condition=%wide.region_3.4_spmd.clone, body=%wide.region_0.3_spmd.clone.sunk | while | flops 136122880 | bytes 5678279 | solution.py:81
  44.0 0.6 dynamic_slice.85
  47.9 0.6 dynamic_slice.85
  51.8 0.6 multiply_reduce_fusion
  52.4 0.8 copy.105
  53.2 0.6 log_add_fusion
  54.4 11.2 %while.41 = (s32[]{:T(128)}, f32[2,256,128]{2,1,0:T(8,128)S(1)}, s32[2]{0:T(128)S(1)}, s32[1024]{0:T(1024)S(1)}, s32[256]{0:T(256)S(1)}, /*index=5*/bf16[2,512,2...) while((s32[]{:T(128)}, f32[2,256,128]{2,1,0:T(8,128)S(1)}, ...), condition=%wide.region_6.7_spmd.clone, body=%wide.region_5.6_spmd.clone.sunk | while | flops 203161600 | bytes 5000545 | solution.py:143
  58.7 0.7 fusion.87
  59.4 0.6 copy-done.10
  64.3 0.7 fusion.87
  65.0 0.6 copy-done.10
  65.6 0.7 copy_bitcast_fusion
  66.3 15.5 %all_gather.22 = bf16[1024,256]{1,0:T(8,128)(2,1)S(1)} all-gather(bf16[256,256]{1,0:T(8,128)(2,1)S(1)} %copy-done), channel_id=1, replica_groups=mesh['groups'=2,'seq'=4,'head'=2,'mp'=2] {'seq'}, dimensions={0}, use_global_device_ids=true | all-gather | bytes 655360 | tf_op jit(solution)/shard_map/all_gather | solution.py:148
  82.6 11.9 %all_gather.23 = f32[1024,2]{0,1:T(2,128)S(1)} all-gather(f32[256,2]{0,1:T(2,128)S(1)} %bitcast.181), channel_id=1, replica_groups=mesh['groups'=2,'seq'=4,'head'=2,'mp'=2] {'seq'}, dimensions={0}, use_global_device_ids=true | all-gather | bytes 10240 | tf_op jit(solution)/shard_map/all_gather | solution.py:87
  94.5 14.9 %all_gather.24 = bf16[1024,256]{1,0:T(8,128)(2,1)S(1)} all-gather(bf16[256,256]{1,0:T(8,128)(2,1)S(1)} %copy-done.2), channel_id=1, replica_groups=mesh['groups'=2,'seq'=4,'head'=2,'mp'=2] {'seq'}, dimensions={0}, use_global_device_ids=true | all-gather | bytes 655360 | tf_op jit(solution)/shard_map/all_gather | solution.py:149
  109.6 11.9 %all_gather.25 = f32[1024,2]{0,1:T(2,128)S(1)} all-gather(f32[256,2]{0,1:T(2,128)S(1)} %get-tuple-element.889), channel_id=1, replica_groups=mesh['groups'=2,'seq'=4,'head'=2,'mp'=2] {'seq'}, dimensions={0}, use_global_device_ids=true | all-gather | bytes 10240 | tf_op jit(solution)/shard_map/all_gather | solution.py:88
  121.5 17.2 %while.42 = (s32[]{:T(128)}, f32[256,2,128]{0,2,1:T(8,128)S(1)}, f32[256,2,128]{0,2,1:T(8,128)S(1)}, bf16[4,256,256]{2,1,0:T(8,128)(2,1)S(1)}, s32[256]{0:T(256)...) while((s32[]{:T(128)}, f32[256,2,128]{0,2,1:T(8,128)S(1)}, ...), condition=%wide.region_8.9_spmd.clone, body=%wide.region_7.8_spmd.clone.sunk | while | flops 135790592 | bytes 5128417 | solution.py:160
  121.7 0.6 dynamic_slice.94
  126.0 0.6 dynamic_slice.94
  130.3 0.6 dynamic_slice.94
  134.6 0.6 dynamic_slice.94
  138.7 0.8 copy.115
  139.5 0.8 copy.116
  (123 shorter events, 16.4 us)
Async XLA Ops:
  0.6 7.6 %copy-start.1 = (bf16[256,256]{1,0:T(8,128)(2,1)S(1)}, bf16[256,256]{1,0:T(8,128)(2,1)}, u32[]{:S(2)}) copy-start(bf16[256,256]{1,0:T(8,128)(2,1)} %param.15) | copy-start | bytes 393220
  1.7 0.7 copy-start.6
  25.6 0.9 copy-start
  26.6 0.9 copy-start.3
  53.8 0.7 copy-start.5
  54.4 0.5 copy-start.9
  57.6 0.7 copy-start.7
  59.4 0.6 copy-start.10
  60.0 0.5 copy-start.9
  63.2 0.7 copy-start.7
  65.0 0.6 copy-start.10
  81.9 0.7 copy-start.8
  81.9 12.6 %copy-start.2 = (bf16[256,256]{1,0:T(8,128)(2,1)S(1)}, bf16[256,256]{1,0:T(8,128)(2,1)}, u32[]{:S(2)}) copy-start(bf16[256,256]{1,0:T(8,128)(2,1)} %param.17) | copy-start | bytes 393220
  94.5 14.9 %copy-start.4 = (bf16[256,256]{1,0:T(8,128)(2,1)S(1)}, bf16[256,256]{1,0:T(8,128)(2,1)}, u32[]{:S(2)}) copy-start(bf16[256,256]{1,0:T(8,128)(2,1)} %param.16) | copy-start | bytes 393220
where the time goes:
time: 141 us; the launch traced here: 140 us
  blocking collectives  87.8 us (62%)
  local copies, waits for them, and re-layouts  18.9 us (13%)
  loops' own time  16.1 us (11%)
  other arithmetic  9.09 us (6%)
  matrix products  7.54 us (5%)
    all_gather x1, blocking collectives, per_device(): lax.all_gather(k_rows, 'seq', axis=0, tiled=True)  17.3 us
    all_gather x1, blocking collectives, per_device(): lax.all_gather(v_rows, 'seq', axis=0, tiled=True)  16.3 us
    all_gather x1, blocking collectives, per_device(): lax.all_gather(q_rows, 'seq', axis=0, tiled=True)  15.5 us
    all_gather x1, blocking collectives, per_device(): lax.all_gather(g_rows, 'seq', axis=0, tiled=True)  14.9 us
    all_gather x1, blocking collectives, per_device(): lax.all_gather(lse_rows, 'seq', axis=0, tiled=True)  11.9 us
    all_gather x1, blocking collectives, per_device(): lax.all_gather(delta_rows, 'seq', axis=0, tiled=True)  11.9 us
    another operation x1, loops' own time, per_device(): carry, unused = lax.scan(key_one_block, carry, stacked + (starts,))  8.11 us
    unnamed x27, local copies, waits for them, and re-layouts  6.19 us

commit v1 on v0

--- a/solution.py
+++ b/solution.py
@@ -1,6 +1,10 @@
+import functools
+
 import jax
 import jax.numpy as jnp
 from jax import lax
+from jax.experimental import pallas as pl
+from jax.experimental.pallas import tpu as pltpu
 from jax.sharding import PartitionSpec as P
 
 HEAD_DIM = 128
@@ -28,7 +32,7 @@
     return (stacked, starts)
 
 
-def per_device(span_order, queries, keys, values, grad_out):
+def gathered_per_device(span_order, queries, keys, values, grad_out):
     q_rows, k_rows, v_rows, g_rows = (queries, keys, values, grad_out)
     my_rows = q_rows.shape[0]
     heads_here = q_rows.shape[1] // HEAD_DIM
@@ -170,23 +174,160 @@
     return (attended_rows, grad_q_rows, grad_k_rows, grad_v_rows)
 
 
+F32=jnp.float32; BF=jnp.bfloat16
+NN=(((1,),(0,)),((),())); NT=(((1,),(1,)),((),()))
+def dot(a,b,dims): return lax.dot_general(a,b,dims,preferred_element_type=F32)
+
+def owner_kernel(rows, blk, order_ref, ids_ref, own, sa, sb, sc, o_own, o_a, o_b, o_c,
+                 q, k, v, g, kt, vt, s, dk, dv):
+    ins=(own,sa,sb,sc); outs=(o_own,o_a,o_b,o_c)
+    sh=own.shape[0]//4
+    per=sh//SPAN
+    total=4*sh
+    factor=HEAD_DIM**-0.5
+    c=factor*1.4426950408889634
+    place=[]
+    for t in range(4):
+        for e in range(per):
+            p=pl.multiple_of(order_ref[ids_ref[t]*per+e]*SPAN,SPAN)
+            place.append((t,e,p))
+    @pl.when(ids_ref[4]==1)
+    def _():
+        for t,e,p in place:
+            for n,dst in enumerate((q,k,v,g)):
+                dst[pl.ds(p,SPAN),:]=ins[t][n*sh+e*SPAN:n*sh+(e+1)*SPAN,:]
+        nb=total//blk
+        for j in range(nb):
+            r=slice(j*blk,(j+1)*blk)
+            kt[:,r]=k[r,:].T
+            vt[:,r]=v[r,:].T
+        dk[...]=jnp.zeros_like(dk); dv[...]=jnp.zeros_like(dv)
+        ki=lax.broadcasted_iota(jnp.int32,(blk,blk),0); qi=lax.broadcasted_iota(jnp.int32,(blk,blk),1)
+        for i in range(nb):
+            ri=slice(i*blk,(i+1)*blk)
+            qb=q[ri,:]
+            m=None
+            for j in range(i+1):
+                rj=slice(j*blk,(j+1)*blk)
+                sj=dot(k[rj,:],qb,NT)*c
+                if j==i: sj=jnp.where(ki<=qi,sj,-1e30)
+                s[rj,:]=sj
+                mj=jnp.max(sj,axis=0,keepdims=True)
+                m=mj if m is None else jnp.maximum(m,mj)
+            l=None; ot=None
+            for j in range(i+1):
+                rj=slice(j*blk,(j+1)*blk)
+                p=jnp.exp2(s[rj,:]-m)
+                s[rj,:]=p
+                lj=jnp.sum(p,axis=0,keepdims=True)
+                oj=dot(vt[:,rj],p.astype(BF),NN)
+                l=lj if l is None else l+lj
+                ot=oj if ot is None else ot+oj
+            rinv=1.0/l
+            ob=(ot*rinv).astype(BF)
+            gt=g[ri,:].T.astype(F32)*rinv
+            gnt=gt.astype(BF)
+            delta=jnp.sum(gt*ob.astype(F32),axis=0,keepdims=True)
+            dqt=None
+            for j in range(i+1):
+                rj=slice(j*blk,(j+1)*blk)
+                dp=dot(v[rj,:],gnt,NN)
+                p=s[rj,:]
+                ds=(p*(dp-delta)).astype(BF)
+                dv[rj,:]+=dot(p.astype(BF),gnt,NT)
+                dk[rj,:]+=dot(ds,qb,NN)
+                dj=dot(kt[:,rj],ds,NN)
+                dqt=dj if dqt is None else dqt+dj
+            q[ri,:]=(dqt*factor).astype(BF).T
+            g[ri,:]=ob.T
+        for t,e,p in place:
+            outs[t][0*sh+e*SPAN:0*sh+(e+1)*SPAN,:]=g[pl.ds(p,SPAN),:]
+            outs[t][1*sh+e*SPAN:1*sh+(e+1)*SPAN,:]=q[pl.ds(p,SPAN),:]
+            outs[t][2*sh+e*SPAN:2*sh+(e+1)*SPAN,:]=(dk[pl.ds(p,SPAN),:]*factor).astype(BF)
+            outs[t][3*sh+e*SPAN:3*sh+(e+1)*SPAN,:]=dv[pl.ds(p,SPAN),:].astype(BF)
+
+def owner_call(order, ids, own, sa, sb, sc, blk=256):
+    sh=own.shape[0]//4; total=4*sh
+    vm=pl.BlockSpec(memory_space=pltpu.VMEM); sm=pl.BlockSpec(memory_space=pltpu.SMEM)
+    return pl.pallas_call(
+        functools.partial(owner_kernel,total,blk),
+        out_shape=tuple(jax.ShapeDtypeStruct(own.shape,BF) for _ in range(4)),
+        in_specs=[sm,sm,vm,vm,vm,vm], out_specs=(vm,)*4,
+        scratch_shapes=[pltpu.VMEM((total,HEAD_DIM),BF)]*4+[pltpu.VMEM((HEAD_DIM,total),BF)]*2+
+            [pltpu.VMEM((total,blk),F32)]+[pltpu.VMEM((total,HEAD_DIM),F32)]*2,
+        compiler_params=pltpu.CompilerParams(vmem_limit_bytes=32<<20),
+        name="owner",
+    )(order,ids,own,sa,sb,sc)
+
+
+def pack_kernel(side_ref, q, k, v, g, near, far):
+    sh = q.shape[0]
+    for s in range(2):
+        @pl.when(side_ref[0] == s)
+        def _():
+            for n, src in enumerate((q, k, v, g)):
+                near[n * sh:(n + 1) * sh, :] = src[:, s * HEAD_DIM:(s + 1) * HEAD_DIM]
+                far[n * sh:(n + 1) * sh, :] = src[:, (1 - s) * HEAD_DIM:(2 - s) * HEAD_DIM]
+
+
+def unpack_kernel(side_ref, own, ra, rb, rc, *outs):
+    sh = outs[0].shape[0]
+    for s in range(2):
+        for owner in range(2):
+            @pl.when((side_ref[0] == s) & (side_ref[1] == owner))
+            def _():
+                near, far = (own, rb) if owner else (ra, rc)
+                for n, dst in enumerate(outs):
+                    dst[:, s * HEAD_DIM:(s + 1) * HEAD_DIM] = near[n * sh:(n + 1) * sh, :]
+                    dst[:, (1 - s) * HEAD_DIM:(2 - s) * HEAD_DIM] = far[n * sh:(n + 1) * sh, :]
+
+
+def owned_per_device(span_order, queries, keys, values, grad_out):
+    rows = queries.shape[0]
+    me = lax.axis_index("seq")
+    side = jnp.where(me < 2, 0, 1)
+    owner = jnp.where((me == 1) | (me == 2), 1, 0)
+    near_outer = 3 * side
+    ids = jnp.stack([me, near_outer, 3 - me, 3 - near_outer, owner]).astype(jnp.int32)
+    flags = jnp.stack([side, owner]).astype(jnp.int32)
+    vm = pl.BlockSpec(memory_space=pltpu.VMEM)
+    sm = pl.BlockSpec(memory_space=pltpu.SMEM)
+    near, far = pl.pallas_call(
+        pack_kernel,
+        out_shape=(jax.ShapeDtypeStruct((4 * rows, HEAD_DIM), BF),) * 2,
+        in_specs=[sm] + [vm] * 4,
+        out_specs=(vm, vm),
+        name="pack",
+    )(flags, queries, keys, values, grad_out)
+    go = lambda x, pairs: lax.ppermute(x, "seq", pairs)
+    ga = go(near, [(0, 1), (3, 2)])
+    gb = go(far, [(1, 2), (2, 1)])
+    gc = go(far, [(0, 2), (3, 1)])
+    own, to_a, to_b, to_c = owner_call(span_order, ids, near, ga, gb, gc, blk=512)
+    rb = go(to_b, [(1, 2), (2, 1)])
+    rc = go(to_c, [(1, 3), (2, 0)])
+    ra = go(to_a, [(1, 0), (2, 3)])
+    return pl.pallas_call(
+        unpack_kernel,
+        out_shape=(jax.ShapeDtypeStruct(queries.shape, BF),) * 4,
+        in_specs=[sm] + [vm] * 4,
+        out_specs=(vm,) * 4,
+        name="unpack",
+    )(flags, own, ra, rb, rc)
+
+
 def solution(mesh):
-    placed = (
-        P("groups"),
-        P(("groups", "seq"), ("head", "mp")),
-        P(("groups", "seq"), ("head", "mp")),
-        P(("groups", "seq"), ("head", "mp")),
-        P(("groups", "seq"), ("head", "mp")),
-    )
-    return jax.shard_map(
-        per_device,
-        mesh=mesh,
-        in_specs=placed,
-        out_specs=(
-            P(("groups", "seq"), ("head", "mp")),
-            P(("groups", "seq"), ("head", "mp")),
-            P(("groups", "seq"), ("head", "mp")),
-            P(("groups", "seq"), ("head", "mp")),
-        ),
-        check_vma=False,
-    )
+    rows_columns = P(("groups", "seq"), ("head", "mp"))
+
+    def run(span_order, queries, keys, values, grad_out):
+        heads_here = queries.shape[1] // HEAD_DIM // (mesh.shape["head"] * mesh.shape["mp"])
+        small = mesh.shape["seq"] == 4 and heads_here == 2
+        return jax.shard_map(
+            owned_per_device if small else gathered_per_device,
+            mesh=mesh,
+            in_specs=(P("groups"),) + (rows_columns,) * 4,
+            out_specs=(rows_columns,) * 4,
+            check_vma=False,
+        )(span_order, queries, keys, values, grad_out)
+
+    return run

time: 141 us -> 48.2 us (0.34)
  blocking collectives: 87.8 us -> 0 us
  waiting for transfers between devices: 0 us -> 28.3 us
  local copies, waits for them, and re-layouts: 18.9 us -> 2.44 us
  loops' own time: 16.1 us -> 0 us
  starting transfers between devices: 0 us -> 11.2 us
  other arithmetic: 9.09 us -> 0.58 us
  matrix products: 7.54 us -> 0 us
  Pallas kernels: 0 us -> 4.66 us
    all_gather x6 -> x0, blocking collectives: 87.8 us -> none  [the longest x1 17.3 us: per_device(): lax.all_gather(k_rows, 'seq', axis=0, tiled=True)]
    ppermute x0 -> x6, waiting for transfers between devices: none -> 28.3 us  [owned_per_device(): go = lambda x, pairs: lax.ppermute(x, 'seq', pairs)]
    another operation x3 -> x0, loops' own time: 16.1 us -> none  [the longest x1 8.11 us: per_device(): carry, unused = lax.scan(key_one_block, carry, stacked + (starts,))]
    ppermute x0 -> x6, starting transfers between devices: none -> 11.2 us  [owned_per_device(): go = lambda x, pairs: lax.ppermute(x, 'seq', pairs)]
    dot_general x20 -> x0, matrix products: 7.54 us -> none  [the longest x8 2.84 us: masked_scores(): jnp.einsum('qhd,khd->hqk', query_block, key_block, preferred_element_type...]
    dynamic_slice x37 -> x0, local copies, waits for them, and re-layouts: 6.45 us -> none  [the longest x20 3.27 us: per_device(): carry, unused = lax.scan(key_one_block, carry, stacked + (starts,))]
    pallas_call x0 -> x3, Pallas kernels: none -> 4.66 us  [the longest x1 2.1 us: owned_per_device(): pl.pallas_call(unpack_kernel, out_shape=(jax.ShapeDtypeStruct(queries.sha...]
    gather x2 -> x0, other arithmetic: 4.41 us -> none  [per_device(): jnp.repeat(span_order, SPAN, total_repeat_length=total_rows) * SPAN]
  transfers between devices with their start and end apart: 0 -> 6, of which waited for: 0 -> 4; matrix products, arithmetic and copies ran while one was open for 0% -> 0% of each run, Pallas kernels for 0% -> 0%
where the time goes in v1:
time: 48.2 us; the launch traced here: 47.9 us
  waiting for transfers between devices  28.3 us (59%)
  starting transfers between devices  11.2 us (23%)
  Pallas kernels  4.66 us (10%)
  local copies, waits for them, and re-layouts  2.44 us (5%)
  between operations  0.74 us (2%)
  other arithmetic  0.58 us (1%)
    ppermute x6, waiting for transfers between devices, owned_per_device(): go = lambda x, pairs: lax.ppermute(x, 'seq', pairs)  28.3 us
    ppermute x6, starting transfers between devices, owned_per_device(): go = lambda x, pairs: lax.ppermute(x, 'seq', pairs)  11.2 us
    unnamed x12, local copies, waits for them, and re-layouts  2.36 us
    pallas_call x1, Pallas kernels, owned_per_device(): pl.pallas_call(unpack_kernel, out_shape=(jax.ShapeDtypeStruct(queries.sha...  2.1 us
    pallas_call x1, Pallas kernels, owned_per_device(): pl.pallas_call(pack_kernel, out_shape=(jax.ShapeDtypeStruct((4 * rows, HE...  2 us
  transfers between devices with their start and end apart: 6, of which 4 were waited for; matrix products, arithmetic and copies ran while one was open for 0% of the time, Pallas kernels for 0%

profile of v1, /device:TPU:0, one launch (start us, length us, event | category | flops | bytes accessed | tf_op | source)
XLA Modules:
  0.0 47.9 jit_solution(16545432841825028190)
XLA Ops:
  0.6 0.6 %pad_add_fusion.side_ref = s32[2]{0:T(128)} fusion(s32[1]{0:T(128)} %bitcast.1, s32[1]{0:T(128)} %bitcast), kind=kLoop, calls=%fused_computation | loop fusion | flops 2 | bytes 16 | tf_op jit(solution)/shard_map/stack | solution.py:292
  1.2 2.0 %pack.1 = (bf16[1024,128]{1,0:T(8,128)(2,1)}, bf16[1024,128]{1,0:T(8,128)(2,1)}) custom-call(s32[2]{0:T(128)} %pad_add_fusion.side_ref, bf16[256,256]{1,0:T(8,128)(2,1)} %q.1, bf16[256,256]{1,0:T(8,128)(2,1)} %k.1, bf16[256,256]{1,0:T(8,128)(2,1)} %v.1, bf16[256,256]{1,0:T(8,128)(2,1)} %g.1), custom_call_target="tpu_custom_call" | custom-call | tf_op jit(solution)/shard_map/pack/pallas_call | solution.py:295
  3.2 4.9 %collective-permute-start = (bf16[1024,128]{1,0:T(8,128)(2,1)}, bf16[1024,128]{1,0:T(8,128)(2,1)S(1)}, u32[]{:S(2)}, u32[]{:S(2)}) collective-permute-start(bf16[1024,128]{1,0:T(8,128)(2,1)} %get-tuple-element.10.own), channel_id=1, source_target_pairs={{0,4},{12,8},{1,5},{13,9},{2,6},{14,10},{3,7},{15,11},{16,20},{28,... | collective-permute-start | bytes 786440 | tf_op jit(solution)/shard_map/ppermute | solution.py:302
  8.2 2.3 %collective-permute-start.2 = (bf16[1024,128]{1,0:T(8,128)(2,1)}, bf16[1024,128]{1,0:T(8,128)(2,1)S(1)}, u32[]{:S(2)}, u32[]{:S(2)}) collective-permute-start(bf16[1024,128]{1,0:T(8,128)(2,1)} %get-tuple-element.11), channel_id=1, source_target_pairs={{0,8},{12,4},{1,9},{13,5},{2,10},{14,6},{3,11},{15,7},{16,24},{28,... | collective-permute-start | bytes 786440 | tf_op jit(solution)/shard_map/ppermute | solution.py:302
  10.5 0.7 %collective-permute-start.1 = (bf16[1024,128]{1,0:T(8,128)(2,1)}, bf16[1024,128]{1,0:T(8,128)(2,1)S(1)}, u32[]{:S(2)}, u32[]{:S(2)}) collective-permute-start(bf16[1024,128]{1,0:T(8,128)(2,1)} %get-tuple-element.11), channel_id=1, source_target_pairs={{4,8},{8,4},{5,9},{9,5},{6,10},{10,6},{7,11},{11,7},{20,24},{24,20... | collective-permute-start | bytes 786440 | tf_op jit(solution)/shard_map/ppermute | solution.py:302
  11.2 0.0 copy-start.2
  11.2 0.1 stack.32.ids_ref
  11.3 3.9 %collective-permute-done.sa = bf16[1024,128]{1,0:T(8,128)(2,1)S(1)} collective-permute-done((bf16[1024,128]{1,0:T(8,128)(2,1)}, bf16[1024,128]{1,0:T(8,128)(2,1)S(1)}, u32[]{:S(2)}, u32[]{:S(2)}) %collective-permute-start) | collective-permute-done | bytes 262176 | tf_op jit(solution)/shard_map/ppermute | solution.py:302
  15.2 4.5 %collective-permute-done.2.sc = bf16[1024,128]{1,0:T(8,128)(2,1)S(1)} collective-permute-done((bf16[1024,128]{1,0:T(8,128)(2,1)}, bf16[1024,128]{1,0:T(8,128)(2,1)S(1)}, u32[]{:S(2)}, u32[]{:S(2)}) %collective-permute-start.2) | collective-permute-done | bytes 262176 | tf_op jit(solution)/shard_map/ppermute | solution.py:302
  19.7 0.0 collective-permute-done.1.sb
  19.7 0.0 copy-done.2
  19.7 0.0 copy-start
  19.7 0.9 %copy-done = bf16[1024,128]{1,0:T(8,128)(2,1)S(1)} copy-done((bf16[1024,128]{1,0:T(8,128)(2,1)S(1)}, bf16[1024,128]{1,0:T(8,128)(2,1)}, u32[]{:S(2)}) %copy-start) | copy-done | bytes 262168
  20.6 0.6 %owner.1 = (bf16[1024,128]{1,0:T(8,128)(2,1)S(1)}, bf16[1024,128]{1,0:T(8,128)(2,1)S(1)}, bf16[1024,128]{1,0:T(8,128)(2,1)S(1)}, bf16[1024,128]{1,0:T(8,128)(2,1)S(1)}) custom-call(s32[8]{0:T(128)S(1)} %copy-done.2, s32[5]{0:T(128)S(1)} %stack.32.ids_ref, bf16[1024,128]{1,0:T(8,128)(2,1)S(1)} %copy-done, bf16[1024,128]{1,0:T(8,128)(2,1)S(1)} %collective-permute-done.sa, ...), custom_call_target="tpu_custom_call" | custom-call | tf_op jit(solution)/shard_map/owner/pallas_call | solution.py:252
  21.2 0.0 copy-start.1
  21.2 0.7 %copy-done.1 = bf16[1024,128]{1,0:T(8,128)(2,1)} copy-done((bf16[1024,128]{1,0:T(8,128)(2,1)}, bf16[1024,128]{1,0:T(8,128)(2,1)S(1)}, u32[]{:S(2)}) %copy-start.1) | copy-done | bytes 262168
  21.9 1.3 %collective-permute-start.3 = (bf16[1024,128]{1,0:T(8,128)(2,1)S(1)}, bf16[1024,128]{1,0:T(8,128)(2,1)S(1)}, u32[]{:S(2)}, u32[]{:S(2)}) collective-permute-start(bf16[1024,128]{1,0:T(8,128)(2,1)S(1)} %get-tuple-element.13), channel_id=1, source_target_pairs={{4,0},{8,12},{5,1},{9,13},{6,2},{10,14},{7,3},{11,15},{20,16},{24,... | collective-permute-start | bytes 786440 | tf_op jit(solution)/shard_map/ppermute | solution.py:302
  23.2 0.7 %collective-permute-start.4 = (bf16[1024,128]{1,0:T(8,128)(2,1)S(1)}, bf16[1024,128]{1,0:T(8,128)(2,1)S(1)}, u32[]{:S(2)}, u32[]{:S(2)}) collective-permute-start(bf16[1024,128]{1,0:T(8,128)(2,1)S(1)} %get-tuple-element.14), channel_id=1, source_target_pairs={{4,8},{8,4},{5,9},{9,5},{6,10},{10,6},{7,11},{11,7},{20,24},{24,20... | collective-permute-start | bytes 786440 | tf_op jit(solution)/shard_map/ppermute | solution.py:302
  23.9 1.3 %collective-permute-start.5 = (bf16[1024,128]{1,0:T(8,128)(2,1)S(1)}, bf16[1024,128]{1,0:T(8,128)(2,1)S(1)}, u32[]{:S(2)}, u32[]{:S(2)}) collective-permute-start(bf16[1024,128]{1,0:T(8,128)(2,1)S(1)} %get-tuple-element.15), channel_id=1, source_target_pairs={{4,12},{8,0},{5,13},{9,1},{6,14},{10,2},{7,15},{11,3},{20,28},{24,... | collective-permute-start | bytes 786440 | tf_op jit(solution)/shard_map/ppermute | solution.py:302
  25.2 11.2 %collective-permute-done.3.ra = bf16[1024,128]{1,0:T(8,128)(2,1)S(1)} collective-permute-done((bf16[1024,128]{1,0:T(8,128)(2,1)S(1)}, bf16[1024,128]{1,0:T(8,128)(2,1)S(1)}, u32[]{:S(2)}, u32[]{:S(2)}) %collective-permute-start.3) | collective-permute-done | bytes 262176 | tf_op jit(solution)/shard_map/ppermute | solution.py:302
  36.4 0.0 copy-start.3
  36.4 0.0 collective-permute-done.4.rb
  36.4 0.0 copy-start.4
  36.4 8.7 %collective-permute-done.5.rc = bf16[1024,128]{1,0:T(8,128)(2,1)S(1)} collective-permute-done((bf16[1024,128]{1,0:T(8,128)(2,1)S(1)}, bf16[1024,128]{1,0:T(8,128)(2,1)S(1)}, u32[]{:S(2)}, u32[]{:S(2)}) %collective-permute-start.5) | collective-permute-done | bytes 262176 | tf_op jit(solution)/shard_map/ppermute | solution.py:302
  45.1 0.0 copy-start.5
  45.1 0.0 copy-done.3
  45.1 0.0 copy-done.4
  45.1 0.7 %copy-done.5 = bf16[1024,128]{1,0:T(8,128)(2,1)} copy-done((bf16[1024,128]{1,0:T(8,128)(2,1)}, bf16[1024,128]{1,0:T(8,128)(2,1)S(1)}, u32[]{:S(2)}) %copy-start.5) | copy-done | bytes 262168
  45.8 2.1 %unpack.1 = (bf16[256,256]{1,0:T(8,128)(2,1)}, bf16[256,256]{1,0:T(8,128)(2,1)}, bf16[256,256]{1,0:T(8,128)(2,1)}, bf16[256,256]{1,0:T(8,128)(2,1)}) custom-call(s32[2]{0:T(128)} %pad_add_fusion.side_ref, bf16[1024,128]{1,0:T(8,128)(2,1)} %copy-done.1, bf16[1024,128]{1,0:T(8,128)(2,1)} %copy-done.3, bf16[1024,128]{1,0:T(8,128)(2,1)} %copy-done.4, ...), custom_call_target="tpu_custom_call" | custom-call | tf_op jit(solution)/shard_map/unpack/pallas_call | solution.py:310
Async XLA Ops:
  3.2 11.9 %collective-permute-start = (bf16[1024,128]{1,0:T(8,128)(2,1)}, bf16[1024,128]{1,0:T(8,128)(2,1)S(1)}, u32[]{:S(2)}, u32[]{:S(2)}) collective-permute-start(bf16[1024,128]{1,0:T(8,128)(2,1)} %get-tuple-element.10.own), channel_id=1, source_target_pairs={{0,4},{12,8},{1,5},{13,9},{2,6},{14,10},{3,7},{15,11},{16,20},{28,... | collective-permute-start | bytes 786440 | tf_op jit(solution)/shard_map/ppermute | solution.py:302
  8.2 11.5 %collective-permute-start.2 = (bf16[1024,128]{1,0:T(8,128)(2,1)}, bf16[1024,128]{1,0:T(8,128)(2,1)S(1)}, u32[]{:S(2)}, u32[]{:S(2)}) collective-permute-start(bf16[1024,128]{1,0:T(8,128)(2,1)} %get-tuple-element.11), channel_id=1, source_target_pairs={{0,8},{12,4},{1,9},{13,5},{2,10},{14,6},{3,11},{15,7},{16,24},{28,... | collective-permute-start | bytes 786440 | tf_op jit(solution)/shard_map/ppermute | solution.py:302
  10.5 9.2 %collective-permute-start.1 = (bf16[1024,128]{1,0:T(8,128)(2,1)}, bf16[1024,128]{1,0:T(8,128)(2,1)S(1)}, u32[]{:S(2)}, u32[]{:S(2)}) collective-permute-start(bf16[1024,128]{1,0:T(8,128)(2,1)} %get-tuple-element.11), channel_id=1, source_target_pairs={{4,8},{8,4},{5,9},{9,5},{6,10},{10,6},{7,11},{11,7},{20,24},{24,20... | collective-permute-start | bytes 786440 | tf_op jit(solution)/shard_map/ppermute | solution.py:302
  11.2 8.5 %copy-start.2 = (s32[8]{0:T(128)S(1)}, s32[8]{0:T(128)}, u32[]{:S(2)}) copy-start(s32[8]{0:T(128)} %order_ref.1) | copy-start | bytes 100
  19.7 1.0 %copy-start = (bf16[1024,128]{1,0:T(8,128)(2,1)S(1)}, bf16[1024,128]{1,0:T(8,128)(2,1)}, u32[]{:S(2)}) copy-start(bf16[1024,128]{1,0:T(8,128)(2,1)} %get-tuple-element.10.own) | copy-start | bytes 786436
  21.2 0.7 %copy-start.1 = (bf16[1024,128]{1,0:T(8,128)(2,1)}, bf16[1024,128]{1,0:T(8,128)(2,1)S(1)}, u32[]{:S(2)}) copy-start(bf16[1024,128]{1,0:T(8,128)(2,1)S(1)} %get-tuple-element.12.own) | copy-start | bytes 786436
  21.9 14.5 %collective-permute-start.3 = (bf16[1024,128]{1,0:T(8,128)(2,1)S(1)}, bf16[1024,128]{1,0:T(8,128)(2,1)S(1)}, u32[]{:S(2)}, u32[]{:S(2)}) collective-permute-start(bf16[1024,128]{1,0:T(8,128)(2,1)S(1)} %get-tuple-element.13), channel_id=1, source_target_pairs={{4,0},{8,12},{5,1},{9,13},{6,2},{10,14},{7,3},{11,15},{20,16},{24,... | collective-permute-start | bytes 786440 | tf_op jit(solution)/shard_map/ppermute | solution.py:302
  23.2 13.2 %collective-permute-start.4 = (bf16[1024,128]{1,0:T(8,128)(2,1)S(1)}, bf16[1024,128]{1,0:T(8,128)(2,1)S(1)}, u32[]{:S(2)}, u32[]{:S(2)}) collective-permute-start(bf16[1024,128]{1,0:T(8,128)(2,1)S(1)} %get-tuple-element.14), channel_id=1, source_target_pairs={{4,8},{8,4},{5,9},{9,5},{6,10},{10,6},{7,11},{11,7},{20,24},{24,20... | collective-permute-start | bytes 786440 | tf_op jit(solution)/shard_map/ppermute | solution.py:302
  23.9 21.2 %collective-permute-start.5 = (bf16[1024,128]{1,0:T(8,128)(2,1)S(1)}, bf16[1024,128]{1,0:T(8,128)(2,1)S(1)}, u32[]{:S(2)}, u32[]{:S(2)}) collective-permute-start(bf16[1024,128]{1,0:T(8,128)(2,1)S(1)} %get-tuple-element.15), channel_id=1, source_target_pairs={{4,12},{8,0},{5,13},{9,1},{6,14},{10,2},{7,15},{11,3},{20,28},{24,... | collective-permute-start | bytes 786440 | tf_op jit(solution)/shard_map/ppermute | solution.py:302
  36.4 8.7 %copy-start.3 = (bf16[1024,128]{1,0:T(8,128)(2,1)}, bf16[1024,128]{1,0:T(8,128)(2,1)S(1)}, u32[]{:S(2)}) copy-start(bf16[1024,128]{1,0:T(8,128)(2,1)S(1)} %collective-permute-done.3.ra) | copy-start | bytes 786436
  36.4 8.7 %copy-start.4 = (bf16[1024,128]{1,0:T(8,128)(2,1)}, bf16[1024,128]{1,0:T(8,128)(2,1)S(1)}, u32[]{:S(2)}) copy-start(bf16[1024,128]{1,0:T(8,128)(2,1)S(1)} %collective-permute-done.4.rb) | copy-start | bytes 786436
  45.1 0.7 %copy-start.5 = (bf16[1024,128]{1,0:T(8,128)(2,1)}, bf16[1024,128]{1,0:T(8,128)(2,1)S(1)}, u32[]{:S(2)}) copy-start(bf16[1024,128]{1,0:T(8,128)(2,1)S(1)} %collective-permute-done.5.rc) | copy-start | bytes 786436

commit v2 on v1

--- a/solution.py
+++ b/solution.py
@@ -178,7 +178,7 @@
 NN=(((1,),(0,)),((),())); NT=(((1,),(1,)),((),()))
 def dot(a,b,dims): return lax.dot_general(a,b,dims,preferred_element_type=F32)
 
-def owner_kernel(rows, blk, order_ref, ids_ref, own, sa, sb, sc, o_own, o_a, o_b, o_c,
+def owner_kernel(rows, blk, order_ref, own, sc, sb, sa, o_own, o_c, o_b, o_a,
                  q, k, v, g, kt, vt, s, dk, dv):
     ins=(own,sa,sb,sc); outs=(o_own,o_a,o_b,o_c)
     sh=own.shape[0]//4
@@ -186,12 +186,13 @@
     total=4*sh
     factor=HEAD_DIM**-0.5
     c=factor*1.4426950408889634
+    _, _, held, ids = place_here()
     place=[]
     for t in range(4):
         for e in range(per):
-            p=pl.multiple_of(order_ref[ids_ref[t]*per+e]*SPAN,SPAN)
+            p=pl.multiple_of(order_ref[ids[t]*per+e]*SPAN,SPAN)
             place.append((t,e,p))
-    @pl.when(ids_ref[4]==1)
+    @pl.when(held)
     def _():
         for t,e,p in place:
             for n,dst in enumerate((q,k,v,g)):
@@ -246,74 +247,92 @@
             outs[t][2*sh+e*SPAN:2*sh+(e+1)*SPAN,:]=(dk[pl.ds(p,SPAN),:]*factor).astype(BF)
             outs[t][3*sh+e*SPAN:3*sh+(e+1)*SPAN,:]=dv[pl.ds(p,SPAN),:].astype(BF)
 
-def owner_call(order, ids, own, sa, sb, sc, blk=256):
+def owner_call(order, own, sa, sb, sc, blk=256):
     sh=own.shape[0]//4; total=4*sh
     vm=pl.BlockSpec(memory_space=pltpu.VMEM); sm=pl.BlockSpec(memory_space=pltpu.SMEM)
     return pl.pallas_call(
         functools.partial(owner_kernel,total,blk),
-        out_shape=tuple(jax.ShapeDtypeStruct(own.shape,BF) for _ in range(4)),
-        in_specs=[sm,sm,vm,vm,vm,vm], out_specs=(vm,)*4,
+        out_shape=tuple(pltpu.VMEM(own.shape,BF) for _ in range(4)),
+        in_specs=[sm,vm,vm,vm,vm], out_specs=(vm,)*4,
         scratch_shapes=[pltpu.VMEM((total,HEAD_DIM),BF)]*4+[pltpu.VMEM((HEAD_DIM,total),BF)]*2+
             [pltpu.VMEM((total,blk),F32)]+[pltpu.VMEM((total,HEAD_DIM),F32)]*2,
         compiler_params=pltpu.CompilerParams(vmem_limit_bytes=32<<20),
         name="owner",
-    )(order,ids,own,sa,sb,sc)
-
-
-def pack_kernel(side_ref, q, k, v, g, near, far):
+    )(order,own,sa,sb,sc)
+
+
+def place_here():
+    me = lax.axis_index("seq")
+    side = lax.div(me, 2)
+    owner = (me == 1) | (me == 2)
+    outer = 3 * side
+    return me, side, owner, (me, outer, 3 - me, 3 - outer)
+
+
+def columns(half):
+    return pl.ds(pl.multiple_of(half * HEAD_DIM, HEAD_DIM), HEAD_DIM)
+
+
+def run_copies(copies):
+    for one in copies:
+        one.start()
+    for one in copies:
+        one.wait()
+
+
+def pack_kernel(q, k, v, g, near, far, sem):
     sh = q.shape[0]
-    for s in range(2):
-        @pl.when(side_ref[0] == s)
+    _, side, _, _ = place_here()
+    run_copies([
+        pltpu.make_async_copy(src.at[:, columns(half)], dst.at[n * sh:(n + 1) * sh, :], sem.at[m, n])
+        for m, (dst, half) in enumerate(((far, 1 - side), (near, side)))
+        for n, src in enumerate((q, k, v, g))
+    ])
+
+
+def unpack_kernel(own, ra, rb, rc, *refs):
+    outs, sem = refs[:4], refs[4]
+    sh = outs[0].shape[0]
+    _, side, owner, _ = place_here()
+    for held in (True, False):
+        @pl.when(owner == held)
         def _():
-            for n, src in enumerate((q, k, v, g)):
-                near[n * sh:(n + 1) * sh, :] = src[:, s * HEAD_DIM:(s + 1) * HEAD_DIM]
-                far[n * sh:(n + 1) * sh, :] = src[:, (1 - s) * HEAD_DIM:(2 - s) * HEAD_DIM]
-
-
-def unpack_kernel(side_ref, own, ra, rb, rc, *outs):
-    sh = outs[0].shape[0]
-    for s in range(2):
-        for owner in range(2):
-            @pl.when((side_ref[0] == s) & (side_ref[1] == owner))
-            def _():
-                near, far = (own, rb) if owner else (ra, rc)
-                for n, dst in enumerate(outs):
-                    dst[:, s * HEAD_DIM:(s + 1) * HEAD_DIM] = near[n * sh:(n + 1) * sh, :]
-                    dst[:, (1 - s) * HEAD_DIM:(2 - s) * HEAD_DIM] = far[n * sh:(n + 1) * sh, :]
+            near, far = (own, rb) if held else (ra, rc)
+            run_copies([
+                pltpu.make_async_copy(src.at[n * sh:(n + 1) * sh, :], dst.at[:, columns(half)], sem.at[m, n])
+                for m, (src, half) in enumerate(((near, side), (far, 1 - side)))
+                for n, dst in enumerate(outs)
+            ])
 
 
 def owned_per_device(span_order, queries, keys, values, grad_out):
     rows = queries.shape[0]
-    me = lax.axis_index("seq")
-    side = jnp.where(me < 2, 0, 1)
-    owner = jnp.where((me == 1) | (me == 2), 1, 0)
-    near_outer = 3 * side
-    ids = jnp.stack([me, near_outer, 3 - me, 3 - near_outer, owner]).astype(jnp.int32)
-    flags = jnp.stack([side, owner]).astype(jnp.int32)
+    anywhere = pl.BlockSpec(memory_space=pl.ANY)
     vm = pl.BlockSpec(memory_space=pltpu.VMEM)
-    sm = pl.BlockSpec(memory_space=pltpu.SMEM)
     near, far = pl.pallas_call(
         pack_kernel,
-        out_shape=(jax.ShapeDtypeStruct((4 * rows, HEAD_DIM), BF),) * 2,
-        in_specs=[sm] + [vm] * 4,
-        out_specs=(vm, vm),
+        out_shape=(pltpu.VMEM((4 * rows, HEAD_DIM), BF),) * 2,
+        in_specs=[anywhere] * 4,
+        out_specs=(vm,) * 2,
+        scratch_shapes=[pltpu.SemaphoreType.DMA((2, 4))],
         name="pack",
-    )(flags, queries, keys, values, grad_out)
+    )(queries, keys, values, grad_out)
     go = lambda x, pairs: lax.ppermute(x, "seq", pairs)
     ga = go(near, [(0, 1), (3, 2)])
     gb = go(far, [(1, 2), (2, 1)])
     gc = go(far, [(0, 2), (3, 1)])
-    own, to_a, to_b, to_c = owner_call(span_order, ids, near, ga, gb, gc, blk=512)
+    own, to_c, to_b, to_a = owner_call(span_order, near, gc, gb, ga, blk=512)
     rb = go(to_b, [(1, 2), (2, 1)])
     rc = go(to_c, [(1, 3), (2, 0)])
     ra = go(to_a, [(1, 0), (2, 3)])
     return pl.pallas_call(
         unpack_kernel,
         out_shape=(jax.ShapeDtypeStruct(queries.shape, BF),) * 4,
-        in_specs=[sm] + [vm] * 4,
-        out_specs=(vm,) * 4,
+        in_specs=[vm] * 4,
+        out_specs=(anywhere,) * 4,
+        scratch_shapes=[pltpu.SemaphoreType.DMA((2, 4))],
         name="unpack",
-    )(flags, own, ra, rb, rc)
+    )(*(pltpu.with_memory_space_constraint(x, pltpu.VMEM) for x in (own, ra, rb, rc)))
 
 
 def solution(mesh):

time: 48.2 us -> 41.5 us (0.86)
  waiting for transfers between devices: 28.3 us -> 25.1 us
  local copies, waits for them, and re-layouts: 2.44 us -> 0.01 us
  Pallas kernels: 4.66 us -> 2.55 us
  starting transfers between devices: 11.2 us -> 12.9 us
  other arithmetic: 0.58 us -> 0 us
    ppermute x6, waiting for transfers between devices: 28.3 us -> 25.1 us  [owned_per_device(): go = lambda x, pairs: lax.ppermute(x, 'seq', pairs)]
    unnamed x12 -> x2, local copies, waits for them, and re-layouts: 2.36 us -> 0.01 us
    ppermute x6, starting transfers between devices: 11.2 us -> 12.9 us  [owned_per_device(): go = lambda x, pairs: lax.ppermute(x, 'seq', pairs)]
    pallas_call x1, Pallas kernels: 2.1 us -> 0.85 us  [owned_per_device(): pl.pallas_call(unpack_kernel, out_shape=(jax.ShapeDtypeStruct(queries.sha...]
    pallas_call x1, Pallas kernels: 2 us -> 1.14 us  [owned_per_device(): pl.pallas_call(pack_kernel, out_shape=(pltpu.VMEM((4 * rows, HEAD_DIM), B...]
    another operation x1 -> x0, other arithmetic: 0.58 us -> none  [owned_per_device(): flags = jnp.stack([side, owner]).astype(jnp.int32)]
where the time goes in v2:
time: 41.5 us; the launch traced here: 41.2 us
  waiting for transfers between devices  25.1 us (60%)
  starting transfers between devices  12.9 us (31%)
  Pallas kernels  2.55 us (6%)
  between operations  0.71 us (2%)
    ppermute x6, waiting for transfers between devices, owned_per_device(): go = lambda x, pairs: lax.ppermute(x, 'seq', pairs)  25.1 us
    ppermute x6, starting transfers between devices, owned_per_device(): go = lambda x, pairs: lax.ppermute(x, 'seq', pairs)  12.9 us
    pallas_call x1, Pallas kernels, owned_per_device(): pl.pallas_call(pack_kernel, out_shape=(pltpu.VMEM((4 * rows, HEAD_DIM), B...  1.14 us
    pallas_call x1, Pallas kernels, owned_per_device(): pl.pallas_call(unpack_kernel, out_shape=(jax.ShapeDtypeStruct(queries.sha...  0.85 us
  transfers between devices with their start and end apart: 6, of which 4 were waited for; matrix products, arithmetic and copies ran while one was open for 0% of the time, Pallas kernels for 0%

profile of v2, /device:TPU:0, one launch (start us, length us, event | category | flops | bytes accessed | tf_op | source)
XLA Modules:
  0.0 41.2 jit_solution(8129055077508624500)
XLA Ops:
  0.6 1.1 %pack.1 = (bf16[1024,128]{1,0:T(8,128)(2,1)S(1)}, bf16[1024,128]{1,0:T(8,128)(2,1)S(1)}) custom-call(bf16[256,256]{1,0:T(8,128)(2,1)} %q.1, bf16[256,256]{1,0:T(8,128)(2,1)} %k.1, bf16[256,256]{1,0:T(8,128)(2,1)} %v.1, bf16[256,256]{1,0:T(8,128)(2,1)} %g.1), custom_call_target="tpu_custom_call" | custom-call | tf_op jit(solution)/shard_map/pack/pallas_call | solution.py:312
  1.8 0.0 copy-start
  1.8 4.9 %collective-permute-start.2 = (bf16[1024,128]{1,0:T(8,128)(2,1)S(1)}, bf16[1024,128]{1,0:T(8,128)(2,1)S(1)}, u32[]{:S(2)}, u32[]{:S(2)}) collective-permute-start(bf16[1024,128]{1,0:T(8,128)(2,1)S(1)} %get-tuple-element.10.own), channel_id=1, source_target_pairs={{0,4},{12,8},{1,5},{13,9},{2,6},{14,10},{3,7},{15,11},{16,20},{28,... | collective-permute-start | bytes 786440 | tf_op jit(solution)/shard_map/ppermute | solution.py:320
  6.7 0.7 %collective-permute-start.1 = (bf16[1024,128]{1,0:T(8,128)(2,1)S(1)}, bf16[1024,128]{1,0:T(8,128)(2,1)S(1)}, u32[]{:S(2)}, u32[]{:S(2)}) collective-permute-start(bf16[1024,128]{1,0:T(8,128)(2,1)S(1)} %get-tuple-element.11), channel_id=1, source_target_pairs={{4,8},{8,4},{5,9},{9,5},{6,10},{10,6},{7,11},{11,7},{20,24},{24,20... | collective-permute-start | bytes 786440 | tf_op jit(solution)/shard_map/ppermute | solution.py:320
  7.4 4.0 %collective-permute-start = (bf16[1024,128]{1,0:T(8,128)(2,1)S(1)}, bf16[1024,128]{1,0:T(8,128)(2,1)S(1)}, u32[]{:S(2)}, u32[]{:S(2)}) collective-permute-start(bf16[1024,128]{1,0:T(8,128)(2,1)S(1)} %get-tuple-element.11), channel_id=1, source_target_pairs={{0,8},{12,4},{1,9},{13,5},{2,10},{14,6},{3,11},{15,7},{16,24},{28,... | collective-permute-start | bytes 786440 | tf_op jit(solution)/shard_map/ppermute | solution.py:320
  11.4 2.0 %collective-permute-done.2.sa = bf16[1024,128]{1,0:T(8,128)(2,1)S(1)} collective-permute-done((bf16[1024,128]{1,0:T(8,128)(2,1)S(1)}, bf16[1024,128]{1,0:T(8,128)(2,1)S(1)}, u32[]{:S(2)}, u32[]{:S(2)}) %collective-permute-start.2) | collective-permute-done | bytes 262176 | tf_op jit(solution)/shard_map/ppermute | solution.py:320
  13.4 0.0 collective-permute-done.1.sb
  13.4 4.5 %collective-permute-done.sc = bf16[1024,128]{1,0:T(8,128)(2,1)S(1)} collective-permute-done((bf16[1024,128]{1,0:T(8,128)(2,1)S(1)}, bf16[1024,128]{1,0:T(8,128)(2,1)S(1)}, u32[]{:S(2)}, u32[]{:S(2)}) %collective-permute-start) | collective-permute-done | bytes 262176 | tf_op jit(solution)/shard_map/ppermute | solution.py:320
  17.9 0.0 copy-done
  17.9 0.6 %owner.1 = (bf16[1024,128]{1,0:T(8,128)(2,1)S(1)}, bf16[1024,128]{1,0:T(8,128)(2,1)S(1)}, bf16[1024,128]{1,0:T(8,128)(2,1)S(1)}, bf16[1024,128]{1,0:T(8,128)(2,1)S(1)}) custom-call(s32[8]{0:T(128)S(1)} %copy-done, bf16[1024,128]{1,0:T(8,128)(2,1)S(1)} %get-tuple-element.10.own, bf16[1024,128]{1,0:T(8,128)(2,1)S(1)} %collective-permute-done.sc, ...), custom_call_target="tpu_custom_call" | custom-call | tf_op jit(solution)/shard_map/owner/pallas_call | solution.py:253
  18.5 1.3 %collective-permute-start.3 = (bf16[1024,128]{1,0:T(8,128)(2,1)S(1)}, bf16[1024,128]{1,0:T(8,128)(2,1)S(1)}, u32[]{:S(2)}, u32[]{:S(2)}) collective-permute-start(bf16[1024,128]{1,0:T(8,128)(2,1)S(1)} %get-tuple-element.13), channel_id=1, source_target_pairs={{4,0},{8,12},{5,1},{9,13},{6,2},{10,14},{7,3},{11,15},{20,16},{24,... | collective-permute-start | bytes 786440 | tf_op jit(solution)/shard_map/ppermute | solution.py:320
  19.8 0.7 %collective-permute-start.4 = (bf16[1024,128]{1,0:T(8,128)(2,1)S(1)}, bf16[1024,128]{1,0:T(8,128)(2,1)S(1)}, u32[]{:S(2)}, u32[]{:S(2)}) collective-permute-start(bf16[1024,128]{1,0:T(8,128)(2,1)S(1)} %get-tuple-element.14), channel_id=1, source_target_pairs={{4,8},{8,4},{5,9},{9,5},{6,10},{10,6},{7,11},{11,7},{20,24},{24,20... | collective-permute-start | bytes 786440 | tf_op jit(solution)/shard_map/ppermute | solution.py:320
  20.5 1.3 %collective-permute-start.5 = (bf16[1024,128]{1,0:T(8,128)(2,1)S(1)}, bf16[1024,128]{1,0:T(8,128)(2,1)S(1)}, u32[]{:S(2)}, u32[]{:S(2)}) collective-permute-start(bf16[1024,128]{1,0:T(8,128)(2,1)S(1)} %get-tuple-element.15), channel_id=1, source_target_pairs={{4,12},{8,0},{5,13},{9,1},{6,14},{10,2},{7,15},{11,3},{20,28},{24,... | collective-permute-start | bytes 786440 | tf_op jit(solution)/shard_map/ppermute | solution.py:320
  21.8 9.8 %collective-permute-done.3.ra = bf16[1024,128]{1,0:T(8,128)(2,1)S(1)} collective-permute-done((bf16[1024,128]{1,0:T(8,128)(2,1)S(1)}, bf16[1024,128]{1,0:T(8,128)(2,1)S(1)}, u32[]{:S(2)}, u32[]{:S(2)}) %collective-permute-start.3) | collective-permute-done | bytes 262176 | tf_op jit(solution)/shard_map/ppermute | solution.py:320
  31.6 0.0 collective-permute-done.4.rb
  31.6 8.8 %collective-permute-done.5.rc = bf16[1024,128]{1,0:T(8,128)(2,1)S(1)} collective-permute-done((bf16[1024,128]{1,0:T(8,128)(2,1)S(1)}, bf16[1024,128]{1,0:T(8,128)(2,1)S(1)}, u32[]{:S(2)}, u32[]{:S(2)}) %collective-permute-start.5) | collective-permute-done | bytes 262176 | tf_op jit(solution)/shard_map/ppermute | solution.py:320
  40.4 0.8 %unpack.1 = (bf16[256,256]{1,0:T(8,128)(2,1)}, bf16[256,256]{1,0:T(8,128)(2,1)}, bf16[256,256]{1,0:T(8,128)(2,1)}, bf16[256,256]{1,0:T(8,128)(2,1)}) custom-call(bf16[1024,128]{1,0:T(8,128)(2,1)S(1)} %get-tuple-element.12.own, bf16[1024,128]{1,0:T(8,128)(2,1)S(1)} %collective-permute-done.3.ra, bf16[1024,128]{1,0:T(8,128)(2,1)S(1)} %collective-permute-done.4.rb, ...), custom_call_target="tpu_custom_call" | custom-call | tf_op jit(solution)/shard_map/unpack/pallas_call | solution.py:328
Async XLA Ops:
  1.8 16.2 %copy-start = (s32[8]{0:T(128)S(1)}, s32[8]{0:T(128)}, u32[]{:S(2)}) copy-start(s32[8]{0:T(128)} %order_ref.1) | copy-start | bytes 100
  1.8 11.6 %collective-permute-start.2 = (bf16[1024,128]{1,0:T(8,128)(2,1)S(1)}, bf16[1024,128]{1,0:T(8,128)(2,1)S(1)}, u32[]{:S(2)}, u32[]{:S(2)}) collective-permute-start(bf16[1024,128]{1,0:T(8,128)(2,1)S(1)} %get-tuple-element.10.own), channel_id=1, source_target_pairs={{0,4},{12,8},{1,5},{13,9},{2,6},{14,10},{3,7},{15,11},{16,20},{28,... | collective-permute-start | bytes 786440 | tf_op jit(solution)/shard_map/ppermute | solution.py:320
  6.7 6.7 %collective-permute-start.1 = (bf16[1024,128]{1,0:T(8,128)(2,1)S(1)}, bf16[1024,128]{1,0:T(8,128)(2,1)S(1)}, u32[]{:S(2)}, u32[]{:S(2)}) collective-permute-start(bf16[1024,128]{1,0:T(8,128)(2,1)S(1)} %get-tuple-element.11), channel_id=1, source_target_pairs={{4,8},{8,4},{5,9},{9,5},{6,10},{10,6},{7,11},{11,7},{20,24},{24,20... | collective-permute-start | bytes 786440 | tf_op jit(solution)/shard_map/ppermute | solution.py:320
  7.4 10.5 %collective-permute-start = (bf16[1024,128]{1,0:T(8,128)(2,1)S(1)}, bf16[1024,128]{1,0:T(8,128)(2,1)S(1)}, u32[]{:S(2)}, u32[]{:S(2)}) collective-permute-start(bf16[1024,128]{1,0:T(8,128)(2,1)S(1)} %get-tuple-element.11), channel_id=1, source_target_pairs={{0,8},{12,4},{1,9},{13,5},{2,10},{14,6},{3,11},{15,7},{16,24},{28,... | collective-permute-start | bytes 786440 | tf_op jit(solution)/shard_map/ppermute | solution.py:320
  18.5 13.1 %collective-permute-start.3 = (bf16[1024,128]{1,0:T(8,128)(2,1)S(1)}, bf16[1024,128]{1,0:T(8,128)(2,1)S(1)}, u32[]{:S(2)}, u32[]{:S(2)}) collective-permute-start(bf16[1024,128]{1,0:T(8,128)(2,1)S(1)} %get-tuple-element.13), channel_id=1, source_target_pairs={{4,0},{8,12},{5,1},{9,13},{6,2},{10,14},{7,3},{11,15},{20,16},{24,... | collective-permute-start | bytes 786440 | tf_op jit(solution)/shard_map/ppermute | solution.py:320
  19.8 11.8 %collective-permute-start.4 = (bf16[1024,128]{1,0:T(8,128)(2,1)S(1)}, bf16[1024,128]{1,0:T(8,128)(2,1)S(1)}, u32[]{:S(2)}, u32[]{:S(2)}) collective-permute-start(bf16[1024,128]{1,0:T(8,128)(2,1)S(1)} %get-tuple-element.14), channel_id=1, source_target_pairs={{4,8},{8,4},{5,9},{9,5},{6,10},{10,6},{7,11},{11,7},{20,24},{24,20... | collective-permute-start | bytes 786440 | tf_op jit(solution)/shard_map/ppermute | solution.py:320
  20.5 19.9 %collective-permute-start.5 = (bf16[1024,128]{1,0:T(8,128)(2,1)S(1)}, bf16[1024,128]{1,0:T(8,128)(2,1)S(1)}, u32[]{:S(2)}, u32[]{:S(2)}) collective-permute-start(bf16[1024,128]{1,0:T(8,128)(2,1)S(1)} %get-tuple-element.15), channel_id=1, source_target_pairs={{4,12},{8,0},{5,13},{9,1},{6,14},{10,2},{7,15},{11,3},{20,28},{24,... | collective-permute-start | bytes 786440 | tf_op jit(solution)/shard_map/ppermute | solution.py:320

commit v3 on v0

--- a/solution.py
+++ b/solution.py
@@ -1,6 +1,8 @@
 import jax
 import jax.numpy as jnp
 from jax import lax
+from jax.experimental import pallas as pl
+from jax.experimental.pallas import tpu as pltpu
 from jax.sharding import PartitionSpec as P
 
 HEAD_DIM = 128
@@ -28,7 +30,7 @@
     return (stacked, starts)
 
 
-def per_device(span_order, queries, keys, values, grad_out):
+def gathered_per_device(span_order, queries, keys, values, grad_out):
     q_rows, k_rows, v_rows, g_rows = (queries, keys, values, grad_out)
     my_rows = q_rows.shape[0]
     heads_here = q_rows.shape[1] // HEAD_DIM
@@ -170,23 +172,203 @@
     return (attended_rows, grad_q_rows, grad_k_rows, grad_v_rows)
 
 
+F32 = jnp.float32
+BF = jnp.bfloat16
+NN = (((1,), (0,)), ((), ()))
+NT = (((1,), (1,)), ((), ()))
+LOG2E = 1.4426950408889634
+FACTOR = HEAD_DIM**-0.5
+BLOCK = 512
+
+
+def dot(a, b, dims):
+    return lax.dot_general(a, b, dims, preferred_element_type=F32)
+
+
+def place_here():
+    me = lax.axis_index("seq")
+    side = lax.div(me, 2)
+    owner = (me == 1) | (me == 2)
+    return me, side, owner
+
+
+def columns(half):
+    return pl.ds(pl.multiple_of(half * HEAD_DIM, HEAD_DIM), HEAD_DIM)
+
+
+def run_copies(copies):
+    for one in copies:
+        one.start()
+    for one in copies:
+        one.wait()
+
+
+def owner_kernel(order_ref, own, s_l, s_r, s_c, o_own, o_l, o_r, o_c, q, k, v, g, kt, vt, s, dk, dv):
+    me, side, held = place_here()
+    rows = own.shape[0] // 4
+    total = 4 * rows
+    per = rows // SPAN
+    far = 3 - 3 * side
+    slots = ((me, own, o_own), (me - 1, s_l, o_l), (me + 1, s_r, o_r), (far, s_c, o_c))
+
+    @pl.when(held)
+    def _():
+        places = [
+            (src, dst, e, pl.ds(pl.multiple_of(order_ref[at * per + e] * SPAN, SPAN), SPAN))
+            for at, src, dst in slots
+            for e in range(per)
+        ]
+        part = lambda n, e: slice(n * rows + e * SPAN, n * rows + (e + 1) * SPAN)
+        for src, _, e, where in places:
+            for n, to in enumerate((q, k, v, g)):
+                to[where, :] = src[part(n, e), :]
+        key_at = lax.broadcasted_iota(jnp.int32, (BLOCK, BLOCK), 0)
+        query_at = lax.broadcasted_iota(jnp.int32, (BLOCK, BLOCK), 1)
+        for i in range(total // BLOCK):
+            ri = slice(i * BLOCK, (i + 1) * BLOCK)
+            kt[:, ri] = k[ri, :].T
+            vt[:, ri] = v[ri, :].T
+            qb = q[ri, :]
+            top = None
+            for j in range(i + 1):
+                rj = slice(j * BLOCK, (j + 1) * BLOCK)
+                sj = dot(k[rj, :], qb, NT) * (FACTOR * LOG2E)
+                if j == i:
+                    sj = jnp.where(key_at <= query_at, sj, -1e30)
+                s[rj, :] = sj
+                tj = jnp.max(sj, axis=0, keepdims=True)
+                top = tj if top is None else jnp.maximum(top, tj)
+            weight, acc = None, None
+            for j in range(i + 1):
+                rj = slice(j * BLOCK, (j + 1) * BLOCK)
+                pj = jnp.exp2(s[rj, :] - top)
+                s[rj, :] = pj
+                lj = jnp.sum(pj, axis=0, keepdims=True)
+                oj = dot(vt[:, rj], pj.astype(BF), NN)
+                weight = lj if weight is None else weight + lj
+                acc = oj if acc is None else acc + oj
+            inverse = 1.0 / weight
+            ob = (acc * inverse).astype(BF)
+            gt = g[ri, :].T.astype(F32) * inverse
+            gb = gt.astype(BF)
+            delta = jnp.sum(gt * ob.astype(F32), axis=0, keepdims=True)
+            acc = None
+            for j in range(i + 1):
+                rj = slice(j * BLOCK, (j + 1) * BLOCK)
+                dp = dot(v[rj, :], gb, NN)
+                pj = s[rj, :]
+                ds = (pj * (dp - delta)).astype(BF)
+                vj = dot(pj.astype(BF), gb, NT)
+                kj = dot(ds, qb, NN)
+                if j == i:
+                    dv[rj, :] = vj
+                    dk[rj, :] = kj
+                else:
+                    dv[rj, :] += vj
+                    dk[rj, :] += kj
+                qj = dot(kt[:, rj], ds, NN)
+                acc = qj if acc is None else acc + qj
+            q[ri, :] = (acc * FACTOR).astype(BF).T
+            g[ri, :] = ob.T
+        for _, dst, e, where in places:
+            dst[part(0, e), :] = g[where, :]
+            dst[part(1, e), :] = q[where, :]
+            dst[part(2, e), :] = (dk[where, :] * FACTOR).astype(BF)
+            dst[part(3, e), :] = dv[where, :].astype(BF)
+
+
+def pack_kernel(q, k, v, g, hopl, hopr, rest, sem):
+    sh = q.shape[0]
+    _, side, owner = place_here()
+    near_rest = jnp.where(owner, side, 1 - side)
+    halves = ((hopl, 1 - near_rest), (hopr, 1 - near_rest), (rest, near_rest),)
+    run_copies([
+        pltpu.make_async_copy(src.at[:, columns(half)], dst.at[n * sh:(n + 1) * sh, :], sem.at[m, n])
+        for m, (dst, half) in enumerate(halves)
+        for n, src in enumerate((q, k, v, g))
+    ])
+
+
+def unpack_kernel(own, r_c, r_r, r_l, *refs):
+    outs, sem = refs[:4], refs[4]
+    sh = outs[0].shape[0]
+    me, side, _ = place_here()
+    for at, near, far in ((0, r_r, r_c), (1, own, r_r), (2, own, r_l), (3, r_l, r_c)):
+        @pl.when(me == at)
+        def _():
+            run_copies([
+                pltpu.make_async_copy(src.at[n * sh:(n + 1) * sh, :], dst.at[:, columns(half)], sem.at[m, n])
+                for m, (src, half) in enumerate(((far, 1 - side), (near, side)))
+                for n, dst in enumerate(outs)
+            ])
+
+
+def in_vmem(*shapes):
+    return tuple(pltpu.VMEM(shape, dtype) for shape, dtype in shapes)
+
+
+def kept(*arrays):
+    return tuple(pltpu.with_memory_space_constraint(x, pltpu.VMEM) for x in arrays)
+
+
+def owned_per_device(span_order, queries, keys, values, grad_out):
+    rows = queries.shape[0]
+    total = 4 * rows
+    anywhere = pl.BlockSpec(memory_space=pl.ANY)
+    vm = pl.BlockSpec(memory_space=pltpu.VMEM)
+    sm = pl.BlockSpec(memory_space=pltpu.SMEM)
+    stack = ((4 * rows, HEAD_DIM), BF)
+    per_row = ((total, HEAD_DIM), BF)
+    per_column = ((HEAD_DIM, total), BF)
+    wide = ((total, HEAD_DIM), F32)
+    hopl, hopr, rest = pl.pallas_call(
+        pack_kernel,
+        out_shape=in_vmem(*(stack,) * 3),
+        in_specs=[anywhere] * 4,
+        out_specs=(vm,) * 3,
+        scratch_shapes=[pltpu.SemaphoreType.DMA((3, 4))],
+        name="pack",
+    )(queries, keys, values, grad_out)
+    go = lambda x, pairs: lax.ppermute(x, "seq", pairs)
+    g_l = go(hopr, [(0, 1), (1, 2)])
+    g_r = go(hopl, [(3, 2), (2, 1)])
+    g_c = go(rest, [(0, 2), (3, 1)])
+    own, to_l, to_r, to_c = pl.pallas_call(
+        owner_kernel,
+        out_shape=in_vmem(*(stack,) * 4),
+        in_specs=[sm] + [vm] * 4,
+        out_specs=(vm,) * 4,
+        scratch_shapes=[
+            *in_vmem(per_row, per_row, per_row, per_row, per_column, per_column, ((total, BLOCK), F32), wide, wide)
+        ],
+        compiler_params=pltpu.CompilerParams(vmem_limit_bytes=32 << 20),
+        name="owner",
+    )(span_order, *kept(rest, g_l, g_r, g_c))
+    r_r = go(to_l, [(1, 0), (2, 1)])
+    r_l = go(to_r, [(1, 2), (2, 3)])
+    r_c = go(to_c, [(1, 3), (2, 0)])
+    return pl.pallas_call(
+        unpack_kernel,
+        out_shape=(jax.ShapeDtypeStruct(queries.shape, BF),) * 4,
+        in_specs=[vm] * 4,
+        out_specs=(anywhere,) * 4,
+        scratch_shapes=[pltpu.SemaphoreType.DMA((2, 4))],
+        name="unpack",
+    )(*kept(own, r_c, r_r, r_l))
+
+
 def solution(mesh):
-    placed = (
-        P("groups"),
-        P(("groups", "seq"), ("head", "mp")),
-        P(("groups", "seq"), ("head", "mp")),
-        P(("groups", "seq"), ("head", "mp")),
-        P(("groups", "seq"), ("head", "mp")),
-    )
-    return jax.shard_map(
-        per_device,
-        mesh=mesh,
-        in_specs=placed,
-        out_specs=(
-            P(("groups", "seq"), ("head", "mp")),
-            P(("groups", "seq"), ("head", "mp")),
-            P(("groups", "seq"), ("head", "mp")),
-            P(("groups", "seq"), ("head", "mp")),
-        ),
-        check_vma=False,
-    )
+    rows_columns = P(("groups", "seq"), ("head", "mp"))
+
+    def run(span_order, queries, keys, values, grad_out):
+        heads_here = queries.shape[1] // HEAD_DIM // (mesh.shape["head"] * mesh.shape["mp"])
+        small = mesh.shape["seq"] == 4 and heads_here == 2
+        return jax.shard_map(
+            owned_per_device if small else gathered_per_device,
+            mesh=mesh,
+            in_specs=(P("groups"),) + (rows_columns,) * 4,
+            out_specs=(rows_columns,) * 4,
+            check_vma=False,
+        )(span_order, queries, keys, values, grad_out)
+
+    return run

time: 141 us -> 38.5 us (0.27)
  blocking collectives: 87.8 us -> 0 us
  waiting for transfers between devices: 0 us -> 19.8 us
  local copies, waits for them, and re-layouts: 18.9 us -> 0.01 us
  loops' own time: 16.1 us -> 0 us
  starting transfers between devices: 0 us -> 15.1 us
  other arithmetic: 9.09 us -> 0 us
  matrix products: 7.54 us -> 0 us
  Pallas kernels: 0 us -> 2.68 us
    all_gather x6 -> x0, blocking collectives: 87.8 us -> none  [the longest x1 17.3 us: per_device(): lax.all_gather(k_rows, 'seq', axis=0, tiled=True)]
    ppermute x0 -> x6, waiting for transfers between devices: none -> 19.8 us  [owned_per_device(): go = lambda x, pairs: lax.ppermute(x, 'seq', pairs)]
    another operation x3 -> x0, loops' own time: 16.1 us -> none  [the longest x1 8.11 us: per_device(): carry, unused = lax.scan(key_one_block, carry, stacked + (starts,))]
    ppermute x0 -> x6, starting transfers between devices: none -> 15.1 us  [owned_per_device(): go = lambda x, pairs: lax.ppermute(x, 'seq', pairs)]
    dot_general x20 -> x0, matrix products: 7.54 us -> none  [the longest x8 2.84 us: masked_scores(): jnp.einsum('qhd,khd->hqk', query_block, key_block, preferred_element_type...]
    dynamic_slice x37 -> x0, local copies, waits for them, and re-layouts: 6.45 us -> none  [the longest x20 3.27 us: per_device(): carry, unused = lax.scan(key_one_block, carry, stacked + (starts,))]
    unnamed x27 -> x2, local copies, waits for them, and re-layouts: 6.19 us -> 0.01 us
    gather x2 -> x0, other arithmetic: 4.41 us -> none  [per_device(): jnp.repeat(span_order, SPAN, total_repeat_length=total_rows) * SPAN]
  transfers between devices with their start and end apart: 0 -> 6, of which waited for: 0 -> 3; matrix products, arithmetic and copies ran while one was open for 0% -> 0% of each run, Pallas kernels for 0% -> 0%
where the time goes in v3:
time: 38.5 us; the launch traced here: 38.2 us
  waiting for transfers between devices  19.8 us (51%)
  starting transfers between devices  15.1 us (39%)
  Pallas kernels  2.68 us (7%)
  between operations  0.72 us (2%)
    ppermute x6, waiting for transfers between devices, owned_per_device(): go = lambda x, pairs: lax.ppermute(x, 'seq', pairs)  19.8 us
    ppermute x6, starting transfers between devices, owned_per_device(): go = lambda x, pairs: lax.ppermute(x, 'seq', pairs)  15.1 us
    pallas_call x1, Pallas kernels, owned_per_device(): pl.pallas_call(pack_kernel, out_shape=in_vmem(*(stack,) * 3), in_specs=[a...  1.28 us
    pallas_call x1, Pallas kernels, owned_per_device(): pl.pallas_call(unpack_kernel, out_shape=(jax.ShapeDtypeStruct(queries.sha...  0.85 us
  transfers between devices with their start and end apart: 6, of which 3 were waited for; matrix products, arithmetic and copies ran while one was open for 0% of the time, Pallas kernels for 0%

profile of v3, /device:TPU:0, one launch (start us, length us, event | category | flops | bytes accessed | tf_op | source)
XLA Modules:
  0.0 38.2 jit_solution(13448022943585965925)
XLA Ops:
  0.6 1.3 %pack.1 = (bf16[1024,128]{1,0:T(8,128)(2,1)S(1)}, bf16[1024,128]{1,0:T(8,128)(2,1)S(1)}, bf16[1024,128]{1,0:T(8,128)(2,1)S(1)}) custom-call(bf16[256,256]{1,0:T(8,128)(2,1)} %q.1, bf16[256,256]{1,0:T(8,128)(2,1)} %k.1, bf16[256,256]{1,0:T(8,128)(2,1)} %v.1, bf16[256,256]{1,0:T(8,128)(2,1)} %g.1), custom_call_target="tpu_custom_call" | custom-call | tf_op jit(solution)/shard_map/pack/pallas_call | solution.py:324
  1.9 4.9 %collective-permute-start = (bf16[1024,128]{1,0:T(8,128)(2,1)S(1)}, bf16[1024,128]{1,0:T(8,128)(2,1)S(1)}, u32[]{:S(2)}, u32[]{:S(2)}) collective-permute-start(bf16[1024,128]{1,0:T(8,128)(2,1)S(1)} %get-tuple-element.12), channel_id=1, source_target_pairs={{0,4},{4,8},{1,5},{5,9},{2,6},{6,10},{3,7},{7,11},{16,20},{20,24},... | collective-permute-start | bytes 786440 | tf_op jit(solution)/shard_map/ppermute | solution.py:332
  6.9 0.0 copy-start
  6.9 0.7 %collective-permute-start.1 = (bf16[1024,128]{1,0:T(8,128)(2,1)S(1)}, bf16[1024,128]{1,0:T(8,128)(2,1)S(1)}, u32[]{:S(2)}, u32[]{:S(2)}) collective-permute-start(bf16[1024,128]{1,0:T(8,128)(2,1)S(1)} %get-tuple-element.13), channel_id=1, source_target_pairs={{12,8},{8,4},{13,9},{9,5},{14,10},{10,6},{15,11},{11,7},{28,24},{2... | collective-permute-start | bytes 786440 | tf_op jit(solution)/shard_map/ppermute | solution.py:332
  7.6 6.2 %collective-permute-start.2 = (bf16[1024,128]{1,0:T(8,128)(2,1)S(1)}, bf16[1024,128]{1,0:T(8,128)(2,1)S(1)}, u32[]{:S(2)}, u32[]{:S(2)}) collective-permute-start(bf16[1024,128]{1,0:T(8,128)(2,1)S(1)} %get-tuple-element.11.own), channel_id=1, source_target_pairs={{0,8},{12,4},{1,9},{13,5},{2,10},{14,6},{3,11},{15,7},{16,24},{28,... | collective-permute-start | bytes 786440 | tf_op jit(solution)/shard_map/ppermute | solution.py:332
  13.8 0.0 collective-permute-done.s_l
  13.8 0.0 collective-permute-done.1.s_r
  13.8 4.9 %collective-permute-done.2.s_c = bf16[1024,128]{1,0:T(8,128)(2,1)S(1)} collective-permute-done((bf16[1024,128]{1,0:T(8,128)(2,1)S(1)}, bf16[1024,128]{1,0:T(8,128)(2,1)S(1)}, u32[]{:S(2)}, u32[]{:S(2)}) %collective-permute-start.2) | collective-permute-done | bytes 262176 | tf_op jit(solution)/shard_map/ppermute | solution.py:332
  18.7 0.0 copy-done
  18.7 0.6 %owner.1 = (bf16[1024,128]{1,0:T(8,128)(2,1)S(1)}, bf16[1024,128]{1,0:T(8,128)(2,1)S(1)}, bf16[1024,128]{1,0:T(8,128)(2,1)S(1)}, bf16[1024,128]{1,0:T(8,128)(2,1)S(1)}) custom-call(s32[8]{0:T(128)S(1)} %copy-done, bf16[1024,128]{1,0:T(8,128)(2,1)S(1)} %get-tuple-element.11.own, bf16[1024,128]{1,0:T(8,128)(2,1)S(1)} %collective-permute-done.s_l, ...), custom_call_target="tpu_custom_call" | custom-call | tf_op jit(solution)/shard_map/owner/pallas_call | solution.py:336
  19.3 1.3 %collective-permute-start.3 = (bf16[1024,128]{1,0:T(8,128)(2,1)S(1)}, bf16[1024,128]{1,0:T(8,128)(2,1)S(1)}, u32[]{:S(2)}, u32[]{:S(2)}) collective-permute-start(bf16[1024,128]{1,0:T(8,128)(2,1)S(1)} %get-tuple-element.15), channel_id=1, source_target_pairs={{4,12},{8,0},{5,13},{9,1},{6,14},{10,2},{7,15},{11,3},{20,28},{24,... | collective-permute-start | bytes 786440 | tf_op jit(solution)/shard_map/ppermute | solution.py:332
  20.6 1.3 %collective-permute-start.4 = (bf16[1024,128]{1,0:T(8,128)(2,1)S(1)}, bf16[1024,128]{1,0:T(8,128)(2,1)S(1)}, u32[]{:S(2)}, u32[]{:S(2)}) collective-permute-start(bf16[1024,128]{1,0:T(8,128)(2,1)S(1)} %get-tuple-element.16), channel_id=1, source_target_pairs={{4,0},{8,4},{5,1},{9,5},{6,2},{10,6},{7,3},{11,7},{20,16},{24,20},... | collective-permute-start | bytes 786440 | tf_op jit(solution)/shard_map/ppermute | solution.py:332
  21.9 0.7 %collective-permute-start.5 = (bf16[1024,128]{1,0:T(8,128)(2,1)S(1)}, bf16[1024,128]{1,0:T(8,128)(2,1)S(1)}, u32[]{:S(2)}, u32[]{:S(2)}) collective-permute-start(bf16[1024,128]{1,0:T(8,128)(2,1)S(1)} %get-tuple-element.17), channel_id=1, source_target_pairs={{4,8},{8,12},{5,9},{9,13},{6,10},{10,14},{7,11},{11,15},{20,24},{2... | collective-permute-start | bytes 786440 | tf_op jit(solution)/shard_map/ppermute | solution.py:332
  22.6 10.4 %collective-permute-done.3.r_c = bf16[1024,128]{1,0:T(8,128)(2,1)S(1)} collective-permute-done((bf16[1024,128]{1,0:T(8,128)(2,1)S(1)}, bf16[1024,128]{1,0:T(8,128)(2,1)S(1)}, u32[]{:S(2)}, u32[]{:S(2)}) %collective-permute-start.3) | collective-permute-done | bytes 262176 | tf_op jit(solution)/shard_map/ppermute | solution.py:332
  33.0 4.4 %collective-permute-done.4.r_r = bf16[1024,128]{1,0:T(8,128)(2,1)S(1)} collective-permute-done((bf16[1024,128]{1,0:T(8,128)(2,1)S(1)}, bf16[1024,128]{1,0:T(8,128)(2,1)S(1)}, u32[]{:S(2)}, u32[]{:S(2)}) %collective-permute-start.4) | collective-permute-done | bytes 262176 | tf_op jit(solution)/shard_map/ppermute | solution.py:332
  37.4 0.0 collective-permute-done.5.r_l
  37.4 0.8 %unpack.1 = (bf16[256,256]{1,0:T(8,128)(2,1)}, bf16[256,256]{1,0:T(8,128)(2,1)}, bf16[256,256]{1,0:T(8,128)(2,1)}, bf16[256,256]{1,0:T(8,128)(2,1)}) custom-call(bf16[1024,128]{1,0:T(8,128)(2,1)S(1)} %get-tuple-element.14.own, bf16[1024,128]{1,0:T(8,128)(2,1)S(1)} %collective-permute-done.3.r_c, bf16[1024,128]{1,0:T(8,128)(2,1)S(1)} %collective-permute-done.4.r_r, ...), custom_call_target="tpu_custom_call" | custom-call | tf_op jit(solution)/shard_map/unpack/pallas_call | solution.py:350
Async XLA Ops:
  1.9 11.8 %collective-permute-start = (bf16[1024,128]{1,0:T(8,128)(2,1)S(1)}, bf16[1024,128]{1,0:T(8,128)(2,1)S(1)}, u32[]{:S(2)}, u32[]{:S(2)}) collective-permute-start(bf16[1024,128]{1,0:T(8,128)(2,1)S(1)} %get-tuple-element.12), channel_id=1, source_target_pairs={{0,4},{4,8},{1,5},{5,9},{2,6},{6,10},{3,7},{7,11},{16,20},{20,24},... | collective-permute-start | bytes 786440 | tf_op jit(solution)/shard_map/ppermute | solution.py:332
  6.9 11.9 %copy-start = (s32[8]{0:T(128)S(1)}, s32[8]{0:T(128)}, u32[]{:S(2)}) copy-start(s32[8]{0:T(128)} %order_ref.1) | copy-start | bytes 100
  6.9 6.9 %collective-permute-start.1 = (bf16[1024,128]{1,0:T(8,128)(2,1)S(1)}, bf16[1024,128]{1,0:T(8,128)(2,1)S(1)}, u32[]{:S(2)}, u32[]{:S(2)}) collective-permute-start(bf16[1024,128]{1,0:T(8,128)(2,1)S(1)} %get-tuple-element.13), channel_id=1, source_target_pairs={{12,8},{8,4},{13,9},{9,5},{14,10},{10,6},{15,11},{11,7},{28,24},{2... | collective-permute-start | bytes 786440 | tf_op jit(solution)/shard_map/ppermute | solution.py:332
  7.6 11.2 %collective-permute-start.2 = (bf16[1024,128]{1,0:T(8,128)(2,1)S(1)}, bf16[1024,128]{1,0:T(8,128)(2,1)S(1)}, u32[]{:S(2)}, u32[]{:S(2)}) collective-permute-start(bf16[1024,128]{1,0:T(8,128)(2,1)S(1)} %get-tuple-element.11.own), channel_id=1, source_target_pairs={{0,8},{12,4},{1,9},{13,5},{2,10},{14,6},{3,11},{15,7},{16,24},{28,... | collective-permute-start | bytes 786440 | tf_op jit(solution)/shard_map/ppermute | solution.py:332
  19.3 13.7 %collective-permute-start.3 = (bf16[1024,128]{1,0:T(8,128)(2,1)S(1)}, bf16[1024,128]{1,0:T(8,128)(2,1)S(1)}, u32[]{:S(2)}, u32[]{:S(2)}) collective-permute-start(bf16[1024,128]{1,0:T(8,128)(2,1)S(1)} %get-tuple-element.15), channel_id=1, source_target_pairs={{4,12},{8,0},{5,13},{9,1},{6,14},{10,2},{7,15},{11,3},{20,28},{24,... | collective-permute-start | bytes 786440 | tf_op jit(solution)/shard_map/ppermute | solution.py:332
  20.6 16.8 %collective-permute-start.4 = (bf16[1024,128]{1,0:T(8,128)(2,1)S(1)}, bf16[1024,128]{1,0:T(8,128)(2,1)S(1)}, u32[]{:S(2)}, u32[]{:S(2)}) collective-permute-start(bf16[1024,128]{1,0:T(8,128)(2,1)S(1)} %get-tuple-element.16), channel_id=1, source_target_pairs={{4,0},{8,4},{5,1},{9,5},{6,2},{10,6},{7,3},{11,7},{20,16},{24,20},... | collective-permute-start | bytes 786440 | tf_op jit(solution)/shard_map/ppermute | solution.py:332
  21.9 15.5 %collective-permute-start.5 = (bf16[1024,128]{1,0:T(8,128)(2,1)S(1)}, bf16[1024,128]{1,0:T(8,128)(2,1)S(1)}, u32[]{:S(2)}, u32[]{:S(2)}) collective-permute-start(bf16[1024,128]{1,0:T(8,128)(2,1)S(1)} %get-tuple-element.17), channel_id=1, source_target_pairs={{4,8},{8,12},{5,9},{9,13},{6,10},{10,14},{7,11},{11,15},{20,24},{2... | collective-permute-start | bytes 786440 | tf_op jit(solution)/shard_map/ppermute | solution.py:332

commit v4 on v3

--- a/solution.py
+++ b/solution.py
@@ -179,6 +179,7 @@
 LOG2E = 1.4426950408889634
 FACTOR = HEAD_DIM**-0.5
 BLOCK = 512
+HALF = 256
 
 
 def dot(a, b, dims):
@@ -203,64 +204,75 @@
         one.wait()
 
 
-def owner_kernel(order_ref, own, s_l, s_r, s_c, o_own, o_l, o_r, o_c, q, k, v, g, kt, vt, s, dk, dv):
+def owner_kernel(order_ref, own, s_l, s_r, s_c, o_own, o_c, o_a, o_b, q, k, v, g, kt, vt, s, dk, dv):
     me, side, held = place_here()
     rows = own.shape[0] // 4
     total = 4 * rows
     per = rows // SPAN
-    far = 3 - 3 * side
-    slots = ((me, own, o_own), (me - 1, s_l, o_l), (me + 1, s_r, o_r), (far, s_c, o_c))
+    near_at, far_at = 3 * side, 3 - 3 * side
+    slots_in = ((me, own), (me - 1, s_l), (me + 1, s_r), (far_at, s_c))
+    slots_out = ((me, o_own), (far_at, o_c), (near_at, o_a), (3 - me, o_b))
 
     @pl.when(held)
     def _():
-        places = [
-            (src, dst, e, pl.ds(pl.multiple_of(order_ref[at * per + e] * SPAN, SPAN), SPAN))
-            for at, src, dst in slots
+        places = lambda slots: [
+            (ref, e, pl.ds(pl.multiple_of(order_ref[at * per + e] * SPAN, SPAN), SPAN))
+            for at, ref in slots
             for e in range(per)
         ]
         part = lambda n, e: slice(n * rows + e * SPAN, n * rows + (e + 1) * SPAN)
-        for src, _, e, where in places:
+        for src, e, where in places(slots_in):
             for n, to in enumerate((q, k, v, g)):
                 to[where, :] = src[part(n, e), :]
-        key_at = lax.broadcasted_iota(jnp.int32, (BLOCK, BLOCK), 0)
-        query_at = lax.broadcasted_iota(jnp.int32, (BLOCK, BLOCK), 1)
+        key_at = lax.broadcasted_iota(jnp.int32, (HALF, HALF), 0)
+        query_at = lax.broadcasted_iota(jnp.int32, (HALF, HALF), 1)
+        seen = key_at <= query_at
+        tail = lambda whole, part: jnp.concatenate([whole[:, :HALF], part(whole[:, HALF:])], axis=1)
         for i in range(total // BLOCK):
+            lo = slice(i * BLOCK, i * BLOCK + HALF)
+            hi = slice(i * BLOCK + HALF, (i + 1) * BLOCK)
             ri = slice(i * BLOCK, (i + 1) * BLOCK)
+            olds = [slice(j * BLOCK, (j + 1) * BLOCK) for j in range(i)] + [lo]
             kt[:, ri] = k[ri, :].T
             vt[:, ri] = v[ri, :].T
             qb = q[ri, :]
+            qh = q[hi, :]
             top = None
-            for j in range(i + 1):
-                rj = slice(j * BLOCK, (j + 1) * BLOCK)
+            for rj in olds:
                 sj = dot(k[rj, :], qb, NT) * (FACTOR * LOG2E)
-                if j == i:
-                    sj = jnp.where(key_at <= query_at, sj, -1e30)
-                s[rj, :] = sj
+                if rj is lo:
+                    sj = jnp.concatenate([jnp.where(seen, sj[:, :HALF], -1e30), sj[:, HALF:]], axis=1)
+                s[rj, ri] = sj
                 tj = jnp.max(sj, axis=0, keepdims=True)
                 top = tj if top is None else jnp.maximum(top, tj)
+            sh = jnp.where(seen, dot(k[hi, :], qh, NT) * (FACTOR * LOG2E), -1e30)
+            s[hi, hi] = sh
+            top = tail(top, lambda x: jnp.maximum(x, jnp.max(sh, axis=0, keepdims=True)))
             weight, acc = None, None
-            for j in range(i + 1):
-                rj = slice(j * BLOCK, (j + 1) * BLOCK)
-                pj = jnp.exp2(s[rj, :] - top)
-                s[rj, :] = pj
+            for rj in olds:
+                pj = jnp.exp2(s[rj, ri] - top)
+                s[rj, ri] = pj
                 lj = jnp.sum(pj, axis=0, keepdims=True)
                 oj = dot(vt[:, rj], pj.astype(BF), NN)
                 weight = lj if weight is None else weight + lj
                 acc = oj if acc is None else acc + oj
+            ph = jnp.exp2(s[hi, hi] - top[:, HALF:])
+            s[hi, hi] = ph
+            weight = tail(weight, lambda x: x + jnp.sum(ph, axis=0, keepdims=True))
+            acc = tail(acc, lambda x: x + dot(vt[:, hi], ph.astype(BF), NN))
             inverse = 1.0 / weight
             ob = (acc * inverse).astype(BF)
             gt = g[ri, :].T.astype(F32) * inverse
             gb = gt.astype(BF)
             delta = jnp.sum(gt * ob.astype(F32), axis=0, keepdims=True)
             acc = None
-            for j in range(i + 1):
-                rj = slice(j * BLOCK, (j + 1) * BLOCK)
+            for rj in olds:
                 dp = dot(v[rj, :], gb, NN)
-                pj = s[rj, :]
+                pj = s[rj, ri]
                 ds = (pj * (dp - delta)).astype(BF)
                 vj = dot(pj.astype(BF), gb, NT)
                 kj = dot(ds, qb, NN)
-                if j == i:
+                if rj is lo:
                     dv[rj, :] = vj
                     dk[rj, :] = kj
                 else:
@@ -268,16 +280,22 @@
                     dk[rj, :] += kj
                 qj = dot(kt[:, rj], ds, NN)
                 acc = qj if acc is None else acc + qj
+            dp = dot(v[hi, :], gb[:, HALF:], NN)
+            ph = s[hi, hi]
+            ds = (ph * (dp - delta[:, HALF:])).astype(BF)
+            dv[hi, :] = dot(ph.astype(BF), gb[:, HALF:], NT)
+            dk[hi, :] = dot(ds, qh, NN)
+            acc = tail(acc, lambda x: x + dot(kt[:, hi], ds, NN))
             q[ri, :] = (acc * FACTOR).astype(BF).T
             g[ri, :] = ob.T
-        for _, dst, e, where in places:
+        for dst, e, where in places(slots_out):
             dst[part(0, e), :] = g[where, :]
             dst[part(1, e), :] = q[where, :]
             dst[part(2, e), :] = (dk[where, :] * FACTOR).astype(BF)
             dst[part(3, e), :] = dv[where, :].astype(BF)
 
 
-def pack_kernel(q, k, v, g, hopl, hopr, rest, sem):
+def pack_kernel(order, q, k, v, g, hopl, hopr, rest, order_out, sem, order_sem):
     sh = q.shape[0]
     _, side, owner = place_here()
     near_rest = jnp.where(owner, side, 1 - side)
@@ -286,14 +304,14 @@
         pltpu.make_async_copy(src.at[:, columns(half)], dst.at[n * sh:(n + 1) * sh, :], sem.at[m, n])
         for m, (dst, half) in enumerate(halves)
         for n, src in enumerate((q, k, v, g))
-    ])
-
-
-def unpack_kernel(own, r_c, r_r, r_l, *refs):
+    ] + [pltpu.make_async_copy(order, order_out, order_sem)])
+
+
+def unpack_kernel(own, r_c, r_a, r_b, *refs):
     outs, sem = refs[:4], refs[4]
     sh = outs[0].shape[0]
     me, side, _ = place_here()
-    for at, near, far in ((0, r_r, r_c), (1, own, r_r), (2, own, r_l), (3, r_l, r_c)):
+    for at, near, far in ((0, r_a, r_c), (1, own, r_b), (2, own, r_b), (3, r_a, r_c)):
         @pl.when(me == at)
         def _():
             run_copies([
@@ -321,31 +339,31 @@
     per_row = ((total, HEAD_DIM), BF)
     per_column = ((HEAD_DIM, total), BF)
     wide = ((total, HEAD_DIM), F32)
-    hopl, hopr, rest = pl.pallas_call(
+    hopl, hopr, rest, order = pl.pallas_call(
         pack_kernel,
-        out_shape=in_vmem(*(stack,) * 3),
-        in_specs=[anywhere] * 4,
-        out_specs=(vm,) * 3,
-        scratch_shapes=[pltpu.SemaphoreType.DMA((3, 4))],
+        out_shape=in_vmem(*(stack,) * 3) + (pltpu.SMEM(span_order.shape, span_order.dtype),),
+        in_specs=[anywhere] * 5,
+        out_specs=(vm,) * 3 + (sm,),
+        scratch_shapes=[pltpu.SemaphoreType.DMA((3, 4)), pltpu.SemaphoreType.DMA],
         name="pack",
-    )(queries, keys, values, grad_out)
+    )(span_order, queries, keys, values, grad_out)
     go = lambda x, pairs: lax.ppermute(x, "seq", pairs)
     g_l = go(hopr, [(0, 1), (1, 2)])
     g_r = go(hopl, [(3, 2), (2, 1)])
     g_c = go(rest, [(0, 2), (3, 1)])
-    own, to_l, to_r, to_c = pl.pallas_call(
+    own, to_c, to_a, to_b = pl.pallas_call(
         owner_kernel,
         out_shape=in_vmem(*(stack,) * 4),
         in_specs=[sm] + [vm] * 4,
         out_specs=(vm,) * 4,
         scratch_shapes=[
-            *in_vmem(per_row, per_row, per_row, per_row, per_column, per_column, ((total, BLOCK), F32), wide, wide)
+            *in_vmem(per_row, per_row, per_row, per_row, per_column, per_column, ((total, total), F32), wide, wide)
         ],
         compiler_params=pltpu.CompilerParams(vmem_limit_bytes=32 << 20),
         name="owner",
-    )(span_order, *kept(rest, g_l, g_r, g_c))
-    r_r = go(to_l, [(1, 0), (2, 1)])
-    r_l = go(to_r, [(1, 2), (2, 3)])
+    )(order, *kept(rest, g_l, g_r, g_c))
+    r_a = go(to_a, [(1, 0), (2, 3)])
+    r_b = go(to_b, [(1, 2), (2, 1)])
     r_c = go(to_c, [(1, 3), (2, 0)])
     return pl.pallas_call(
         unpack_kernel,
@@ -354,7 +372,7 @@
         out_specs=(anywhere,) * 4,
         scratch_shapes=[pltpu.SemaphoreType.DMA((2, 4))],
         name="unpack",
-    )(*kept(own, r_c, r_r, r_l))
+    )(*kept(own, r_c, r_a, r_b))
 
 
 def solution(mesh):

time: 38.5 us -> 37.8 us (0.982)
  Pallas kernels: 2.68 us -> 2.14 us
    pallas_call x1, Pallas kernels: 0.56 us -> 0.01 us  [owned_per_device(): pl.pallas_call(owner_kernel, out_shape=in_vmem(*(stack,) * 4), in_specs=[...]
where the time goes in v4:
time: 37.8 us; the launch traced here: 37.5 us
  waiting for transfers between devices  19.6 us (52%)
  starting transfers between devices  15 us (40%)
  Pallas kernels  2.14 us (6%)
  between operations  0.71 us (2%)
    ppermute x6, waiting for transfers between devices, owned_per_device(): go = lambda x, pairs: lax.ppermute(x, 'seq', pairs)  19.6 us
    ppermute x6, starting transfers between devices, owned_per_device(): go = lambda x, pairs: lax.ppermute(x, 'seq', pairs)  15 us
    pallas_call x1, Pallas kernels, owned_per_device(): pl.pallas_call(pack_kernel, out_shape=in_vmem(*(stack,) * 3) + (pltpu.SME...  1.29 us
    pallas_call x1, Pallas kernels, owned_per_device(): pl.pallas_call(unpack_kernel, out_shape=(jax.ShapeDtypeStruct(queries.sha...  0.85 us
  transfers between devices with their start and end apart: 6, of which 3 were waited for; matrix products, arithmetic and copies ran while one was open for 0% of the time, Pallas kernels for 0%

profile of v4, /device:TPU:0, one launch (start us, length us, event | category | flops | bytes accessed | tf_op | source)
XLA Modules:
  0.0 37.5 jit_solution(7753795484647363699)
XLA Ops:
  0.6 1.3 %pack.1 = (bf16[1024,128]{1,0:T(8,128)(2,1)S(1)}, bf16[1024,128]{1,0:T(8,128)(2,1)S(1)}, bf16[1024,128]{1,0:T(8,128)(2,1)S(1)}, s32[8]{0:T(128)S(4)}) custom-call(s32[8]{0:T(128)} %order.1, bf16[256,256]{1,0:T(8,128)(2,1)} %q.1, bf16[256,256]{1,0:T(8,128)(2,1)} %k.1, bf16[256,256]{1,0:T(8,128)(2,1)} %v.1, bf16[256,256]{1,0:T(8,128)(2,1)} %g.1), custom_call_target="tpu_custom_call" | custom-call | tf_op jit(solution)/shard_map/pack/pallas_call | solution.py:342
  1.9 4.9 %collective-permute-start = (bf16[1024,128]{1,0:T(8,128)(2,1)S(1)}, bf16[1024,128]{1,0:T(8,128)(2,1)S(1)}, u32[]{:S(2)}, u32[]{:S(2)}) collective-permute-start(bf16[1024,128]{1,0:T(8,128)(2,1)S(1)} %get-tuple-element.14), channel_id=1, source_target_pairs={{0,4},{4,8},{1,5},{5,9},{2,6},{6,10},{3,7},{7,11},{16,20},{20,24},... | collective-permute-start | bytes 786440 | tf_op jit(solution)/shard_map/ppermute | solution.py:350
  6.9 0.7 %collective-permute-start.1 = (bf16[1024,128]{1,0:T(8,128)(2,1)S(1)}, bf16[1024,128]{1,0:T(8,128)(2,1)S(1)}, u32[]{:S(2)}, u32[]{:S(2)}) collective-permute-start(bf16[1024,128]{1,0:T(8,128)(2,1)S(1)} %get-tuple-element.15), channel_id=1, source_target_pairs={{12,8},{8,4},{13,9},{9,5},{14,10},{10,6},{15,11},{11,7},{28,24},{2... | collective-permute-start | bytes 786440 | tf_op jit(solution)/shard_map/ppermute | solution.py:350
  7.6 6.2 %collective-permute-start.2 = (bf16[1024,128]{1,0:T(8,128)(2,1)S(1)}, bf16[1024,128]{1,0:T(8,128)(2,1)S(1)}, u32[]{:S(2)}, u32[]{:S(2)}) collective-permute-start(bf16[1024,128]{1,0:T(8,128)(2,1)S(1)} %get-tuple-element.13.own), channel_id=1, source_target_pairs={{0,8},{12,4},{1,9},{13,5},{2,10},{14,6},{3,11},{15,7},{16,24},{28,... | collective-permute-start | bytes 786440 | tf_op jit(solution)/shard_map/ppermute | solution.py:350
  13.8 0.0 collective-permute-done.s_l
  13.8 0.0 collective-permute-done.1.s_r
  13.8 4.9 %collective-permute-done.2.s_c = bf16[1024,128]{1,0:T(8,128)(2,1)S(1)} collective-permute-done((bf16[1024,128]{1,0:T(8,128)(2,1)S(1)}, bf16[1024,128]{1,0:T(8,128)(2,1)S(1)}, u32[]{:S(2)}, u32[]{:S(2)}) %collective-permute-start.2) | collective-permute-done | bytes 262176 | tf_op jit(solution)/shard_map/ppermute | solution.py:350
  18.7 1.3 %collective-permute-start.3 = (bf16[1024,128]{1,0:T(8,128)(2,1)S(1)}, bf16[1024,128]{1,0:T(8,128)(2,1)S(1)}, u32[]{:S(2)}, u32[]{:S(2)}) collective-permute-start(bf16[1024,128]{1,0:T(8,128)(2,1)S(1)} %get-tuple-element.17), channel_id=1, source_target_pairs={{4,12},{8,0},{5,13},{9,1},{6,14},{10,2},{7,15},{11,3},{20,28},{24,... | collective-permute-start | bytes 786440 | tf_op jit(solution)/shard_map/ppermute | solution.py:350
  20.0 1.3 %collective-permute-start.4 = (bf16[1024,128]{1,0:T(8,128)(2,1)S(1)}, bf16[1024,128]{1,0:T(8,128)(2,1)S(1)}, u32[]{:S(2)}, u32[]{:S(2)}) collective-permute-start(bf16[1024,128]{1,0:T(8,128)(2,1)S(1)} %get-tuple-element.18), channel_id=1, source_target_pairs={{4,0},{8,12},{5,1},{9,13},{6,2},{10,14},{7,3},{11,15},{20,16},{24,... | collective-permute-start | bytes 786440 | tf_op jit(solution)/shard_map/ppermute | solution.py:350
  21.3 0.7 %collective-permute-start.5 = (bf16[1024,128]{1,0:T(8,128)(2,1)S(1)}, bf16[1024,128]{1,0:T(8,128)(2,1)S(1)}, u32[]{:S(2)}, u32[]{:S(2)}) collective-permute-start(bf16[1024,128]{1,0:T(8,128)(2,1)S(1)} %get-tuple-element.19), channel_id=1, source_target_pairs={{4,8},{8,4},{5,9},{9,5},{6,10},{10,6},{7,11},{11,7},{20,24},{24,20... | collective-permute-start | bytes 786440 | tf_op jit(solution)/shard_map/ppermute | solution.py:350
  22.0 9.2 %collective-permute-done.3.r_c = bf16[1024,128]{1,0:T(8,128)(2,1)S(1)} collective-permute-done((bf16[1024,128]{1,0:T(8,128)(2,1)S(1)}, bf16[1024,128]{1,0:T(8,128)(2,1)S(1)}, u32[]{:S(2)}, u32[]{:S(2)}) %collective-permute-start.3) | collective-permute-done | bytes 262176 | tf_op jit(solution)/shard_map/ppermute | solution.py:350
  31.2 5.4 %collective-permute-done.4.r_a = bf16[1024,128]{1,0:T(8,128)(2,1)S(1)} collective-permute-done((bf16[1024,128]{1,0:T(8,128)(2,1)S(1)}, bf16[1024,128]{1,0:T(8,128)(2,1)S(1)}, u32[]{:S(2)}, u32[]{:S(2)}) %collective-permute-start.4) | collective-permute-done | bytes 262176 | tf_op jit(solution)/shard_map/ppermute | solution.py:350
  36.7 0.0 collective-permute-done.5.r_b
  36.7 0.8 %unpack.1 = (bf16[256,256]{1,0:T(8,128)(2,1)}, bf16[256,256]{1,0:T(8,128)(2,1)}, bf16[256,256]{1,0:T(8,128)(2,1)}, bf16[256,256]{1,0:T(8,128)(2,1)}) custom-call(bf16[1024,128]{1,0:T(8,128)(2,1)S(1)} %get-tuple-element.16.own, bf16[1024,128]{1,0:T(8,128)(2,1)S(1)} %collective-permute-done.3.r_c, bf16[1024,128]{1,0:T(8,128)(2,1)S(1)} %collective-permute-done.4.r_a, ...), custom_call_target="tpu_custom_call" | custom-call | tf_op jit(solution)/shard_map/unpack/pallas_call | solution.py:368
  (1 shorter events, 0.0 us)
Async XLA Ops:
  1.9 11.8 %collective-permute-start = (bf16[1024,128]{1,0:T(8,128)(2,1)S(1)}, bf16[1024,128]{1,0:T(8,128)(2,1)S(1)}, u32[]{:S(2)}, u32[]{:S(2)}) collective-permute-start(bf16[1024,128]{1,0:T(8,128)(2,1)S(1)} %get-tuple-element.14), channel_id=1, source_target_pairs={{0,4},{4,8},{1,5},{5,9},{2,6},{6,10},{3,7},{7,11},{16,20},{20,24},... | collective-permute-start | bytes 786440 | tf_op jit(solution)/shard_map/ppermute | solution.py:350
  6.9 6.9 %collective-permute-start.1 = (bf16[1024,128]{1,0:T(8,128)(2,1)S(1)}, bf16[1024,128]{1,0:T(8,128)(2,1)S(1)}, u32[]{:S(2)}, u32[]{:S(2)}) collective-permute-start(bf16[1024,128]{1,0:T(8,128)(2,1)S(1)} %get-tuple-element.15), channel_id=1, source_target_pairs={{12,8},{8,4},{13,9},{9,5},{14,10},{10,6},{15,11},{11,7},{28,24},{2... | collective-permute-start | bytes 786440 | tf_op jit(solution)/shard_map/ppermute | solution.py:350
  7.6 11.2 %collective-permute-start.2 = (bf16[1024,128]{1,0:T(8,128)(2,1)S(1)}, bf16[1024,128]{1,0:T(8,128)(2,1)S(1)}, u32[]{:S(2)}, u32[]{:S(2)}) collective-permute-start(bf16[1024,128]{1,0:T(8,128)(2,1)S(1)} %get-tuple-element.13.own), channel_id=1, source_target_pairs={{0,8},{12,4},{1,9},{13,5},{2,10},{14,6},{3,11},{15,7},{16,24},{28,... | collective-permute-start | bytes 786440 | tf_op jit(solution)/shard_map/ppermute | solution.py:350
  18.7 12.5 %collective-permute-start.3 = (bf16[1024,128]{1,0:T(8,128)(2,1)S(1)}, bf16[1024,128]{1,0:T(8,128)(2,1)S(1)}, u32[]{:S(2)}, u32[]{:S(2)}) collective-permute-start(bf16[1024,128]{1,0:T(8,128)(2,1)S(1)} %get-tuple-element.17), channel_id=1, source_target_pairs={{4,12},{8,0},{5,13},{9,1},{6,14},{10,2},{7,15},{11,3},{20,28},{24,... | collective-permute-start | bytes 786440 | tf_op jit(solution)/shard_map/ppermute | solution.py:350
  20.0 16.6 %collective-permute-start.4 = (bf16[1024,128]{1,0:T(8,128)(2,1)S(1)}, bf16[1024,128]{1,0:T(8,128)(2,1)S(1)}, u32[]{:S(2)}, u32[]{:S(2)}) collective-permute-start(bf16[1024,128]{1,0:T(8,128)(2,1)S(1)} %get-tuple-element.18), channel_id=1, source_target_pairs={{4,0},{8,12},{5,1},{9,13},{6,2},{10,14},{7,3},{11,15},{20,16},{24,... | collective-permute-start | bytes 786440 | tf_op jit(solution)/shard_map/ppermute | solution.py:350
  21.3 15.4 %collective-permute-start.5 = (bf16[1024,128]{1,0:T(8,128)(2,1)S(1)}, bf16[1024,128]{1,0:T(8,128)(2,1)S(1)}, u32[]{:S(2)}, u32[]{:S(2)}) collective-permute-start(bf16[1024,128]{1,0:T(8,128)(2,1)S(1)} %get-tuple-element.19), channel_id=1, source_target_pairs={{4,8},{8,4},{5,9},{9,5},{6,10},{10,6},{7,11},{11,7},{20,24},{24,20... | collective-permute-start | bytes 786440 | tf_op jit(solution)/shard_map/ppermute | solution.py:350

commit v5 on v4

--- a/solution.py
+++ b/solution.py
@@ -1,3 +1,5 @@
+import functools
+
 import jax
 import jax.numpy as jnp
 from jax import lax
@@ -204,14 +206,13 @@
         one.wait()
 
 
-def owner_kernel(order_ref, own, s_l, s_r, s_c, o_own, o_c, o_a, o_b, q, k, v, g, kt, vt, s, dk, dv):
+def owner_kernel(order_ref, turn, own, s_c1, s_a1, s_b1, s_a0, s_b0, s_c0, o_own, o_a, o_c, o_b, q, k, v, g, kt, vt, s, dk, dv):
     me, side, held = place_here()
     rows = own.shape[0] // 4
     total = 4 * rows
     per = rows // SPAN
     near_at, far_at = 3 * side, 3 - 3 * side
-    slots_in = ((me, own), (me - 1, s_l), (me + 1, s_r), (far_at, s_c))
-    slots_out = ((me, o_own), (far_at, o_c), (near_at, o_a), (3 - me, o_b))
+    slots_out = ((me, o_own), (near_at, o_a), (far_at, o_c), (3 - me, o_b))
 
     @pl.when(held)
     def _():
@@ -221,9 +222,16 @@
             for e in range(per)
         ]
         part = lambda n, e: slice(n * rows + e * SPAN, n * rows + (e + 1) * SPAN)
-        for src, e, where in places(slots_in):
-            for n, to in enumerate((q, k, v, g)):
-                to[where, :] = src[part(n, e), :]
+        def collect(slots):
+            for src, e, where in places(slots):
+                for n, to in enumerate((q, k, v, g)):
+                    to[where, :] = src[part(n, e), :]
+
+        for core, arrived in enumerate((
+            ((me, own), (far_at, s_c0), (near_at, s_a0), (3 - me, s_b0)),
+            ((me, own), (far_at, s_c1), (near_at, s_a1), (3 - me, s_b1)),
+        )):
+            pl.when(lax.axis_index("mp") == core)(functools.partial(collect, arrived))
         key_at = lax.broadcasted_iota(jnp.int32, (HALF, HALF), 0)
         query_at = lax.broadcasted_iota(jnp.int32, (HALF, HALF), 1)
         seen = key_at <= query_at
@@ -295,19 +303,23 @@
             dst[part(3, e), :] = dv[where, :].astype(BF)
 
 
-def pack_kernel(order, q, k, v, g, hopl, hopr, rest, order_out, sem, order_sem):
+def pack_kernel(order, q, k, v, g, rest1, hopl1, hopr1, hopl0, hopr0, rest0, mine, turn, order_out, sem, order_sem):
     sh = q.shape[0]
     _, side, owner = place_here()
-    near_rest = jnp.where(owner, side, 1 - side)
-    halves = ((hopl, 1 - near_rest), (hopr, 1 - near_rest), (rest, near_rest),)
-    run_copies([
-        pltpu.make_async_copy(src.at[:, columns(half)], dst.at[n * sh:(n + 1) * sh, :], sem.at[m, n])
-        for m, (dst, half) in enumerate(halves)
-        for n, src in enumerate((q, k, v, g))
-    ] + [pltpu.make_async_copy(order, order_out, order_sem)])
-
-
-def unpack_kernel(own, r_c, r_a, r_b, *refs):
+    rest_half = jnp.where(owner, side, 1 - side)
+    turn[...] = jnp.zeros_like(turn)
+    for core, hopl, hopr, rest in ((0, hopl0, hopr0, rest0), (1, hopl1, hopr1, rest1)):
+        @pl.when(lax.axis_index("mp") == core)
+        def _():
+            halves = ((rest, 1 - side), (hopl, 1 - rest_half), (hopr, 1 - rest_half), (mine, side))
+            run_copies([
+                pltpu.make_async_copy(src.at[:, columns(half)], dst.at[n * sh:(n + 1) * sh, :], sem.at[m, n])
+                for m, (dst, half) in enumerate(halves)
+                for n, src in enumerate((q, k, v, g))
+            ] + [pltpu.make_async_copy(order, order_out, order_sem)])
+
+
+def unpack_kernel(own, r_a, r_c, r_b, *refs):
     outs, sem = refs[:4], refs[4]
     sh = outs[0].shape[0]
     me, side, _ = place_here()
@@ -339,29 +351,38 @@
     per_row = ((total, HEAD_DIM), BF)
     per_column = ((HEAD_DIM, total), BF)
     wide = ((total, HEAD_DIM), F32)
-    hopl, hopr, rest, order = pl.pallas_call(
+    rest1, hopl1, hopr1, hopl0, hopr0, rest0, mine, turn, order = pl.pallas_call(
         pack_kernel,
-        out_shape=in_vmem(*(stack,) * 3) + (pltpu.SMEM(span_order.shape, span_order.dtype),),
+        out_shape=in_vmem(*(stack,) * 7, ((16, HEAD_DIM), BF)) + (pltpu.SMEM(span_order.shape, span_order.dtype),),
         in_specs=[anywhere] * 5,
-        out_specs=(vm,) * 3 + (sm,),
-        scratch_shapes=[pltpu.SemaphoreType.DMA((3, 4)), pltpu.SemaphoreType.DMA],
+        out_specs=(vm,) * 8 + (sm,),
+        scratch_shapes=[pltpu.SemaphoreType.DMA((4, 4)), pltpu.SemaphoreType.DMA],
         name="pack",
     )(span_order, queries, keys, values, grad_out)
     go = lambda x, pairs: lax.ppermute(x, "seq", pairs)
-    g_l = go(hopr, [(0, 1), (1, 2)])
-    g_r = go(hopl, [(3, 2), (2, 1)])
-    g_c = go(rest, [(0, 2), (3, 1)])
-    own, to_c, to_a, to_b = pl.pallas_call(
+
+    def go_core(x, pairs, core):
+        return lax.ppermute(x, ("seq", "mp"), [(2 * a + core, 2 * b + core) for a, b in pairs])
+
+    g_c1 = go_core(rest1, [(0, 2), (3, 1)], 1)
+    g_a1 = go_core(hopl1, [(0, 1), (3, 2)], 1)
+    g_b1 = go_core(hopr1, [(1, 2), (2, 1)], 1)
+    turn = lax.ppermute(turn, ("seq", "mp"), [(2 * a + 1, 2 * a + 0) for a in range(4)])
+    hopl0, hopr0, rest0, turn = lax.optimization_barrier((hopl0, hopr0, rest0, turn))
+    g_a0 = go_core(hopl0, [(0, 1), (3, 2)], 0)
+    g_b0 = go_core(hopr0, [(1, 2), (2, 1)], 0)
+    g_c0 = go_core(rest0, [(0, 2), (3, 1)], 0)
+    own, to_a, to_c, to_b = pl.pallas_call(
         owner_kernel,
         out_shape=in_vmem(*(stack,) * 4),
-        in_specs=[sm] + [vm] * 4,
+        in_specs=[sm] + [vm] * 8,
         out_specs=(vm,) * 4,
         scratch_shapes=[
             *in_vmem(per_row, per_row, per_row, per_row, per_column, per_column, ((total, total), F32), wide, wide)
         ],
         compiler_params=pltpu.CompilerParams(vmem_limit_bytes=32 << 20),
         name="owner",
-    )(order, *kept(rest, g_l, g_r, g_c))
+    )(order, *kept(turn, mine, g_c1, g_a1, g_b1, g_a0, g_b0, g_c0))
     r_a = go(to_a, [(1, 0), (2, 3)])
     r_b = go(to_b, [(1, 2), (2, 1)])
     r_c = go(to_c, [(1, 3), (2, 0)])
@@ -372,7 +393,7 @@
         out_specs=(anywhere,) * 4,
         scratch_shapes=[pltpu.SemaphoreType.DMA((2, 4))],
         name="unpack",
-    )(*kept(own, r_c, r_a, r_b))
+    )(*kept(own, r_a, r_c, r_b))
 
 
 def solution(mesh):

time: 37.8 us -> 35.5 us (0.939)
  starting transfers between devices: 15 us -> 12.4 us
    ppermute x6 -> x3, starting transfers between devices: 15 us -> 3.25 us  [owned_per_device(): go = lambda x, pairs: lax.ppermute(x, 'seq', pairs)]
    ppermute x0 -> x7, starting transfers between devices: none -> 9.16 us  [the longest x6 7.87 us: go_core(): lax.ppermute(x, ('seq', 'mp'), [(2 * a + core, 2 * b + core) for a, b in...]
    ppermute x0 -> x7, waiting for transfers between devices: none -> 7.98 us  [the longest x1 4.09 us: owned_per_device(): lax.ppermute(turn, ('seq', 'mp'), [(2 * a + 1, 2 * a + 0) for a in range(...]
    ppermute x6 -> x3, waiting for transfers between devices: 19.6 us -> 11.7 us  [owned_per_device(): go = lambda x, pairs: lax.ppermute(x, 'seq', pairs)]
  transfers between devices with their start and end apart: 6 -> 10, of which waited for: 3 -> 4; matrix products, arithmetic and copies ran while one was open for 0% -> 0% of each run, Pallas kernels for 0% -> 0%
where the time goes in v5:
time: 35.5 us; the launch traced here: 35.2 us
  waiting for transfers between devices  19.7 us (55%)
  starting transfers between devices  12.4 us (35%)
  Pallas kernels  2.32 us (7%)
  between operations  0.75 us (2%)
    ppermute x3, waiting for transfers between devices, owned_per_device(): go = lambda x, pairs: lax.ppermute(x, 'seq', pairs)  11.7 us
    ppermute x6, starting transfers between devices, go_core(): lax.ppermute(x, ('seq', 'mp'), [(2 * a + core, 2 * b + core) for a, b in...  7.87 us
    ppermute x1, waiting for transfers between devices, owned_per_device(): lax.ppermute(turn, ('seq', 'mp'), [(2 * a + 1, 2 * a + 0) for a in range(...  4.09 us
    ppermute x6, waiting for transfers between devices, go_core(): lax.ppermute(x, ('seq', 'mp'), [(2 * a + core, 2 * b + core) for a, b in...  3.89 us
    ppermute x3, starting transfers between devices, owned_per_device(): go = lambda x, pairs: lax.ppermute(x, 'seq', pairs)  3.25 us
    pallas_call x1, Pallas kernels, owned_per_device(): pl.pallas_call(pack_kernel, out_shape=in_vmem(*(stack,) * 7, ((16, HEAD_D...  1.47 us
    ppermute x1, starting transfers between devices, owned_per_device(): lax.ppermute(turn, ('seq', 'mp'), [(2 * a + 1, 2 * a + 0) for a in range(...  1.29 us
    pallas_call x1, Pallas kernels, owned_per_device(): pl.pallas_call(unpack_kernel, out_shape=(jax.ShapeDtypeStruct(queries.sha...  0.85 us
  transfers between devices with their start and end apart: 10, of which 4 were waited for; matrix products, arithmetic and copies ran while one was open for 0% of the time, Pallas kernels for 0%

profile of v5, /device:TPU:0, one launch (start us, length us, event | category | flops | bytes accessed | tf_op | source)
XLA Modules:
  0.0 35.2 jit_solution(17978804576797227244)
XLA Ops:
  0.6 1.5 %pack.1 = (bf16[1024,128]{1,0:T(8,128)(2,1)S(1)}, bf16[1024,128]{1,0:T(8,128)(2,1)S(1)}, bf16[1024,128]{1,0:T(8,128)(2,1)S(1)}, bf16[1024,128]{1,0:T(8,128)(2,1)...) custom-call(s32[8]{0:T(128)} %order.1, ...), custom_call_target="tpu_custom_call" | custom-call | tf_op jit(solution)/shard_map/pack/pallas_call | solution.py:354
  2.1 0.7 %collective-permute-start.1 = (bf16[1024,128]{1,0:T(8,128)(2,1)S(1)}, bf16[1024,128]{1,0:T(8,128)(2,1)S(1)}, u32[]{:S(2)}, u32[]{:S(2)}) collective-permute-start(bf16[1024,128]{1,0:T(8,128)(2,1)S(1)} %get-tuple-element.28), channel_id=1, source_target_pairs={{1,9},{13,5},{3,11},{15,7},{17,25},{29,21},{19,27},{31,23}} | collective-permute-start | bytes 786440 | tf_op jit(solution)/shard_map/ppermute | solution.py:365
  2.8 1.3 %collective-permute-start = (bf16[16,128]{1,0:T(8,128)(2,1)S(1)}, bf16[16,128]{1,0:T(8,128)(2,1)S(1)}, u32[]{:S(2)}, u32[]{:S(2)}) collective-permute-start(bf16[16,128]{1,0:T(8,128)(2,1)S(1)} %get-tuple-element.25), channel_id=1, source_target_pairs={{1,0},{5,4},{9,8},{13,12},{3,2},{7,6},{11,10},{15,14},{17,16},{21,... | collective-permute-start | bytes 12296 | tf_op jit(solution)/shard_map/ppermute | solution.py:370
  4.1 0.7 %collective-permute-start.2 = (bf16[1024,128]{1,0:T(8,128)(2,1)S(1)}, bf16[1024,128]{1,0:T(8,128)(2,1)S(1)}, u32[]{:S(2)}, u32[]{:S(2)}) collective-permute-start(bf16[1024,128]{1,0:T(8,128)(2,1)S(1)} %get-tuple-element.29), channel_id=1, source_target_pairs={{1,5},{13,9},{3,7},{15,11},{17,21},{29,25},{19,23},{31,27}} | collective-permute-start | bytes 786440 | tf_op jit(solution)/shard_map/ppermute | solution.py:365
  4.8 0.7 %collective-permute-start.3 = (bf16[1024,128]{1,0:T(8,128)(2,1)S(1)}, bf16[1024,128]{1,0:T(8,128)(2,1)S(1)}, u32[]{:S(2)}, u32[]{:S(2)}) collective-permute-start(bf16[1024,128]{1,0:T(8,128)(2,1)S(1)} %get-tuple-element.30), channel_id=1, source_target_pairs={{5,9},{9,5},{7,11},{11,7},{21,25},{25,21},{23,27},{27,23}} | collective-permute-start | bytes 786440 | tf_op jit(solution)/shard_map/ppermute | solution.py:365
  5.5 4.1 %collective-permute-done.turn = bf16[16,128]{1,0:T(8,128)(2,1)S(1)} collective-permute-done((bf16[16,128]{1,0:T(8,128)(2,1)S(1)}, bf16[16,128]{1,0:T(8,128)(2,1)S(1)}, u32[]{:S(2)}, u32[]{:S(2)}) %collective-permute-start) | collective-permute-done | bytes 4128 | tf_op jit(solution)/shard_map/ppermute | solution.py:370
  9.6 1.3 %collective-permute-start.4 = (bf16[1024,128]{1,0:T(8,128)(2,1)S(1)}, bf16[1024,128]{1,0:T(8,128)(2,1)S(1)}, u32[]{:S(2)}, u32[]{:S(2)}) collective-permute-start(bf16[1024,128]{1,0:T(8,128)(2,1)S(1)} %get-tuple-element.31), channel_id=1, source_target_pairs={{0,4},{12,8},{2,6},{14,10},{16,20},{28,24},{18,22},{30,26}} | collective-permute-start | bytes 786440 | tf_op jit(solution)/shard_map/ppermute | solution.py:365
  10.9 0.7 %collective-permute-start.5 = (bf16[1024,128]{1,0:T(8,128)(2,1)S(1)}, bf16[1024,128]{1,0:T(8,128)(2,1)S(1)}, u32[]{:S(2)}, u32[]{:S(2)}) collective-permute-start(bf16[1024,128]{1,0:T(8,128)(2,1)S(1)} %get-tuple-element.32), channel_id=1, source_target_pairs={{4,8},{8,4},{6,10},{10,6},{20,24},{24,20},{22,26},{26,22}} | collective-permute-start | bytes 786440 | tf_op jit(solution)/shard_map/ppermute | solution.py:365
  11.5 0.0 collective-permute-done.1.s_c1
  11.6 3.9 %collective-permute-start.6 = (bf16[1024,128]{1,0:T(8,128)(2,1)S(1)}, bf16[1024,128]{1,0:T(8,128)(2,1)S(1)}, u32[]{:S(2)}, u32[]{:S(2)}) collective-permute-start(bf16[1024,128]{1,0:T(8,128)(2,1)S(1)} %get-tuple-element.33), channel_id=1, source_target_pairs={{0,8},{12,4},{2,10},{14,6},{16,24},{28,20},{18,26},{30,22}} | collective-permute-start | bytes 786440 | tf_op jit(solution)/shard_map/ppermute | solution.py:365
  15.4 0.0 collective-permute-done.2.s_a1
  15.4 0.0 collective-permute-done.3.s_b1
  15.4 1.0 %collective-permute-done.4.s_a0 = bf16[1024,128]{1,0:T(8,128)(2,1)S(1)} collective-permute-done((bf16[1024,128]{1,0:T(8,128)(2,1)S(1)}, bf16[1024,128]{1,0:T(8,128)(2,1)S(1)}, u32[]{:S(2)}, u32[]{:S(2)}) %collective-permute-start.4) | collective-permute-done | bytes 262176 | tf_op jit(solution)/shard_map/ppermute | solution.py:365
  16.4 0.0 collective-permute-done.5.s_b0
  16.4 2.9 %collective-permute-done.6.s_c0 = bf16[1024,128]{1,0:T(8,128)(2,1)S(1)} collective-permute-done((bf16[1024,128]{1,0:T(8,128)(2,1)S(1)}, bf16[1024,128]{1,0:T(8,128)(2,1)S(1)}, u32[]{:S(2)}, u32[]{:S(2)}) %collective-permute-start.6) | collective-permute-done | bytes 262176 | tf_op jit(solution)/shard_map/ppermute | solution.py:365
  19.3 1.3 %collective-permute-start.7 = (bf16[1024,128]{1,0:T(8,128)(2,1)S(1)}, bf16[1024,128]{1,0:T(8,128)(2,1)S(1)}, u32[]{:S(2)}, u32[]{:S(2)}) collective-permute-start(bf16[1024,128]{1,0:T(8,128)(2,1)S(1)} %get-tuple-element.35), channel_id=1, source_target_pairs={{4,0},{8,12},{5,1},{9,13},{6,2},{10,14},{7,3},{11,15},{20,16},{24,... | collective-permute-start | bytes 786440 | tf_op jit(solution)/shard_map/ppermute | solution.py:362
  20.6 1.3 %collective-permute-start.8 = (bf16[1024,128]{1,0:T(8,128)(2,1)S(1)}, bf16[1024,128]{1,0:T(8,128)(2,1)S(1)}, u32[]{:S(2)}, u32[]{:S(2)}) collective-permute-start(bf16[1024,128]{1,0:T(8,128)(2,1)S(1)} %get-tuple-element.36), channel_id=1, source_target_pairs={{4,12},{8,0},{5,13},{9,1},{6,14},{10,2},{7,15},{11,3},{20,28},{24,... | collective-permute-start | bytes 786440 | tf_op jit(solution)/shard_map/ppermute | solution.py:362
  21.9 0.7 %collective-permute-start.9 = (bf16[1024,128]{1,0:T(8,128)(2,1)S(1)}, bf16[1024,128]{1,0:T(8,128)(2,1)S(1)}, u32[]{:S(2)}, u32[]{:S(2)}) collective-permute-start(bf16[1024,128]{1,0:T(8,128)(2,1)S(1)} %get-tuple-element.37), channel_id=1, source_target_pairs={{4,8},{8,4},{5,9},{9,5},{6,10},{10,6},{7,11},{11,7},{20,24},{24,20... | collective-permute-start | bytes 786440 | tf_op jit(solution)/shard_map/ppermute | solution.py:362
  22.6 11.7 %collective-permute-done.7.r_a = bf16[1024,128]{1,0:T(8,128)(2,1)S(1)} collective-permute-done((bf16[1024,128]{1,0:T(8,128)(2,1)S(1)}, bf16[1024,128]{1,0:T(8,128)(2,1)S(1)}, u32[]{:S(2)}, u32[]{:S(2)}) %collective-permute-start.7) | collective-permute-done | bytes 262176 | tf_op jit(solution)/shard_map/ppermute | solution.py:362
  34.3 0.0 collective-permute-done.8.r_c
  34.3 0.0 collective-permute-done.9.r_b
  34.3 0.8 %unpack.1 = (bf16[256,256]{1,0:T(8,128)(2,1)}, bf16[256,256]{1,0:T(8,128)(2,1)}, bf16[256,256]{1,0:T(8,128)(2,1)}, bf16[256,256]{1,0:T(8,128)(2,1)}) custom-call(bf16[1024,128]{1,0:T(8,128)(2,1)S(1)} %get-tuple-element.34.own, bf16[1024,128]{1,0:T(8,128)(2,1)S(1)} %collective-permute-done.7.r_a, bf16[1024,128]{1,0:T(8,128)(2,1)S(1)} %collective-permute-done.8.r_c, ...), custom_call_target="tpu_custom_call" | custom-call | tf_op jit(solution)/shard_map/unpack/pallas_call | solution.py:389
  (1 shorter events, 0.0 us)
Async XLA Ops:
  2.1 9.4 %collective-permute-start.1 = (bf16[1024,128]{1,0:T(8,128)(2,1)S(1)}, bf16[1024,128]{1,0:T(8,128)(2,1)S(1)}, u32[]{:S(2)}, u32[]{:S(2)}) collective-permute-start(bf16[1024,128]{1,0:T(8,128)(2,1)S(1)} %get-tuple-element.28), channel_id=1, source_target_pairs={{1,9},{13,5},{3,11},{15,7},{17,25},{29,21},{19,27},{31,23}} | collective-permute-start | bytes 786440 | tf_op jit(solution)/shard_map/ppermute | solution.py:365
  2.8 6.8 %collective-permute-start = (bf16[16,128]{1,0:T(8,128)(2,1)S(1)}, bf16[16,128]{1,0:T(8,128)(2,1)S(1)}, u32[]{:S(2)}, u32[]{:S(2)}) collective-permute-start(bf16[16,128]{1,0:T(8,128)(2,1)S(1)} %get-tuple-element.25), channel_id=1, source_target_pairs={{1,0},{5,4},{9,8},{13,12},{3,2},{7,6},{11,10},{15,14},{17,16},{21,... | collective-permute-start | bytes 12296 | tf_op jit(solution)/shard_map/ppermute | solution.py:370
  4.1 11.3 %collective-permute-start.2 = (bf16[1024,128]{1,0:T(8,128)(2,1)S(1)}, bf16[1024,128]{1,0:T(8,128)(2,1)S(1)}, u32[]{:S(2)}, u32[]{:S(2)}) collective-permute-start(bf16[1024,128]{1,0:T(8,128)(2,1)S(1)} %get-tuple-element.29), channel_id=1, source_target_pairs={{1,5},{13,9},{3,7},{15,11},{17,21},{29,25},{19,23},{31,27}} | collective-permute-start | bytes 786440 | tf_op jit(solution)/shard_map/ppermute | solution.py:365
  4.8 10.7 %collective-permute-start.3 = (bf16[1024,128]{1,0:T(8,128)(2,1)S(1)}, bf16[1024,128]{1,0:T(8,128)(2,1)S(1)}, u32[]{:S(2)}, u32[]{:S(2)}) collective-permute-start(bf16[1024,128]{1,0:T(8,128)(2,1)S(1)} %get-tuple-element.30), channel_id=1, source_target_pairs={{5,9},{9,5},{7,11},{11,7},{21,25},{25,21},{23,27},{27,23}} | collective-permute-start | bytes 786440 | tf_op jit(solution)/shard_map/ppermute | solution.py:365
  9.6 6.8 %collective-permute-start.4 = (bf16[1024,128]{1,0:T(8,128)(2,1)S(1)}, bf16[1024,128]{1,0:T(8,128)(2,1)S(1)}, u32[]{:S(2)}, u32[]{:S(2)}) collective-permute-start(bf16[1024,128]{1,0:T(8,128)(2,1)S(1)} %get-tuple-element.31), channel_id=1, source_target_pairs={{0,4},{12,8},{2,6},{14,10},{16,20},{28,24},{18,22},{30,26}} | collective-permute-start | bytes 786440 | tf_op jit(solution)/shard_map/ppermute | solution.py:365
  10.9 5.5 %collective-permute-start.5 = (bf16[1024,128]{1,0:T(8,128)(2,1)S(1)}, bf16[1024,128]{1,0:T(8,128)(2,1)S(1)}, u32[]{:S(2)}, u32[]{:S(2)}) collective-permute-start(bf16[1024,128]{1,0:T(8,128)(2,1)S(1)} %get-tuple-element.32), channel_id=1, source_target_pairs={{4,8},{8,4},{6,10},{10,6},{20,24},{24,20},{22,26},{26,22}} | collective-permute-start | bytes 786440 | tf_op jit(solution)/shard_map/ppermute | solution.py:365
  11.6 7.8 %collective-permute-start.6 = (bf16[1024,128]{1,0:T(8,128)(2,1)S(1)}, bf16[1024,128]{1,0:T(8,128)(2,1)S(1)}, u32[]{:S(2)}, u32[]{:S(2)}) collective-permute-start(bf16[1024,128]{1,0:T(8,128)(2,1)S(1)} %get-tuple-element.33), channel_id=1, source_target_pairs={{0,8},{12,4},{2,10},{14,6},{16,24},{28,20},{18,26},{30,22}} | collective-permute-start | bytes 786440 | tf_op jit(solution)/shard_map/ppermute | solution.py:365
  19.3 15.0 %collective-permute-start.7 = (bf16[1024,128]{1,0:T(8,128)(2,1)S(1)}, bf16[1024,128]{1,0:T(8,128)(2,1)S(1)}, u32[]{:S(2)}, u32[]{:S(2)}) collective-permute-start(bf16[1024,128]{1,0:T(8,128)(2,1)S(1)} %get-tuple-element.35), channel_id=1, source_target_pairs={{4,0},{8,12},{5,1},{9,13},{6,2},{10,14},{7,3},{11,15},{20,16},{24,... | collective-permute-start | bytes 786440 | tf_op jit(solution)/shard_map/ppermute | solution.py:362
  20.6 13.7 %collective-permute-start.8 = (bf16[1024,128]{1,0:T(8,128)(2,1)S(1)}, bf16[1024,128]{1,0:T(8,128)(2,1)S(1)}, u32[]{:S(2)}, u32[]{:S(2)}) collective-permute-start(bf16[1024,128]{1,0:T(8,128)(2,1)S(1)} %get-tuple-element.36), channel_id=1, source_target_pairs={{4,12},{8,0},{5,13},{9,1},{6,14},{10,2},{7,15},{11,3},{20,28},{24,... | collective-permute-start | bytes 786440 | tf_op jit(solution)/shard_map/ppermute | solution.py:362
  21.9 12.4 %collective-permute-start.9 = (bf16[1024,128]{1,0:T(8,128)(2,1)S(1)}, bf16[1024,128]{1,0:T(8,128)(2,1)S(1)}, u32[]{:S(2)}, u32[]{:S(2)}) collective-permute-start(bf16[1024,128]{1,0:T(8,128)(2,1)S(1)} %get-tuple-element.37), channel_id=1, source_target_pairs={{4,8},{8,4},{5,9},{9,5},{6,10},{10,6},{7,11},{11,7},{20,24},{24,20... | collective-permute-start | bytes 786440 | tf_op jit(solution)/shard_map/ppermute | solution.py:362

commit v6 on v5

--- a/solution.py
+++ b/solution.py
@@ -236,6 +236,7 @@
         query_at = lax.broadcasted_iota(jnp.int32, (HALF, HALF), 1)
         seen = key_at <= query_at
         tail = lambda whole, part: jnp.concatenate([whole[:, :HALF], part(whole[:, HALF:])], axis=1)
+        stages = []
         for i in range(total // BLOCK):
             lo = slice(i * BLOCK, i * BLOCK + HALF)
             hi = slice(i * BLOCK + HALF, (i + 1) * BLOCK)
@@ -256,6 +257,9 @@
             sh = jnp.where(seen, dot(k[hi, :], qh, NT) * (FACTOR * LOG2E), -1e30)
             s[hi, hi] = sh
             top = tail(top, lambda x: jnp.maximum(x, jnp.max(sh, axis=0, keepdims=True)))
+            stages.append((lo, hi, ri, olds, qb, qh, top))
+        later = []
+        for lo, hi, ri, olds, qb, qh, top in stages:
             weight, acc = None, None
             for rj in olds:
                 pj = jnp.exp2(s[rj, ri] - top)
@@ -303,20 +307,19 @@
             dst[part(3, e), :] = dv[where, :].astype(BF)
 
 
-def pack_kernel(order, q, k, v, g, rest1, hopl1, hopr1, hopl0, hopr0, rest0, mine, turn, order_out, sem, order_sem):
+def pack_kernel(order, q, k, v, g, rest1, outer1, cross1, outer0, cross0, rest0, mine, turn, order_out, sem, order_sem):
     sh = q.shape[0]
     _, side, owner = place_here()
-    rest_half = jnp.where(owner, side, 1 - side)
     turn[...] = jnp.zeros_like(turn)
-    for core, hopl, hopr, rest in ((0, hopl0, hopr0, rest0), (1, hopl1, hopr1, rest1)):
-        @pl.when(lax.axis_index("mp") == core)
-        def _():
-            halves = ((rest, 1 - side), (hopl, 1 - rest_half), (hopr, 1 - rest_half), (mine, side))
-            run_copies([
-                pltpu.make_async_copy(src.at[:, columns(half)], dst.at[n * sh:(n + 1) * sh, :], sem.at[m, n])
-                for m, (dst, half) in enumerate(halves)
-                for n, src in enumerate((q, k, v, g))
-            ] + [pltpu.make_async_copy(order, order_out, order_sem)])
+    for core, outer, cross, rest in ((0, outer0, cross0, rest0), (1, outer1, cross1, rest1)):
+        for held, halves in ((True, ((cross, 1 - side), (mine, side))), (False, ((rest, 1 - side), (outer, side)))):
+            @pl.when((lax.axis_index("mp") == core) & (owner == held))
+            def _():
+                run_copies([
+                    pltpu.make_async_copy(src.at[:, columns(half)], dst.at[n * sh:(n + 1) * sh, :], sem.at[m, n])
+                    for m, (dst, half) in enumerate(halves)
+                    for n, src in enumerate((q, k, v, g))
+                ] + [pltpu.make_async_copy(order, order_out, order_sem)])
 
 
 def unpack_kernel(own, r_a, r_c, r_b, *refs):
@@ -351,12 +354,12 @@
     per_row = ((total, HEAD_DIM), BF)
     per_column = ((HEAD_DIM, total), BF)
     wide = ((total, HEAD_DIM), F32)
-    rest1, hopl1, hopr1, hopl0, hopr0, rest0, mine, turn, order = pl.pallas_call(
+    rest1, outer1, cross1, outer0, cross0, rest0, mine, turn, order = pl.pallas_call(
         pack_kernel,
         out_shape=in_vmem(*(stack,) * 7, ((16, HEAD_DIM), BF)) + (pltpu.SMEM(span_order.shape, span_order.dtype),),
         in_specs=[anywhere] * 5,
         out_specs=(vm,) * 8 + (sm,),
-        scratch_shapes=[pltpu.SemaphoreType.DMA((4, 4)), pltpu.SemaphoreType.DMA],
+        scratch_shapes=[pltpu.SemaphoreType.DMA((2, 4)), pltpu.SemaphoreType.DMA],
         name="pack",
     )(span_order, queries, keys, values, grad_out)
     go = lambda x, pairs: lax.ppermute(x, "seq", pairs)
@@ -365,12 +368,12 @@
         return lax.ppermute(x, ("seq", "mp"), [(2 * a + core, 2 * b + core) for a, b in pairs])
 
     g_c1 = go_core(rest1, [(0, 2), (3, 1)], 1)
-    g_a1 = go_core(hopl1, [(0, 1), (3, 2)], 1)
-    g_b1 = go_core(hopr1, [(1, 2), (2, 1)], 1)
+    g_a1 = go_core(outer1, [(0, 1), (3, 2)], 1)
+    g_b1 = go_core(cross1, [(1, 2), (2, 1)], 1)
     turn = lax.ppermute(turn, ("seq", "mp"), [(2 * a + 1, 2 * a + 0) for a in range(4)])
-    hopl0, hopr0, rest0, turn = lax.optimization_barrier((hopl0, hopr0, rest0, turn))
-    g_a0 = go_core(hopl0, [(0, 1), (3, 2)], 0)
-    g_b0 = go_core(hopr0, [(1, 2), (2, 1)], 0)
+    outer0, cross0, rest0, turn = lax.optimization_barrier((outer0, cross0, rest0, turn))
+    g_a0 = go_core(outer0, [(0, 1), (3, 2)], 0)
+    g_b0 = go_core(cross0, [(1, 2), (2, 1)], 0)
     g_c0 = go_core(rest0, [(0, 2), (3, 1)], 0)
     own, to_a, to_c, to_b = pl.pallas_call(
         owner_kernel,

time: 35.5 us -> 34.9 us (0.983)
    ppermute x3, waiting for transfers between devices: 11.7 us -> 11.4 us  [owned_per_device(): go = lambda x, pairs: lax.ppermute(x, 'seq', pairs)]
where the time goes in v6:
time: 34.9 us; the launch traced here: 34.6 us
  waiting for transfers between devices  19.4 us (56%)
  starting transfers between devices  12.5 us (36%)
  Pallas kernels  2.03 us (6%)
  between operations  0.75 us (2%)
    ppermute x3, waiting for transfers between devices, owned_per_device(): go = lambda x, pairs: lax.ppermute(x, 'seq', pairs)  11.4 us
    ppermute x6, starting transfers between devices, go_core(): lax.ppermute(x, ('seq', 'mp'), [(2 * a + core, 2 * b + core) for a, b in...  7.92 us
    ppermute x1, waiting for transfers between devices, owned_per_device(): lax.ppermute(turn, ('seq', 'mp'), [(2 * a + 1, 2 * a + 0) for a in range(...  4.1 us
    ppermute x6, waiting for transfers between devices, go_core(): lax.ppermute(x, ('seq', 'mp'), [(2 * a + core, 2 * b + core) for a, b in...  3.89 us
    ppermute x3, starting transfers between devices, owned_per_device(): go = lambda x, pairs: lax.ppermute(x, 'seq', pairs)  3.25 us
    ppermute x1, starting transfers between devices, owned_per_device(): lax.ppermute(turn, ('seq', 'mp'), [(2 * a + 1, 2 * a + 0) for a in range(...  1.29 us
    pallas_call x1, Pallas kernels, owned_per_device(): pl.pallas_call(pack_kernel, out_shape=in_vmem(*(stack,) * 7, ((16, HEAD_D...  1.18 us
    pallas_call x1, Pallas kernels, owned_per_device(): pl.pallas_call(unpack_kernel, out_shape=(jax.ShapeDtypeStruct(queries.sha...  0.85 us
  transfers between devices with their start and end apart: 10, of which 4 were waited for; matrix products, arithmetic and copies ran while one was open for 0% of the time, Pallas kernels for 0%

profile of v6, /device:TPU:0, one launch (start us, length us, event | category | flops | bytes accessed | tf_op | source)
XLA Modules:
  0.0 34.6 jit_solution(4194488092007640441)
XLA Ops:
  0.6 1.2 %pack.1 = (bf16[1024,128]{1,0:T(8,128)(2,1)S(1)}, bf16[1024,128]{1,0:T(8,128)(2,1)S(1)}, bf16[1024,128]{1,0:T(8,128)(2,1)S(1)}, bf16[1024,128]{1,0:T(8,128)(2,1)...) custom-call(s32[8]{0:T(128)} %order.1, ...), custom_call_target="tpu_custom_call" | custom-call | tf_op jit(solution)/shard_map/pack/pallas_call | solution.py:357
  1.8 0.7 %collective-permute-start.1 = (bf16[1024,128]{1,0:T(8,128)(2,1)S(1)}, bf16[1024,128]{1,0:T(8,128)(2,1)S(1)}, u32[]{:S(2)}, u32[]{:S(2)}) collective-permute-start(bf16[1024,128]{1,0:T(8,128)(2,1)S(1)} %get-tuple-element.28), channel_id=1, source_target_pairs={{1,9},{13,5},{3,11},{15,7},{17,25},{29,21},{19,27},{31,23}} | collective-permute-start | bytes 786440 | tf_op jit(solution)/shard_map/ppermute | solution.py:368
  2.5 1.3 %collective-permute-start = (bf16[16,128]{1,0:T(8,128)(2,1)S(1)}, bf16[16,128]{1,0:T(8,128)(2,1)S(1)}, u32[]{:S(2)}, u32[]{:S(2)}) collective-permute-start(bf16[16,128]{1,0:T(8,128)(2,1)S(1)} %get-tuple-element.25), channel_id=1, source_target_pairs={{1,0},{5,4},{9,8},{13,12},{3,2},{7,6},{11,10},{15,14},{17,16},{21,... | collective-permute-start | bytes 12296 | tf_op jit(solution)/shard_map/ppermute | solution.py:373
  3.8 0.7 %collective-permute-start.2 = (bf16[1024,128]{1,0:T(8,128)(2,1)S(1)}, bf16[1024,128]{1,0:T(8,128)(2,1)S(1)}, u32[]{:S(2)}, u32[]{:S(2)}) collective-permute-start(bf16[1024,128]{1,0:T(8,128)(2,1)S(1)} %get-tuple-element.29), channel_id=1, source_target_pairs={{1,5},{13,9},{3,7},{15,11},{17,21},{29,25},{19,23},{31,27}} | collective-permute-start | bytes 786440 | tf_op jit(solution)/shard_map/ppermute | solution.py:368
  4.5 0.7 %collective-permute-start.3 = (bf16[1024,128]{1,0:T(8,128)(2,1)S(1)}, bf16[1024,128]{1,0:T(8,128)(2,1)S(1)}, u32[]{:S(2)}, u32[]{:S(2)}) collective-permute-start(bf16[1024,128]{1,0:T(8,128)(2,1)S(1)} %get-tuple-element.30), channel_id=1, source_target_pairs={{5,9},{9,5},{7,11},{11,7},{21,25},{25,21},{23,27},{27,23}} | collective-permute-start | bytes 786440 | tf_op jit(solution)/shard_map/ppermute | solution.py:368
  5.2 4.1 %collective-permute-done.turn = bf16[16,128]{1,0:T(8,128)(2,1)S(1)} collective-permute-done((bf16[16,128]{1,0:T(8,128)(2,1)S(1)}, bf16[16,128]{1,0:T(8,128)(2,1)S(1)}, u32[]{:S(2)}, u32[]{:S(2)}) %collective-permute-start) | collective-permute-done | bytes 4128 | tf_op jit(solution)/shard_map/ppermute | solution.py:373
  9.3 1.3 %collective-permute-start.4 = (bf16[1024,128]{1,0:T(8,128)(2,1)S(1)}, bf16[1024,128]{1,0:T(8,128)(2,1)S(1)}, u32[]{:S(2)}, u32[]{:S(2)}) collective-permute-start(bf16[1024,128]{1,0:T(8,128)(2,1)S(1)} %get-tuple-element.31), channel_id=1, source_target_pairs={{0,4},{12,8},{2,6},{14,10},{16,20},{28,24},{18,22},{30,26}} | collective-permute-start | bytes 786440 | tf_op jit(solution)/shard_map/ppermute | solution.py:368
  10.6 0.7 %collective-permute-start.5 = (bf16[1024,128]{1,0:T(8,128)(2,1)S(1)}, bf16[1024,128]{1,0:T(8,128)(2,1)S(1)}, u32[]{:S(2)}, u32[]{:S(2)}) collective-permute-start(bf16[1024,128]{1,0:T(8,128)(2,1)S(1)} %get-tuple-element.32), channel_id=1, source_target_pairs={{4,8},{8,4},{6,10},{10,6},{20,24},{24,20},{22,26},{26,22}} | collective-permute-start | bytes 786440 | tf_op jit(solution)/shard_map/ppermute | solution.py:368
  11.3 0.0 collective-permute-done.1.s_c1
  11.3 3.9 %collective-permute-start.6 = (bf16[1024,128]{1,0:T(8,128)(2,1)S(1)}, bf16[1024,128]{1,0:T(8,128)(2,1)S(1)}, u32[]{:S(2)}, u32[]{:S(2)}) collective-permute-start(bf16[1024,128]{1,0:T(8,128)(2,1)S(1)} %get-tuple-element.33), channel_id=1, source_target_pairs={{0,8},{12,4},{2,10},{14,6},{16,24},{28,20},{18,26},{30,22}} | collective-permute-start | bytes 786440 | tf_op jit(solution)/shard_map/ppermute | solution.py:368
  15.2 0.0 collective-permute-done.2.s_a1
  15.2 0.0 collective-permute-done.3.s_b1
  15.2 0.9 %collective-permute-done.4.s_a0 = bf16[1024,128]{1,0:T(8,128)(2,1)S(1)} collective-permute-done((bf16[1024,128]{1,0:T(8,128)(2,1)S(1)}, bf16[1024,128]{1,0:T(8,128)(2,1)S(1)}, u32[]{:S(2)}, u32[]{:S(2)}) %collective-permute-start.4) | collective-permute-done | bytes 262176 | tf_op jit(solution)/shard_map/ppermute | solution.py:368
  16.1 0.0 collective-permute-done.5.s_b0
  16.1 3.0 %collective-permute-done.6.s_c0 = bf16[1024,128]{1,0:T(8,128)(2,1)S(1)} collective-permute-done((bf16[1024,128]{1,0:T(8,128)(2,1)S(1)}, bf16[1024,128]{1,0:T(8,128)(2,1)S(1)}, u32[]{:S(2)}, u32[]{:S(2)}) %collective-permute-start.6) | collective-permute-done | bytes 262176 | tf_op jit(solution)/shard_map/ppermute | solution.py:368
  19.1 1.3 %collective-permute-start.7 = (bf16[1024,128]{1,0:T(8,128)(2,1)S(1)}, bf16[1024,128]{1,0:T(8,128)(2,1)S(1)}, u32[]{:S(2)}, u32[]{:S(2)}) collective-permute-start(bf16[1024,128]{1,0:T(8,128)(2,1)S(1)} %get-tuple-element.35), channel_id=1, source_target_pairs={{4,0},{8,12},{5,1},{9,13},{6,2},{10,14},{7,3},{11,15},{20,16},{24,... | collective-permute-start | bytes 786440 | tf_op jit(solution)/shard_map/ppermute | solution.py:365
  20.4 1.3 %collective-permute-start.8 = (bf16[1024,128]{1,0:T(8,128)(2,1)S(1)}, bf16[1024,128]{1,0:T(8,128)(2,1)S(1)}, u32[]{:S(2)}, u32[]{:S(2)}) collective-permute-start(bf16[1024,128]{1,0:T(8,128)(2,1)S(1)} %get-tuple-element.36), channel_id=1, source_target_pairs={{4,12},{8,0},{5,13},{9,1},{6,14},{10,2},{7,15},{11,3},{20,28},{24,... | collective-permute-start | bytes 786440 | tf_op jit(solution)/shard_map/ppermute | solution.py:365
  21.7 0.7 %collective-permute-start.9 = (bf16[1024,128]{1,0:T(8,128)(2,1)S(1)}, bf16[1024,128]{1,0:T(8,128)(2,1)S(1)}, u32[]{:S(2)}, u32[]{:S(2)}) collective-permute-start(bf16[1024,128]{1,0:T(8,128)(2,1)S(1)} %get-tuple-element.37), channel_id=1, source_target_pairs={{4,8},{8,4},{5,9},{9,5},{6,10},{10,6},{7,11},{11,7},{20,24},{24,20... | collective-permute-start | bytes 786440 | tf_op jit(solution)/shard_map/ppermute | solution.py:365
  22.4 11.4 %collective-permute-done.7.r_a = bf16[1024,128]{1,0:T(8,128)(2,1)S(1)} collective-permute-done((bf16[1024,128]{1,0:T(8,128)(2,1)S(1)}, bf16[1024,128]{1,0:T(8,128)(2,1)S(1)}, u32[]{:S(2)}, u32[]{:S(2)}) %collective-permute-start.7) | collective-permute-done | bytes 262176 | tf_op jit(solution)/shard_map/ppermute | solution.py:365
  33.7 0.0 collective-permute-done.8.r_c
  33.7 0.0 collective-permute-done.9.r_b
  33.7 0.8 %unpack.1 = (bf16[256,256]{1,0:T(8,128)(2,1)}, bf16[256,256]{1,0:T(8,128)(2,1)}, bf16[256,256]{1,0:T(8,128)(2,1)}, bf16[256,256]{1,0:T(8,128)(2,1)}) custom-call(bf16[1024,128]{1,0:T(8,128)(2,1)S(1)} %get-tuple-element.34.own, bf16[1024,128]{1,0:T(8,128)(2,1)S(1)} %collective-permute-done.7.r_a, bf16[1024,128]{1,0:T(8,128)(2,1)S(1)} %collective-permute-done.8.r_c, ...), custom_call_target="tpu_custom_call" | custom-call | tf_op jit(solution)/shard_map/unpack/pallas_call | solution.py:392
  (1 shorter events, 0.0 us)
Async XLA Ops:
  1.8 9.4 %collective-permute-start.1 = (bf16[1024,128]{1,0:T(8,128)(2,1)S(1)}, bf16[1024,128]{1,0:T(8,128)(2,1)S(1)}, u32[]{:S(2)}, u32[]{:S(2)}) collective-permute-start(bf16[1024,128]{1,0:T(8,128)(2,1)S(1)} %get-tuple-element.28), channel_id=1, source_target_pairs={{1,9},{13,5},{3,11},{15,7},{17,25},{29,21},{19,27},{31,23}} | collective-permute-start | bytes 786440 | tf_op jit(solution)/shard_map/ppermute | solution.py:368
  2.5 6.8 %collective-permute-start = (bf16[16,128]{1,0:T(8,128)(2,1)S(1)}, bf16[16,128]{1,0:T(8,128)(2,1)S(1)}, u32[]{:S(2)}, u32[]{:S(2)}) collective-permute-start(bf16[16,128]{1,0:T(8,128)(2,1)S(1)} %get-tuple-element.25), channel_id=1, source_target_pairs={{1,0},{5,4},{9,8},{13,12},{3,2},{7,6},{11,10},{15,14},{17,16},{21,... | collective-permute-start | bytes 12296 | tf_op jit(solution)/shard_map/ppermute | solution.py:373
  3.8 11.4 %collective-permute-start.2 = (bf16[1024,128]{1,0:T(8,128)(2,1)S(1)}, bf16[1024,128]{1,0:T(8,128)(2,1)S(1)}, u32[]{:S(2)}, u32[]{:S(2)}) collective-permute-start(bf16[1024,128]{1,0:T(8,128)(2,1)S(1)} %get-tuple-element.29), channel_id=1, source_target_pairs={{1,5},{13,9},{3,7},{15,11},{17,21},{29,25},{19,23},{31,27}} | collective-permute-start | bytes 786440 | tf_op jit(solution)/shard_map/ppermute | solution.py:368
  4.5 10.7 %collective-permute-start.3 = (bf16[1024,128]{1,0:T(8,128)(2,1)S(1)}, bf16[1024,128]{1,0:T(8,128)(2,1)S(1)}, u32[]{:S(2)}, u32[]{:S(2)}) collective-permute-start(bf16[1024,128]{1,0:T(8,128)(2,1)S(1)} %get-tuple-element.30), channel_id=1, source_target_pairs={{5,9},{9,5},{7,11},{11,7},{21,25},{25,21},{23,27},{27,23}} | collective-permute-start | bytes 786440 | tf_op jit(solution)/shard_map/ppermute | solution.py:368
  9.3 6.8 %collective-permute-start.4 = (bf16[1024,128]{1,0:T(8,128)(2,1)S(1)}, bf16[1024,128]{1,0:T(8,128)(2,1)S(1)}, u32[]{:S(2)}, u32[]{:S(2)}) collective-permute-start(bf16[1024,128]{1,0:T(8,128)(2,1)S(1)} %get-tuple-element.31), channel_id=1, source_target_pairs={{0,4},{12,8},{2,6},{14,10},{16,20},{28,24},{18,22},{30,26}} | collective-permute-start | bytes 786440 | tf_op jit(solution)/shard_map/ppermute | solution.py:368
  10.6 5.5 %collective-permute-start.5 = (bf16[1024,128]{1,0:T(8,128)(2,1)S(1)}, bf16[1024,128]{1,0:T(8,128)(2,1)S(1)}, u32[]{:S(2)}, u32[]{:S(2)}) collective-permute-start(bf16[1024,128]{1,0:T(8,128)(2,1)S(1)} %get-tuple-element.32), channel_id=1, source_target_pairs={{4,8},{8,4},{6,10},{10,6},{20,24},{24,20},{22,26},{26,22}} | collective-permute-start | bytes 786440 | tf_op jit(solution)/shard_map/ppermute | solution.py:368
  11.3 7.8 %collective-permute-start.6 = (bf16[1024,128]{1,0:T(8,128)(2,1)S(1)}, bf16[1024,128]{1,0:T(8,128)(2,1)S(1)}, u32[]{:S(2)}, u32[]{:S(2)}) collective-permute-start(bf16[1024,128]{1,0:T(8,128)(2,1)S(1)} %get-tuple-element.33), channel_id=1, source_target_pairs={{0,8},{12,4},{2,10},{14,6},{16,24},{28,20},{18,26},{30,22}} | collective-permute-start | bytes 786440 | tf_op jit(solution)/shard_map/ppermute | solution.py:368
  19.1 14.6 %collective-permute-start.7 = (bf16[1024,128]{1,0:T(8,128)(2,1)S(1)}, bf16[1024,128]{1,0:T(8,128)(2,1)S(1)}, u32[]{:S(2)}, u32[]{:S(2)}) collective-permute-start(bf16[1024,128]{1,0:T(8,128)(2,1)S(1)} %get-tuple-element.35), channel_id=1, source_target_pairs={{4,0},{8,12},{5,1},{9,13},{6,2},{10,14},{7,3},{11,15},{20,16},{24,... | collective-permute-start | bytes 786440 | tf_op jit(solution)/shard_map/ppermute | solution.py:365
  20.4 13.3 %collective-permute-start.8 = (bf16[1024,128]{1,0:T(8,128)(2,1)S(1)}, bf16[1024,128]{1,0:T(8,128)(2,1)S(1)}, u32[]{:S(2)}, u32[]{:S(2)}) collective-permute-start(bf16[1024,128]{1,0:T(8,128)(2,1)S(1)} %get-tuple-element.36), channel_id=1, source_target_pairs={{4,12},{8,0},{5,13},{9,1},{6,14},{10,2},{7,15},{11,3},{20,28},{24,... | collective-permute-start | bytes 786440 | tf_op jit(solution)/shard_map/ppermute | solution.py:365
  21.7 12.0 %collective-permute-start.9 = (bf16[1024,128]{1,0:T(8,128)(2,1)S(1)}, bf16[1024,128]{1,0:T(8,128)(2,1)S(1)}, u32[]{:S(2)}, u32[]{:S(2)}) collective-permute-start(bf16[1024,128]{1,0:T(8,128)(2,1)S(1)} %get-tuple-element.37), channel_id=1, source_target_pairs={{4,8},{8,4},{5,9},{9,5},{6,10},{10,6},{7,11},{11,7},{20,24},{24,20... | collective-permute-start | bytes 786440 | tf_op jit(solution)/shard_map/ppermute | solution.py:365

commit v7 on v6

--- a/solution.py
+++ b/solution.py
@@ -206,7 +206,7 @@
         one.wait()
 
 
-def owner_kernel(order_ref, turn, own, s_c1, s_a1, s_b1, s_a0, s_b0, s_c0, o_own, o_a, o_c, o_b, q, k, v, g, kt, vt, s, dk, dv):
+def owner_kernel(order_ref, turn, own, s_c1, s_a1, s_b1, s_a0, s_c0, s_b0, o_own, o_a, o_c, o_b, q, k, v, g, kt, vt, s, dk, dv):
     me, side, held = place_here()
     rows = own.shape[0] // 4
     total = 4 * rows
@@ -373,8 +373,8 @@
     turn = lax.ppermute(turn, ("seq", "mp"), [(2 * a + 1, 2 * a + 0) for a in range(4)])
     outer0, cross0, rest0, turn = lax.optimization_barrier((outer0, cross0, rest0, turn))
     g_a0 = go_core(outer0, [(0, 1), (3, 2)], 0)
+    g_c0 = go_core(rest0, [(0, 2), (3, 1)], 0)
     g_b0 = go_core(cross0, [(1, 2), (2, 1)], 0)
-    g_c0 = go_core(rest0, [(0, 2), (3, 1)], 0)
     own, to_a, to_c, to_b = pl.pallas_call(
         owner_kernel,
         out_shape=in_vmem(*(stack,) * 4),
@@ -385,7 +385,7 @@
         ],
         compiler_params=pltpu.CompilerParams(vmem_limit_bytes=32 << 20),
         name="owner",
-    )(order, *kept(turn, mine, g_c1, g_a1, g_b1, g_a0, g_b0, g_c0))
+    )(order, *kept(turn, mine, g_c1, g_a1, g_b1, g_a0, g_c0, g_b0))
     r_a = go(to_a, [(1, 0), (2, 3)])
     r_b = go(to_b, [(1, 2), (2, 1)])
     r_c = go(to_c, [(1, 3), (2, 0)])

time: 34.9 us -> 34.6 us (level)
  starting transfers between devices: 12.5 us -> 10.8 us
  waiting for transfers between devices: 19.4 us -> 20.8 us
    ppermute x6, starting transfers between devices: 7.92 us -> 6.24 us  [go_core(): lax.ppermute(x, ('seq', 'mp'), [(2 * a + core, 2 * b + core) for a, b in...]
    ppermute x6, waiting for transfers between devices: 3.89 us -> 5.45 us  [go_core(): lax.ppermute(x, ('seq', 'mp'), [(2 * a + core, 2 * b + core) for a, b in...]
where the time goes in v7:
time: 34.6 us; the launch traced here: 34.3 us
  waiting for transfers between devices  20.8 us (60%)
  starting transfers between devices  10.8 us (31%)
  Pallas kernels  2.03 us (6%)
  between operations  0.75 us (2%)
    ppermute x3, waiting for transfers between devices, owned_per_device(): go = lambda x, pairs: lax.ppermute(x, 'seq', pairs)  11.2 us
    ppermute x6, starting transfers between devices, go_core(): lax.ppermute(x, ('seq', 'mp'), [(2 * a + core, 2 * b + core) for a, b in...  6.24 us
    ppermute x6, waiting for transfers between devices, go_core(): lax.ppermute(x, ('seq', 'mp'), [(2 * a + core, 2 * b + core) for a, b in...  5.45 us
    ppermute x1, waiting for transfers between devices, owned_per_device(): lax.ppermute(turn, ('seq', 'mp'), [(2 * a + 1, 2 * a + 0) for a in range(...  4.1 us
    ppermute x3, starting transfers between devices, owned_per_device(): go = lambda x, pairs: lax.ppermute(x, 'seq', pairs)  3.25 us
    ppermute x1, starting transfers between devices, owned_per_device(): lax.ppermute(turn, ('seq', 'mp'), [(2 * a + 1, 2 * a + 0) for a in range(...  1.29 us
    pallas_call x1, Pallas kernels, owned_per_device(): pl.pallas_call(pack_kernel, out_shape=in_vmem(*(stack,) * 7, ((16, HEAD_D...  1.18 us
    pallas_call x1, Pallas kernels, owned_per_device(): pl.pallas_call(unpack_kernel, out_shape=(jax.ShapeDtypeStruct(queries.sha...  0.85 us
  transfers between devices with their start and end apart: 10, of which 4 were waited for; matrix products, arithmetic and copies ran while one was open for 0% of the time, Pallas kernels for 0%

profile of v7, /device:TPU:0, one launch (start us, length us, event | category | flops | bytes accessed | tf_op | source)
XLA Modules:
  0.0 34.3 jit_solution(12813044556377377233)
XLA Ops:
  0.6 1.2 %pack.1 = (bf16[1024,128]{1,0:T(8,128)(2,1)S(1)}, bf16[1024,128]{1,0:T(8,128)(2,1)S(1)}, bf16[1024,128]{1,0:T(8,128)(2,1)S(1)}, bf16[1024,128]{1,0:T(8,128)(2,1)...) custom-call(s32[8]{0:T(128)} %order.1, ...), custom_call_target="tpu_custom_call" | custom-call | tf_op jit(solution)/shard_map/pack/pallas_call | solution.py:357
  1.8 0.7 %collective-permute-start.1 = (bf16[1024,128]{1,0:T(8,128)(2,1)S(1)}, bf16[1024,128]{1,0:T(8,128)(2,1)S(1)}, u32[]{:S(2)}, u32[]{:S(2)}) collective-permute-start(bf16[1024,128]{1,0:T(8,128)(2,1)S(1)} %get-tuple-element.28), channel_id=1, source_target_pairs={{1,9},{13,5},{3,11},{15,7},{17,25},{29,21},{19,27},{31,23}} | collective-permute-start | bytes 786440 | tf_op jit(solution)/shard_map/ppermute | solution.py:368
  2.5 1.3 %collective-permute-start = (bf16[16,128]{1,0:T(8,128)(2,1)S(1)}, bf16[16,128]{1,0:T(8,128)(2,1)S(1)}, u32[]{:S(2)}, u32[]{:S(2)}) collective-permute-start(bf16[16,128]{1,0:T(8,128)(2,1)S(1)} %get-tuple-element.25), channel_id=1, source_target_pairs={{1,0},{5,4},{9,8},{13,12},{3,2},{7,6},{11,10},{15,14},{17,16},{21,... | collective-permute-start | bytes 12296 | tf_op jit(solution)/shard_map/ppermute | solution.py:373
  3.8 0.7 %collective-permute-start.2 = (bf16[1024,128]{1,0:T(8,128)(2,1)S(1)}, bf16[1024,128]{1,0:T(8,128)(2,1)S(1)}, u32[]{:S(2)}, u32[]{:S(2)}) collective-permute-start(bf16[1024,128]{1,0:T(8,128)(2,1)S(1)} %get-tuple-element.29), channel_id=1, source_target_pairs={{1,5},{13,9},{3,7},{15,11},{17,21},{29,25},{19,23},{31,27}} | collective-permute-start | bytes 786440 | tf_op jit(solution)/shard_map/ppermute | solution.py:368
  4.5 0.7 %collective-permute-start.3 = (bf16[1024,128]{1,0:T(8,128)(2,1)S(1)}, bf16[1024,128]{1,0:T(8,128)(2,1)S(1)}, u32[]{:S(2)}, u32[]{:S(2)}) collective-permute-start(bf16[1024,128]{1,0:T(8,128)(2,1)S(1)} %get-tuple-element.30), channel_id=1, source_target_pairs={{5,9},{9,5},{7,11},{11,7},{21,25},{25,21},{23,27},{27,23}} | collective-permute-start | bytes 786440 | tf_op jit(solution)/shard_map/ppermute | solution.py:368
  5.2 4.1 %collective-permute-done.turn = bf16[16,128]{1,0:T(8,128)(2,1)S(1)} collective-permute-done((bf16[16,128]{1,0:T(8,128)(2,1)S(1)}, bf16[16,128]{1,0:T(8,128)(2,1)S(1)}, u32[]{:S(2)}, u32[]{:S(2)}) %collective-permute-start) | collective-permute-done | bytes 4128 | tf_op jit(solution)/shard_map/ppermute | solution.py:373
  9.3 1.3 %collective-permute-start.4 = (bf16[1024,128]{1,0:T(8,128)(2,1)S(1)}, bf16[1024,128]{1,0:T(8,128)(2,1)S(1)}, u32[]{:S(2)}, u32[]{:S(2)}) collective-permute-start(bf16[1024,128]{1,0:T(8,128)(2,1)S(1)} %get-tuple-element.31), channel_id=1, source_target_pairs={{0,4},{12,8},{2,6},{14,10},{16,20},{28,24},{18,22},{30,26}} | collective-permute-start | bytes 786440 | tf_op jit(solution)/shard_map/ppermute | solution.py:368
  10.6 2.2 %collective-permute-start.5 = (bf16[1024,128]{1,0:T(8,128)(2,1)S(1)}, bf16[1024,128]{1,0:T(8,128)(2,1)S(1)}, u32[]{:S(2)}, u32[]{:S(2)}) collective-permute-start(bf16[1024,128]{1,0:T(8,128)(2,1)S(1)} %get-tuple-element.32), channel_id=1, source_target_pairs={{0,8},{12,4},{2,10},{14,6},{16,24},{28,20},{18,26},{30,22}} | collective-permute-start | bytes 786440 | tf_op jit(solution)/shard_map/ppermute | solution.py:368
  12.8 0.0 collective-permute-done.1.s_c1
  12.8 0.7 %collective-permute-start.6 = (bf16[1024,128]{1,0:T(8,128)(2,1)S(1)}, bf16[1024,128]{1,0:T(8,128)(2,1)S(1)}, u32[]{:S(2)}, u32[]{:S(2)}) collective-permute-start(bf16[1024,128]{1,0:T(8,128)(2,1)S(1)} %get-tuple-element.33), channel_id=1, source_target_pairs={{4,8},{8,4},{6,10},{10,6},{20,24},{24,20},{22,26},{26,22}} | collective-permute-start | bytes 786440 | tf_op jit(solution)/shard_map/ppermute | solution.py:368
  13.5 0.0 collective-permute-done.2.s_a1
  13.5 0.0 collective-permute-done.3.s_b1
  13.5 2.6 %collective-permute-done.4.s_a0 = bf16[1024,128]{1,0:T(8,128)(2,1)S(1)} collective-permute-done((bf16[1024,128]{1,0:T(8,128)(2,1)S(1)}, bf16[1024,128]{1,0:T(8,128)(2,1)S(1)}, u32[]{:S(2)}, u32[]{:S(2)}) %collective-permute-start.4) | collective-permute-done | bytes 262176 | tf_op jit(solution)/shard_map/ppermute | solution.py:368
  16.1 2.9 %collective-permute-done.5.s_c0 = bf16[1024,128]{1,0:T(8,128)(2,1)S(1)} collective-permute-done((bf16[1024,128]{1,0:T(8,128)(2,1)S(1)}, bf16[1024,128]{1,0:T(8,128)(2,1)S(1)}, u32[]{:S(2)}, u32[]{:S(2)}) %collective-permute-start.5) | collective-permute-done | bytes 262176 | tf_op jit(solution)/shard_map/ppermute | solution.py:368
  19.0 0.0 collective-permute-done.6.s_b0
  19.0 1.3 %collective-permute-start.7 = (bf16[1024,128]{1,0:T(8,128)(2,1)S(1)}, bf16[1024,128]{1,0:T(8,128)(2,1)S(1)}, u32[]{:S(2)}, u32[]{:S(2)}) collective-permute-start(bf16[1024,128]{1,0:T(8,128)(2,1)S(1)} %get-tuple-element.35), channel_id=1, source_target_pairs={{4,0},{8,12},{5,1},{9,13},{6,2},{10,14},{7,3},{11,15},{20,16},{24,... | collective-permute-start | bytes 786440 | tf_op jit(solution)/shard_map/ppermute | solution.py:365
  20.3 1.3 %collective-permute-start.8 = (bf16[1024,128]{1,0:T(8,128)(2,1)S(1)}, bf16[1024,128]{1,0:T(8,128)(2,1)S(1)}, u32[]{:S(2)}, u32[]{:S(2)}) collective-permute-start(bf16[1024,128]{1,0:T(8,128)(2,1)S(1)} %get-tuple-element.36), channel_id=1, source_target_pairs={{4,12},{8,0},{5,13},{9,1},{6,14},{10,2},{7,15},{11,3},{20,28},{24,... | collective-permute-start | bytes 786440 | tf_op jit(solution)/shard_map/ppermute | solution.py:365
  21.6 0.7 %collective-permute-start.9 = (bf16[1024,128]{1,0:T(8,128)(2,1)S(1)}, bf16[1024,128]{1,0:T(8,128)(2,1)S(1)}, u32[]{:S(2)}, u32[]{:S(2)}) collective-permute-start(bf16[1024,128]{1,0:T(8,128)(2,1)S(1)} %get-tuple-element.37), channel_id=1, source_target_pairs={{4,8},{8,4},{5,9},{9,5},{6,10},{10,6},{7,11},{11,7},{20,24},{24,20... | collective-permute-start | bytes 786440 | tf_op jit(solution)/shard_map/ppermute | solution.py:365
  22.3 11.2 %collective-permute-done.7.r_a = bf16[1024,128]{1,0:T(8,128)(2,1)S(1)} collective-permute-done((bf16[1024,128]{1,0:T(8,128)(2,1)S(1)}, bf16[1024,128]{1,0:T(8,128)(2,1)S(1)}, u32[]{:S(2)}, u32[]{:S(2)}) %collective-permute-start.7) | collective-permute-done | bytes 262176 | tf_op jit(solution)/shard_map/ppermute | solution.py:365
  33.5 0.0 collective-permute-done.8.r_c
  33.5 0.0 collective-permute-done.9.r_b
  33.5 0.8 %unpack.1 = (bf16[256,256]{1,0:T(8,128)(2,1)}, bf16[256,256]{1,0:T(8,128)(2,1)}, bf16[256,256]{1,0:T(8,128)(2,1)}, bf16[256,256]{1,0:T(8,128)(2,1)}) custom-call(bf16[1024,128]{1,0:T(8,128)(2,1)S(1)} %get-tuple-element.34.own, bf16[1024,128]{1,0:T(8,128)(2,1)S(1)} %collective-permute-done.7.r_a, bf16[1024,128]{1,0:T(8,128)(2,1)S(1)} %collective-permute-done.8.r_c, ...), custom_call_target="tpu_custom_call" | custom-call | tf_op jit(solution)/shard_map/unpack/pallas_call | solution.py:392
  (1 shorter events, 0.0 us)
Async XLA Ops:
  1.8 11.0 %collective-permute-start.1 = (bf16[1024,128]{1,0:T(8,128)(2,1)S(1)}, bf16[1024,128]{1,0:T(8,128)(2,1)S(1)}, u32[]{:S(2)}, u32[]{:S(2)}) collective-permute-start(bf16[1024,128]{1,0:T(8,128)(2,1)S(1)} %get-tuple-element.28), channel_id=1, source_target_pairs={{1,9},{13,5},{3,11},{15,7},{17,25},{29,21},{19,27},{31,23}} | collective-permute-start | bytes 786440 | tf_op jit(solution)/shard_map/ppermute | solution.py:368
  2.5 6.8 %collective-permute-start = (bf16[16,128]{1,0:T(8,128)(2,1)S(1)}, bf16[16,128]{1,0:T(8,128)(2,1)S(1)}, u32[]{:S(2)}, u32[]{:S(2)}) collective-permute-start(bf16[16,128]{1,0:T(8,128)(2,1)S(1)} %get-tuple-element.25), channel_id=1, source_target_pairs={{1,0},{5,4},{9,8},{13,12},{3,2},{7,6},{11,10},{15,14},{17,16},{21,... | collective-permute-start | bytes 12296 | tf_op jit(solution)/shard_map/ppermute | solution.py:373
  3.8 9.7 %collective-permute-start.2 = (bf16[1024,128]{1,0:T(8,128)(2,1)S(1)}, bf16[1024,128]{1,0:T(8,128)(2,1)S(1)}, u32[]{:S(2)}, u32[]{:S(2)}) collective-permute-start(bf16[1024,128]{1,0:T(8,128)(2,1)S(1)} %get-tuple-element.29), channel_id=1, source_target_pairs={{1,5},{13,9},{3,7},{15,11},{17,21},{29,25},{19,23},{31,27}} | collective-permute-start | bytes 786440 | tf_op jit(solution)/shard_map/ppermute | solution.py:368
  4.5 9.0 %collective-permute-start.3 = (bf16[1024,128]{1,0:T(8,128)(2,1)S(1)}, bf16[1024,128]{1,0:T(8,128)(2,1)S(1)}, u32[]{:S(2)}, u32[]{:S(2)}) collective-permute-start(bf16[1024,128]{1,0:T(8,128)(2,1)S(1)} %get-tuple-element.30), channel_id=1, source_target_pairs={{5,9},{9,5},{7,11},{11,7},{21,25},{25,21},{23,27},{27,23}} | collective-permute-start | bytes 786440 | tf_op jit(solution)/shard_map/ppermute | solution.py:368
  9.3 6.8 %collective-permute-start.4 = (bf16[1024,128]{1,0:T(8,128)(2,1)S(1)}, bf16[1024,128]{1,0:T(8,128)(2,1)S(1)}, u32[]{:S(2)}, u32[]{:S(2)}) collective-permute-start(bf16[1024,128]{1,0:T(8,128)(2,1)S(1)} %get-tuple-element.31), channel_id=1, source_target_pairs={{0,4},{12,8},{2,6},{14,10},{16,20},{28,24},{18,22},{30,26}} | collective-permute-start | bytes 786440 | tf_op jit(solution)/shard_map/ppermute | solution.py:368
  10.6 8.4 %collective-permute-start.5 = (bf16[1024,128]{1,0:T(8,128)(2,1)S(1)}, bf16[1024,128]{1,0:T(8,128)(2,1)S(1)}, u32[]{:S(2)}, u32[]{:S(2)}) collective-permute-start(bf16[1024,128]{1,0:T(8,128)(2,1)S(1)} %get-tuple-element.32), channel_id=1, source_target_pairs={{0,8},{12,4},{2,10},{14,6},{16,24},{28,20},{18,26},{30,22}} | collective-permute-start | bytes 786440 | tf_op jit(solution)/shard_map/ppermute | solution.py:368
  12.8 6.2 %collective-permute-start.6 = (bf16[1024,128]{1,0:T(8,128)(2,1)S(1)}, bf16[1024,128]{1,0:T(8,128)(2,1)S(1)}, u32[]{:S(2)}, u32[]{:S(2)}) collective-permute-start(bf16[1024,128]{1,0:T(8,128)(2,1)S(1)} %get-tuple-element.33), channel_id=1, source_target_pairs={{4,8},{8,4},{6,10},{10,6},{20,24},{24,20},{22,26},{26,22}} | collective-permute-start | bytes 786440 | tf_op jit(solution)/shard_map/ppermute | solution.py:368
  19.0 14.5 %collective-permute-start.7 = (bf16[1024,128]{1,0:T(8,128)(2,1)S(1)}, bf16[1024,128]{1,0:T(8,128)(2,1)S(1)}, u32[]{:S(2)}, u32[]{:S(2)}) collective-permute-start(bf16[1024,128]{1,0:T(8,128)(2,1)S(1)} %get-tuple-element.35), channel_id=1, source_target_pairs={{4,0},{8,12},{5,1},{9,13},{6,2},{10,14},{7,3},{11,15},{20,16},{24,... | collective-permute-start | bytes 786440 | tf_op jit(solution)/shard_map/ppermute | solution.py:365
  20.3 13.2 %collective-permute-start.8 = (bf16[1024,128]{1,0:T(8,128)(2,1)S(1)}, bf16[1024,128]{1,0:T(8,128)(2,1)S(1)}, u32[]{:S(2)}, u32[]{:S(2)}) collective-permute-start(bf16[1024,128]{1,0:T(8,128)(2,1)S(1)} %get-tuple-element.36), channel_id=1, source_target_pairs={{4,12},{8,0},{5,13},{9,1},{6,14},{10,2},{7,15},{11,3},{20,28},{24,... | collective-permute-start | bytes 786440 | tf_op jit(solution)/shard_map/ppermute | solution.py:365
  21.6 11.9 %collective-permute-start.9 = (bf16[1024,128]{1,0:T(8,128)(2,1)S(1)}, bf16[1024,128]{1,0:T(8,128)(2,1)S(1)}, u32[]{:S(2)}, u32[]{:S(2)}) collective-permute-start(bf16[1024,128]{1,0:T(8,128)(2,1)S(1)} %get-tuple-element.37), channel_id=1, source_target_pairs={{4,8},{8,4},{5,9},{9,5},{6,10},{10,6},{7,11},{11,7},{20,24},{24,20... | collective-permute-start | bytes 786440 | tf_op jit(solution)/shard_map/ppermute | solution.py:365

commit v8 on v7

--- a/solution.py
+++ b/solution.py
@@ -248,13 +248,13 @@
             qh = q[hi, :]
             top = None
             for rj in olds:
-                sj = dot(k[rj, :], qb, NT) * (FACTOR * LOG2E)
+                sj = dot(k[rj, :], qb, NT)
                 if rj is lo:
                     sj = jnp.concatenate([jnp.where(seen, sj[:, :HALF], -1e30), sj[:, HALF:]], axis=1)
                 s[rj, ri] = sj
                 tj = jnp.max(sj, axis=0, keepdims=True)
                 top = tj if top is None else jnp.maximum(top, tj)
-            sh = jnp.where(seen, dot(k[hi, :], qh, NT) * (FACTOR * LOG2E), -1e30)
+            sh = jnp.where(seen, dot(k[hi, :], qh, NT), -1e30)
             s[hi, hi] = sh
             top = tail(top, lambda x: jnp.maximum(x, jnp.max(sh, axis=0, keepdims=True)))
             stages.append((lo, hi, ri, olds, qb, qh, top))
@@ -262,13 +262,13 @@
         for lo, hi, ri, olds, qb, qh, top in stages:
             weight, acc = None, None
             for rj in olds:
-                pj = jnp.exp2(s[rj, ri] - top)
+                pj = jnp.exp2((s[rj, ri] - top) * (FACTOR * LOG2E))
                 s[rj, ri] = pj
                 lj = jnp.sum(pj, axis=0, keepdims=True)
                 oj = dot(vt[:, rj], pj.astype(BF), NN)
                 weight = lj if weight is None else weight + lj
                 acc = oj if acc is None else acc + oj
-            ph = jnp.exp2(s[hi, hi] - top[:, HALF:])
+            ph = jnp.exp2((s[hi, hi] - top[:, HALF:]) * (FACTOR * LOG2E))
             s[hi, hi] = ph
             weight = tail(weight, lambda x: x + jnp.sum(ph, axis=0, keepdims=True))
             acc = tail(acc, lambda x: x + dot(vt[:, hi], ph.astype(BF), NN))

time: 34.6 us -> 34.6 us (level)
  no operation moved by 1% of the time
where the time goes in v8:
time: 34.6 us; the launch traced here: 34.3 us
  waiting for transfers between devices  20.7 us (60%)
  starting transfers between devices  10.8 us (31%)
  Pallas kernels  2.03 us (6%)
  between operations  0.75 us (2%)
    ppermute x3, waiting for transfers between devices, owned_per_device(): go = lambda x, pairs: lax.ppermute(x, 'seq', pairs)  11.2 us
    ppermute x6, starting transfers between devices, go_core(): lax.ppermute(x, ('seq', 'mp'), [(2 * a + core, 2 * b + core) for a, b in...  6.24 us
    ppermute x6, waiting for transfers between devices, go_core(): lax.ppermute(x, ('seq', 'mp'), [(2 * a + core, 2 * b + core) for a, b in...  5.45 us
    ppermute x1, waiting for transfers between devices, owned_per_device(): lax.ppermute(turn, ('seq', 'mp'), [(2 * a + 1, 2 * a + 0) for a in range(...  4.1 us
    ppermute x3, starting transfers between devices, owned_per_device(): go = lambda x, pairs: lax.ppermute(x, 'seq', pairs)  3.25 us
    ppermute x1, starting transfers between devices, owned_per_device(): lax.ppermute(turn, ('seq', 'mp'), [(2 * a + 1, 2 * a + 0) for a in range(...  1.29 us
    pallas_call x1, Pallas kernels, owned_per_device(): pl.pallas_call(pack_kernel, out_shape=in_vmem(*(stack,) * 7, ((16, HEAD_D...  1.18 us
    pallas_call x1, Pallas kernels, owned_per_device(): pl.pallas_call(unpack_kernel, out_shape=(jax.ShapeDtypeStruct(queries.sha...  0.85 us
  transfers between devices with their start and end apart: 10, of which 4 were waited for; matrix products, arithmetic and copies ran while one was open for 0% of the time, Pallas kernels for 0%

profile of v8, /device:TPU:0, one launch (start us, length us, event | category | flops | bytes accessed | tf_op | source)
XLA Modules:
  0.0 34.3 jit_solution(12453854445152613202)
XLA Ops:
  0.6 1.2 %pack.1 = (bf16[1024,128]{1,0:T(8,128)(2,1)S(1)}, bf16[1024,128]{1,0:T(8,128)(2,1)S(1)}, bf16[1024,128]{1,0:T(8,128)(2,1)S(1)}, bf16[1024,128]{1,0:T(8,128)(2,1)...) custom-call(s32[8]{0:T(128)} %order.1, ...), custom_call_target="tpu_custom_call" | custom-call | tf_op jit(solution)/shard_map/pack/pallas_call | solution.py:357
  1.8 0.7 %collective-permute-start.1 = (bf16[1024,128]{1,0:T(8,128)(2,1)S(1)}, bf16[1024,128]{1,0:T(8,128)(2,1)S(1)}, u32[]{:S(2)}, u32[]{:S(2)}) collective-permute-start(bf16[1024,128]{1,0:T(8,128)(2,1)S(1)} %get-tuple-element.28), channel_id=1, source_target_pairs={{1,9},{13,5},{3,11},{15,7},{17,25},{29,21},{19,27},{31,23}} | collective-permute-start | bytes 786440 | tf_op jit(solution)/shard_map/ppermute | solution.py:368
  2.5 1.3 %collective-permute-start = (bf16[16,128]{1,0:T(8,128)(2,1)S(1)}, bf16[16,128]{1,0:T(8,128)(2,1)S(1)}, u32[]{:S(2)}, u32[]{:S(2)}) collective-permute-start(bf16[16,128]{1,0:T(8,128)(2,1)S(1)} %get-tuple-element.25), channel_id=1, source_target_pairs={{1,0},{5,4},{9,8},{13,12},{3,2},{7,6},{11,10},{15,14},{17,16},{21,... | collective-permute-start | bytes 12296 | tf_op jit(solution)/shard_map/ppermute | solution.py:373
  3.8 0.7 %collective-permute-start.2 = (bf16[1024,128]{1,0:T(8,128)(2,1)S(1)}, bf16[1024,128]{1,0:T(8,128)(2,1)S(1)}, u32[]{:S(2)}, u32[]{:S(2)}) collective-permute-start(bf16[1024,128]{1,0:T(8,128)(2,1)S(1)} %get-tuple-element.29), channel_id=1, source_target_pairs={{1,5},{13,9},{3,7},{15,11},{17,21},{29,25},{19,23},{31,27}} | collective-permute-start | bytes 786440 | tf_op jit(solution)/shard_map/ppermute | solution.py:368
  4.5 0.7 %collective-permute-start.3 = (bf16[1024,128]{1,0:T(8,128)(2,1)S(1)}, bf16[1024,128]{1,0:T(8,128)(2,1)S(1)}, u32[]{:S(2)}, u32[]{:S(2)}) collective-permute-start(bf16[1024,128]{1,0:T(8,128)(2,1)S(1)} %get-tuple-element.30), channel_id=1, source_target_pairs={{5,9},{9,5},{7,11},{11,7},{21,25},{25,21},{23,27},{27,23}} | collective-permute-start | bytes 786440 | tf_op jit(solution)/shard_map/ppermute | solution.py:368
  5.2 4.1 %collective-permute-done.turn = bf16[16,128]{1,0:T(8,128)(2,1)S(1)} collective-permute-done((bf16[16,128]{1,0:T(8,128)(2,1)S(1)}, bf16[16,128]{1,0:T(8,128)(2,1)S(1)}, u32[]{:S(2)}, u32[]{:S(2)}) %collective-permute-start) | collective-permute-done | bytes 4128 | tf_op jit(solution)/shard_map/ppermute | solution.py:373
  9.3 1.3 %collective-permute-start.4 = (bf16[1024,128]{1,0:T(8,128)(2,1)S(1)}, bf16[1024,128]{1,0:T(8,128)(2,1)S(1)}, u32[]{:S(2)}, u32[]{:S(2)}) collective-permute-start(bf16[1024,128]{1,0:T(8,128)(2,1)S(1)} %get-tuple-element.31), channel_id=1, source_target_pairs={{0,4},{12,8},{2,6},{14,10},{16,20},{28,24},{18,22},{30,26}} | collective-permute-start | bytes 786440 | tf_op jit(solution)/shard_map/ppermute | solution.py:368
  10.6 2.2 %collective-permute-start.5 = (bf16[1024,128]{1,0:T(8,128)(2,1)S(1)}, bf16[1024,128]{1,0:T(8,128)(2,1)S(1)}, u32[]{:S(2)}, u32[]{:S(2)}) collective-permute-start(bf16[1024,128]{1,0:T(8,128)(2,1)S(1)} %get-tuple-element.32), channel_id=1, source_target_pairs={{0,8},{12,4},{2,10},{14,6},{16,24},{28,20},{18,26},{30,22}} | collective-permute-start | bytes 786440 | tf_op jit(solution)/shard_map/ppermute | solution.py:368
  12.8 0.0 collective-permute-done.1.s_c1
  12.8 0.7 %collective-permute-start.6 = (bf16[1024,128]{1,0:T(8,128)(2,1)S(1)}, bf16[1024,128]{1,0:T(8,128)(2,1)S(1)}, u32[]{:S(2)}, u32[]{:S(2)}) collective-permute-start(bf16[1024,128]{1,0:T(8,128)(2,1)S(1)} %get-tuple-element.33), channel_id=1, source_target_pairs={{4,8},{8,4},{6,10},{10,6},{20,24},{24,20},{22,26},{26,22}} | collective-permute-start | bytes 786440 | tf_op jit(solution)/shard_map/ppermute | solution.py:368
  13.5 0.0 collective-permute-done.2.s_a1
  13.5 0.0 collective-permute-done.3.s_b1
  13.5 2.6 %collective-permute-done.4.s_a0 = bf16[1024,128]{1,0:T(8,128)(2,1)S(1)} collective-permute-done((bf16[1024,128]{1,0:T(8,128)(2,1)S(1)}, bf16[1024,128]{1,0:T(8,128)(2,1)S(1)}, u32[]{:S(2)}, u32[]{:S(2)}) %collective-permute-start.4) | collective-permute-done | bytes 262176 | tf_op jit(solution)/shard_map/ppermute | solution.py:368
  16.1 2.9 %collective-permute-done.5.s_c0 = bf16[1024,128]{1,0:T(8,128)(2,1)S(1)} collective-permute-done((bf16[1024,128]{1,0:T(8,128)(2,1)S(1)}, bf16[1024,128]{1,0:T(8,128)(2,1)S(1)}, u32[]{:S(2)}, u32[]{:S(2)}) %collective-permute-start.5) | collective-permute-done | bytes 262176 | tf_op jit(solution)/shard_map/ppermute | solution.py:368
  19.0 0.0 collective-permute-done.6.s_b0
  19.0 1.3 %collective-permute-start.7 = (bf16[1024,128]{1,0:T(8,128)(2,1)S(1)}, bf16[1024,128]{1,0:T(8,128)(2,1)S(1)}, u32[]{:S(2)}, u32[]{:S(2)}) collective-permute-start(bf16[1024,128]{1,0:T(8,128)(2,1)S(1)} %get-tuple-element.35), channel_id=1, source_target_pairs={{4,0},{8,12},{5,1},{9,13},{6,2},{10,14},{7,3},{11,15},{20,16},{24,... | collective-permute-start | bytes 786440 | tf_op jit(solution)/shard_map/ppermute | solution.py:365
  20.3 1.3 %collective-permute-start.8 = (bf16[1024,128]{1,0:T(8,128)(2,1)S(1)}, bf16[1024,128]{1,0:T(8,128)(2,1)S(1)}, u32[]{:S(2)}, u32[]{:S(2)}) collective-permute-start(bf16[1024,128]{1,0:T(8,128)(2,1)S(1)} %get-tuple-element.36), channel_id=1, source_target_pairs={{4,12},{8,0},{5,13},{9,1},{6,14},{10,2},{7,15},{11,3},{20,28},{24,... | collective-permute-start | bytes 786440 | tf_op jit(solution)/shard_map/ppermute | solution.py:365
  21.6 0.7 %collective-permute-start.9 = (bf16[1024,128]{1,0:T(8,128)(2,1)S(1)}, bf16[1024,128]{1,0:T(8,128)(2,1)S(1)}, u32[]{:S(2)}, u32[]{:S(2)}) collective-permute-start(bf16[1024,128]{1,0:T(8,128)(2,1)S(1)} %get-tuple-element.37), channel_id=1, source_target_pairs={{4,8},{8,4},{5,9},{9,5},{6,10},{10,6},{7,11},{11,7},{20,24},{24,20... | collective-permute-start | bytes 786440 | tf_op jit(solution)/shard_map/ppermute | solution.py:365
  22.3 11.1 %collective-permute-done.7.r_a = bf16[1024,128]{1,0:T(8,128)(2,1)S(1)} collective-permute-done((bf16[1024,128]{1,0:T(8,128)(2,1)S(1)}, bf16[1024,128]{1,0:T(8,128)(2,1)S(1)}, u32[]{:S(2)}, u32[]{:S(2)}) %collective-permute-start.7) | collective-permute-done | bytes 262176 | tf_op jit(solution)/shard_map/ppermute | solution.py:365
  33.4 0.0 collective-permute-done.8.r_c
  33.4 0.0 collective-permute-done.9.r_b
  33.4 0.8 %unpack.1 = (bf16[256,256]{1,0:T(8,128)(2,1)}, bf16[256,256]{1,0:T(8,128)(2,1)}, bf16[256,256]{1,0:T(8,128)(2,1)}, bf16[256,256]{1,0:T(8,128)(2,1)}) custom-call(bf16[1024,128]{1,0:T(8,128)(2,1)S(1)} %get-tuple-element.34.own, bf16[1024,128]{1,0:T(8,128)(2,1)S(1)} %collective-permute-done.7.r_a, bf16[1024,128]{1,0:T(8,128)(2,1)S(1)} %collective-permute-done.8.r_c, ...), custom_call_target="tpu_custom_call" | custom-call | tf_op jit(solution)/shard_map/unpack/pallas_call | solution.py:392
  (1 shorter events, 0.0 us)
Async XLA Ops:
  1.8 11.0 %collective-permute-start.1 = (bf16[1024,128]{1,0:T(8,128)(2,1)S(1)}, bf16[1024,128]{1,0:T(8,128)(2,1)S(1)}, u32[]{:S(2)}, u32[]{:S(2)}) collective-permute-start(bf16[1024,128]{1,0:T(8,128)(2,1)S(1)} %get-tuple-element.28), channel_id=1, source_target_pairs={{1,9},{13,5},{3,11},{15,7},{17,25},{29,21},{19,27},{31,23}} | collective-permute-start | bytes 786440 | tf_op jit(solution)/shard_map/ppermute | solution.py:368
  2.5 6.8 %collective-permute-start = (bf16[16,128]{1,0:T(8,128)(2,1)S(1)}, bf16[16,128]{1,0:T(8,128)(2,1)S(1)}, u32[]{:S(2)}, u32[]{:S(2)}) collective-permute-start(bf16[16,128]{1,0:T(8,128)(2,1)S(1)} %get-tuple-element.25), channel_id=1, source_target_pairs={{1,0},{5,4},{9,8},{13,12},{3,2},{7,6},{11,10},{15,14},{17,16},{21,... | collective-permute-start | bytes 12296 | tf_op jit(solution)/shard_map/ppermute | solution.py:373
  3.8 9.7 %collective-permute-start.2 = (bf16[1024,128]{1,0:T(8,128)(2,1)S(1)}, bf16[1024,128]{1,0:T(8,128)(2,1)S(1)}, u32[]{:S(2)}, u32[]{:S(2)}) collective-permute-start(bf16[1024,128]{1,0:T(8,128)(2,1)S(1)} %get-tuple-element.29), channel_id=1, source_target_pairs={{1,5},{13,9},{3,7},{15,11},{17,21},{29,25},{19,23},{31,27}} | collective-permute-start | bytes 786440 | tf_op jit(solution)/shard_map/ppermute | solution.py:368
  4.5 9.0 %collective-permute-start.3 = (bf16[1024,128]{1,0:T(8,128)(2,1)S(1)}, bf16[1024,128]{1,0:T(8,128)(2,1)S(1)}, u32[]{:S(2)}, u32[]{:S(2)}) collective-permute-start(bf16[1024,128]{1,0:T(8,128)(2,1)S(1)} %get-tuple-element.30), channel_id=1, source_target_pairs={{5,9},{9,5},{7,11},{11,7},{21,25},{25,21},{23,27},{27,23}} | collective-permute-start | bytes 786440 | tf_op jit(solution)/shard_map/ppermute | solution.py:368
  9.3 6.8 %collective-permute-start.4 = (bf16[1024,128]{1,0:T(8,128)(2,1)S(1)}, bf16[1024,128]{1,0:T(8,128)(2,1)S(1)}, u32[]{:S(2)}, u32[]{:S(2)}) collective-permute-start(bf16[1024,128]{1,0:T(8,128)(2,1)S(1)} %get-tuple-element.31), channel_id=1, source_target_pairs={{0,4},{12,8},{2,6},{14,10},{16,20},{28,24},{18,22},{30,26}} | collective-permute-start | bytes 786440 | tf_op jit(solution)/shard_map/ppermute | solution.py:368
  10.6 8.4 %collective-permute-start.5 = (bf16[1024,128]{1,0:T(8,128)(2,1)S(1)}, bf16[1024,128]{1,0:T(8,128)(2,1)S(1)}, u32[]{:S(2)}, u32[]{:S(2)}) collective-permute-start(bf16[1024,128]{1,0:T(8,128)(2,1)S(1)} %get-tuple-element.32), channel_id=1, source_target_pairs={{0,8},{12,4},{2,10},{14,6},{16,24},{28,20},{18,26},{30,22}} | collective-permute-start | bytes 786440 | tf_op jit(solution)/shard_map/ppermute | solution.py:368
  12.8 6.2 %collective-permute-start.6 = (bf16[1024,128]{1,0:T(8,128)(2,1)S(1)}, bf16[1024,128]{1,0:T(8,128)(2,1)S(1)}, u32[]{:S(2)}, u32[]{:S(2)}) collective-permute-start(bf16[1024,128]{1,0:T(8,128)(2,1)S(1)} %get-tuple-element.33), channel_id=1, source_target_pairs={{4,8},{8,4},{6,10},{10,6},{20,24},{24,20},{22,26},{26,22}} | collective-permute-start | bytes 786440 | tf_op jit(solution)/shard_map/ppermute | solution.py:368
  19.0 14.4 %collective-permute-start.7 = (bf16[1024,128]{1,0:T(8,128)(2,1)S(1)}, bf16[1024,128]{1,0:T(8,128)(2,1)S(1)}, u32[]{:S(2)}, u32[]{:S(2)}) collective-permute-start(bf16[1024,128]{1,0:T(8,128)(2,1)S(1)} %get-tuple-element.35), channel_id=1, source_target_pairs={{4,0},{8,12},{5,1},{9,13},{6,2},{10,14},{7,3},{11,15},{20,16},{24,... | collective-permute-start | bytes 786440 | tf_op jit(solution)/shard_map/ppermute | solution.py:365
  20.3 13.1 %collective-permute-start.8 = (bf16[1024,128]{1,0:T(8,128)(2,1)S(1)}, bf16[1024,128]{1,0:T(8,128)(2,1)S(1)}, u32[]{:S(2)}, u32[]{:S(2)}) collective-permute-start(bf16[1024,128]{1,0:T(8,128)(2,1)S(1)} %get-tuple-element.36), channel_id=1, source_target_pairs={{4,12},{8,0},{5,13},{9,1},{6,14},{10,2},{7,15},{11,3},{20,28},{24,... | collective-permute-start | bytes 786440 | tf_op jit(solution)/shard_map/ppermute | solution.py:365
  21.6 11.8 %collective-permute-start.9 = (bf16[1024,128]{1,0:T(8,128)(2,1)S(1)}, bf16[1024,128]{1,0:T(8,128)(2,1)S(1)}, u32[]{:S(2)}, u32[]{:S(2)}) collective-permute-start(bf16[1024,128]{1,0:T(8,128)(2,1)S(1)} %get-tuple-element.37), channel_id=1, source_target_pairs={{4,8},{8,4},{5,9},{9,5},{6,10},{10,6},{7,11},{11,7},{20,24},{24,20... | collective-permute-start | bytes 786440 | tf_op jit(solution)/shard_map/ppermute | solution.py:365

commit v9 on v8

--- a/solution.py
+++ b/solution.py
@@ -242,8 +242,6 @@
             hi = slice(i * BLOCK + HALF, (i + 1) * BLOCK)
             ri = slice(i * BLOCK, (i + 1) * BLOCK)
             olds = [slice(j * BLOCK, (j + 1) * BLOCK) for j in range(i)] + [lo]
-            kt[:, ri] = k[ri, :].T
-            vt[:, ri] = v[ri, :].T
             qb = q[ri, :]
             qh = q[hi, :]
             top = None
@@ -260,6 +258,8 @@
             stages.append((lo, hi, ri, olds, qb, qh, top))
         later = []
         for lo, hi, ri, olds, qb, qh, top in stages:
+            kt[:, ri] = k[ri, :].T
+            vt[:, ri] = v[ri, :].T
             weight, acc = None, None
             for rj in olds:
                 pj = jnp.exp2((s[rj, ri] - top) * (FACTOR * LOG2E))

time: 34.6 us -> 34.6 us (level)
  no operation moved by 1% of the time
where the time goes in v9:
time: 34.6 us; the launch traced here: 34.3 us
  waiting for transfers between devices  20.7 us (60%)
  starting transfers between devices  10.8 us (31%)
  Pallas kernels  2.03 us (6%)
  between operations  0.75 us (2%)
    ppermute x3, waiting for transfers between devices, owned_per_device(): go = lambda x, pairs: lax.ppermute(x, 'seq', pairs)  11.2 us
    ppermute x6, starting transfers between devices, go_core(): lax.ppermute(x, ('seq', 'mp'), [(2 * a + core, 2 * b + core) for a, b in...  6.24 us
    ppermute x6, waiting for transfers between devices, go_core(): lax.ppermute(x, ('seq', 'mp'), [(2 * a + core, 2 * b + core) for a, b in...  5.45 us
    ppermute x1, waiting for transfers between devices, owned_per_device(): lax.ppermute(turn, ('seq', 'mp'), [(2 * a + 1, 2 * a + 0) for a in range(...  4.1 us
    ppermute x3, starting transfers between devices, owned_per_device(): go = lambda x, pairs: lax.ppermute(x, 'seq', pairs)  3.25 us
    ppermute x1, starting transfers between devices, owned_per_device(): lax.ppermute(turn, ('seq', 'mp'), [(2 * a + 1, 2 * a + 0) for a in range(...  1.29 us
    pallas_call x1, Pallas kernels, owned_per_device(): pl.pallas_call(pack_kernel, out_shape=in_vmem(*(stack,) * 7, ((16, HEAD_D...  1.18 us
    pallas_call x1, Pallas kernels, owned_per_device(): pl.pallas_call(unpack_kernel, out_shape=(jax.ShapeDtypeStruct(queries.sha...  0.85 us
  transfers between devices with their start and end apart: 10, of which 4 were waited for; matrix products, arithmetic and copies ran while one was open for 0% of the time, Pallas kernels for 0%

profile of v9, /device:TPU:0, one launch (start us, length us, event | category | flops | bytes accessed | tf_op | source)
XLA Modules:
  0.0 34.3 jit_solution(10197433051593565520)
XLA Ops:
  0.6 1.2 %pack.1 = (bf16[1024,128]{1,0:T(8,128)(2,1)S(1)}, bf16[1024,128]{1,0:T(8,128)(2,1)S(1)}, bf16[1024,128]{1,0:T(8,128)(2,1)S(1)}, bf16[1024,128]{1,0:T(8,128)(2,1)...) custom-call(s32[8]{0:T(128)} %order.1, ...), custom_call_target="tpu_custom_call" | custom-call | tf_op jit(solution)/shard_map/pack/pallas_call | solution.py:357
  1.8 0.7 %collective-permute-start.1 = (bf16[1024,128]{1,0:T(8,128)(2,1)S(1)}, bf16[1024,128]{1,0:T(8,128)(2,1)S(1)}, u32[]{:S(2)}, u32[]{:S(2)}) collective-permute-start(bf16[1024,128]{1,0:T(8,128)(2,1)S(1)} %get-tuple-element.28), channel_id=1, source_target_pairs={{1,9},{13,5},{3,11},{15,7},{17,25},{29,21},{19,27},{31,23}} | collective-permute-start | bytes 786440 | tf_op jit(solution)/shard_map/ppermute | solution.py:368
  2.5 1.3 %collective-permute-start = (bf16[16,128]{1,0:T(8,128)(2,1)S(1)}, bf16[16,128]{1,0:T(8,128)(2,1)S(1)}, u32[]{:S(2)}, u32[]{:S(2)}) collective-permute-start(bf16[16,128]{1,0:T(8,128)(2,1)S(1)} %get-tuple-element.25), channel_id=1, source_target_pairs={{1,0},{5,4},{9,8},{13,12},{3,2},{7,6},{11,10},{15,14},{17,16},{21,... | collective-permute-start | bytes 12296 | tf_op jit(solution)/shard_map/ppermute | solution.py:373
  3.8 0.7 %collective-permute-start.2 = (bf16[1024,128]{1,0:T(8,128)(2,1)S(1)}, bf16[1024,128]{1,0:T(8,128)(2,1)S(1)}, u32[]{:S(2)}, u32[]{:S(2)}) collective-permute-start(bf16[1024,128]{1,0:T(8,128)(2,1)S(1)} %get-tuple-element.29), channel_id=1, source_target_pairs={{1,5},{13,9},{3,7},{15,11},{17,21},{29,25},{19,23},{31,27}} | collective-permute-start | bytes 786440 | tf_op jit(solution)/shard_map/ppermute | solution.py:368
  4.5 0.7 %collective-permute-start.3 = (bf16[1024,128]{1,0:T(8,128)(2,1)S(1)}, bf16[1024,128]{1,0:T(8,128)(2,1)S(1)}, u32[]{:S(2)}, u32[]{:S(2)}) collective-permute-start(bf16[1024,128]{1,0:T(8,128)(2,1)S(1)} %get-tuple-element.30), channel_id=1, source_target_pairs={{5,9},{9,5},{7,11},{11,7},{21,25},{25,21},{23,27},{27,23}} | collective-permute-start | bytes 786440 | tf_op jit(solution)/shard_map/ppermute | solution.py:368
  5.2 4.1 %collective-permute-done.turn = bf16[16,128]{1,0:T(8,128)(2,1)S(1)} collective-permute-done((bf16[16,128]{1,0:T(8,128)(2,1)S(1)}, bf16[16,128]{1,0:T(8,128)(2,1)S(1)}, u32[]{:S(2)}, u32[]{:S(2)}) %collective-permute-start) | collective-permute-done | bytes 4128 | tf_op jit(solution)/shard_map/ppermute | solution.py:373
  9.3 1.3 %collective-permute-start.4 = (bf16[1024,128]{1,0:T(8,128)(2,1)S(1)}, bf16[1024,128]{1,0:T(8,128)(2,1)S(1)}, u32[]{:S(2)}, u32[]{:S(2)}) collective-permute-start(bf16[1024,128]{1,0:T(8,128)(2,1)S(1)} %get-tuple-element.31), channel_id=1, source_target_pairs={{0,4},{12,8},{2,6},{14,10},{16,20},{28,24},{18,22},{30,26}} | collective-permute-start | bytes 786440 | tf_op jit(solution)/shard_map/ppermute | solution.py:368
  10.6 2.2 %collective-permute-start.5 = (bf16[1024,128]{1,0:T(8,128)(2,1)S(1)}, bf16[1024,128]{1,0:T(8,128)(2,1)S(1)}, u32[]{:S(2)}, u32[]{:S(2)}) collective-permute-start(bf16[1024,128]{1,0:T(8,128)(2,1)S(1)} %get-tuple-element.32), channel_id=1, source_target_pairs={{0,8},{12,4},{2,10},{14,6},{16,24},{28,20},{18,26},{30,22}} | collective-permute-start | bytes 786440 | tf_op jit(solution)/shard_map/ppermute | solution.py:368
  12.8 0.0 collective-permute-done.1.s_c1
  12.8 0.7 %collective-permute-start.6 = (bf16[1024,128]{1,0:T(8,128)(2,1)S(1)}, bf16[1024,128]{1,0:T(8,128)(2,1)S(1)}, u32[]{:S(2)}, u32[]{:S(2)}) collective-permute-start(bf16[1024,128]{1,0:T(8,128)(2,1)S(1)} %get-tuple-element.33), channel_id=1, source_target_pairs={{4,8},{8,4},{6,10},{10,6},{20,24},{24,20},{22,26},{26,22}} | collective-permute-start | bytes 786440 | tf_op jit(solution)/shard_map/ppermute | solution.py:368
  13.5 0.0 collective-permute-done.2.s_a1
  13.5 0.0 collective-permute-done.3.s_b1
  13.5 2.6 %collective-permute-done.4.s_a0 = bf16[1024,128]{1,0:T(8,128)(2,1)S(1)} collective-permute-done((bf16[1024,128]{1,0:T(8,128)(2,1)S(1)}, bf16[1024,128]{1,0:T(8,128)(2,1)S(1)}, u32[]{:S(2)}, u32[]{:S(2)}) %collective-permute-start.4) | collective-permute-done | bytes 262176 | tf_op jit(solution)/shard_map/ppermute | solution.py:368
  16.1 2.9 %collective-permute-done.5.s_c0 = bf16[1024,128]{1,0:T(8,128)(2,1)S(1)} collective-permute-done((bf16[1024,128]{1,0:T(8,128)(2,1)S(1)}, bf16[1024,128]{1,0:T(8,128)(2,1)S(1)}, u32[]{:S(2)}, u32[]{:S(2)}) %collective-permute-start.5) | collective-permute-done | bytes 262176 | tf_op jit(solution)/shard_map/ppermute | solution.py:368
  19.0 0.0 collective-permute-done.6.s_b0
  19.0 1.3 %collective-permute-start.7 = (bf16[1024,128]{1,0:T(8,128)(2,1)S(1)}, bf16[1024,128]{1,0:T(8,128)(2,1)S(1)}, u32[]{:S(2)}, u32[]{:S(2)}) collective-permute-start(bf16[1024,128]{1,0:T(8,128)(2,1)S(1)} %get-tuple-element.35), channel_id=1, source_target_pairs={{4,0},{8,12},{5,1},{9,13},{6,2},{10,14},{7,3},{11,15},{20,16},{24,... | collective-permute-start | bytes 786440 | tf_op jit(solution)/shard_map/ppermute | solution.py:365
  20.3 1.3 %collective-permute-start.8 = (bf16[1024,128]{1,0:T(8,128)(2,1)S(1)}, bf16[1024,128]{1,0:T(8,128)(2,1)S(1)}, u32[]{:S(2)}, u32[]{:S(2)}) collective-permute-start(bf16[1024,128]{1,0:T(8,128)(2,1)S(1)} %get-tuple-element.36), channel_id=1, source_target_pairs={{4,12},{8,0},{5,13},{9,1},{6,14},{10,2},{7,15},{11,3},{20,28},{24,... | collective-permute-start | bytes 786440 | tf_op jit(solution)/shard_map/ppermute | solution.py:365
  21.6 0.7 %collective-permute-start.9 = (bf16[1024,128]{1,0:T(8,128)(2,1)S(1)}, bf16[1024,128]{1,0:T(8,128)(2,1)S(1)}, u32[]{:S(2)}, u32[]{:S(2)}) collective-permute-start(bf16[1024,128]{1,0:T(8,128)(2,1)S(1)} %get-tuple-element.37), channel_id=1, source_target_pairs={{4,8},{8,4},{5,9},{9,5},{6,10},{10,6},{7,11},{11,7},{20,24},{24,20... | collective-permute-start | bytes 786440 | tf_op jit(solution)/shard_map/ppermute | solution.py:365
  22.3 11.2 %collective-permute-done.7.r_a = bf16[1024,128]{1,0:T(8,128)(2,1)S(1)} collective-permute-done((bf16[1024,128]{1,0:T(8,128)(2,1)S(1)}, bf16[1024,128]{1,0:T(8,128)(2,1)S(1)}, u32[]{:S(2)}, u32[]{:S(2)}) %collective-permute-start.7) | collective-permute-done | bytes 262176 | tf_op jit(solution)/shard_map/ppermute | solution.py:365
  33.4 0.0 collective-permute-done.8.r_c
  33.4 0.0 collective-permute-done.9.r_b
  33.4 0.8 %unpack.1 = (bf16[256,256]{1,0:T(8,128)(2,1)}, bf16[256,256]{1,0:T(8,128)(2,1)}, bf16[256,256]{1,0:T(8,128)(2,1)}, bf16[256,256]{1,0:T(8,128)(2,1)}) custom-call(bf16[1024,128]{1,0:T(8,128)(2,1)S(1)} %get-tuple-element.34.own, bf16[1024,128]{1,0:T(8,128)(2,1)S(1)} %collective-permute-done.7.r_a, bf16[1024,128]{1,0:T(8,128)(2,1)S(1)} %collective-permute-done.8.r_c, ...), custom_call_target="tpu_custom_call" | custom-call | tf_op jit(solution)/shard_map/unpack/pallas_call | solution.py:392
  (1 shorter events, 0.0 us)
Async XLA Ops:
  1.8 11.0 %collective-permute-start.1 = (bf16[1024,128]{1,0:T(8,128)(2,1)S(1)}, bf16[1024,128]{1,0:T(8,128)(2,1)S(1)}, u32[]{:S(2)}, u32[]{:S(2)}) collective-permute-start(bf16[1024,128]{1,0:T(8,128)(2,1)S(1)} %get-tuple-element.28), channel_id=1, source_target_pairs={{1,9},{13,5},{3,11},{15,7},{17,25},{29,21},{19,27},{31,23}} | collective-permute-start | bytes 786440 | tf_op jit(solution)/shard_map/ppermute | solution.py:368
  2.5 6.8 %collective-permute-start = (bf16[16,128]{1,0:T(8,128)(2,1)S(1)}, bf16[16,128]{1,0:T(8,128)(2,1)S(1)}, u32[]{:S(2)}, u32[]{:S(2)}) collective-permute-start(bf16[16,128]{1,0:T(8,128)(2,1)S(1)} %get-tuple-element.25), channel_id=1, source_target_pairs={{1,0},{5,4},{9,8},{13,12},{3,2},{7,6},{11,10},{15,14},{17,16},{21,... | collective-permute-start | bytes 12296 | tf_op jit(solution)/shard_map/ppermute | solution.py:373
  3.8 9.7 %collective-permute-start.2 = (bf16[1024,128]{1,0:T(8,128)(2,1)S(1)}, bf16[1024,128]{1,0:T(8,128)(2,1)S(1)}, u32[]{:S(2)}, u32[]{:S(2)}) collective-permute-start(bf16[1024,128]{1,0:T(8,128)(2,1)S(1)} %get-tuple-element.29), channel_id=1, source_target_pairs={{1,5},{13,9},{3,7},{15,11},{17,21},{29,25},{19,23},{31,27}} | collective-permute-start | bytes 786440 | tf_op jit(solution)/shard_map/ppermute | solution.py:368
  4.5 9.0 %collective-permute-start.3 = (bf16[1024,128]{1,0:T(8,128)(2,1)S(1)}, bf16[1024,128]{1,0:T(8,128)(2,1)S(1)}, u32[]{:S(2)}, u32[]{:S(2)}) collective-permute-start(bf16[1024,128]{1,0:T(8,128)(2,1)S(1)} %get-tuple-element.30), channel_id=1, source_target_pairs={{5,9},{9,5},{7,11},{11,7},{21,25},{25,21},{23,27},{27,23}} | collective-permute-start | bytes 786440 | tf_op jit(solution)/shard_map/ppermute | solution.py:368
  9.3 6.8 %collective-permute-start.4 = (bf16[1024,128]{1,0:T(8,128)(2,1)S(1)}, bf16[1024,128]{1,0:T(8,128)(2,1)S(1)}, u32[]{:S(2)}, u32[]{:S(2)}) collective-permute-start(bf16[1024,128]{1,0:T(8,128)(2,1)S(1)} %get-tuple-element.31), channel_id=1, source_target_pairs={{0,4},{12,8},{2,6},{14,10},{16,20},{28,24},{18,22},{30,26}} | collective-permute-start | bytes 786440 | tf_op jit(solution)/shard_map/ppermute | solution.py:368
  10.6 8.4 %collective-permute-start.5 = (bf16[1024,128]{1,0:T(8,128)(2,1)S(1)}, bf16[1024,128]{1,0:T(8,128)(2,1)S(1)}, u32[]{:S(2)}, u32[]{:S(2)}) collective-permute-start(bf16[1024,128]{1,0:T(8,128)(2,1)S(1)} %get-tuple-element.32), channel_id=1, source_target_pairs={{0,8},{12,4},{2,10},{14,6},{16,24},{28,20},{18,26},{30,22}} | collective-permute-start | bytes 786440 | tf_op jit(solution)/shard_map/ppermute | solution.py:368
  12.8 6.2 %collective-permute-start.6 = (bf16[1024,128]{1,0:T(8,128)(2,1)S(1)}, bf16[1024,128]{1,0:T(8,128)(2,1)S(1)}, u32[]{:S(2)}, u32[]{:S(2)}) collective-permute-start(bf16[1024,128]{1,0:T(8,128)(2,1)S(1)} %get-tuple-element.33), channel_id=1, source_target_pairs={{4,8},{8,4},{6,10},{10,6},{20,24},{24,20},{22,26},{26,22}} | collective-permute-start | bytes 786440 | tf_op jit(solution)/shard_map/ppermute | solution.py:368
  19.0 14.4 %collective-permute-start.7 = (bf16[1024,128]{1,0:T(8,128)(2,1)S(1)}, bf16[1024,128]{1,0:T(8,128)(2,1)S(1)}, u32[]{:S(2)}, u32[]{:S(2)}) collective-permute-start(bf16[1024,128]{1,0:T(8,128)(2,1)S(1)} %get-tuple-element.35), channel_id=1, source_target_pairs={{4,0},{8,12},{5,1},{9,13},{6,2},{10,14},{7,3},{11,15},{20,16},{24,... | collective-permute-start | bytes 786440 | tf_op jit(solution)/shard_map/ppermute | solution.py:365
  20.3 13.1 %collective-permute-start.8 = (bf16[1024,128]{1,0:T(8,128)(2,1)S(1)}, bf16[1024,128]{1,0:T(8,128)(2,1)S(1)}, u32[]{:S(2)}, u32[]{:S(2)}) collective-permute-start(bf16[1024,128]{1,0:T(8,128)(2,1)S(1)} %get-tuple-element.36), channel_id=1, source_target_pairs={{4,12},{8,0},{5,13},{9,1},{6,14},{10,2},{7,15},{11,3},{20,28},{24,... | collective-permute-start | bytes 786440 | tf_op jit(solution)/shard_map/ppermute | solution.py:365
  21.6 11.9 %collective-permute-start.9 = (bf16[1024,128]{1,0:T(8,128)(2,1)S(1)}, bf16[1024,128]{1,0:T(8,128)(2,1)S(1)}, u32[]{:S(2)}, u32[]{:S(2)}) collective-permute-start(bf16[1024,128]{1,0:T(8,128)(2,1)S(1)} %get-tuple-element.37), channel_id=1, source_target_pairs={{4,8},{8,4},{5,9},{9,5},{6,10},{10,6},{7,11},{11,7},{20,24},{24,20... | collective-permute-start | bytes 786440 | tf_op jit(solution)/shard_map/ppermute | solution.py:365

commit v10 on v9

--- a/solution.py
+++ b/solution.py
@@ -281,8 +281,8 @@
             for rj in olds:
                 dp = dot(v[rj, :], gb, NN)
                 pj = s[rj, ri]
+                vj = dot(pj.astype(BF), gb, NT)
                 ds = (pj * (dp - delta)).astype(BF)
-                vj = dot(pj.astype(BF), gb, NT)
                 kj = dot(ds, qb, NN)
                 if rj is lo:
                     dv[rj, :] = vj

time: 34.6 us -> 34.6 us (level)
  no operation moved by 1% of the time
where the time goes in v10:
time: 34.6 us; the launch traced here: 34.3 us
  waiting for transfers between devices  20.7 us (60%)
  starting transfers between devices  10.8 us (31%)
  Pallas kernels  2.03 us (6%)
  between operations  0.75 us (2%)
    ppermute x3, waiting for transfers between devices, owned_per_device(): go = lambda x, pairs: lax.ppermute(x, 'seq', pairs)  11.2 us
    ppermute x6, starting transfers between devices, go_core(): lax.ppermute(x, ('seq', 'mp'), [(2 * a + core, 2 * b + core) for a, b in...  6.24 us
    ppermute x6, waiting for transfers between devices, go_core(): lax.ppermute(x, ('seq', 'mp'), [(2 * a + core, 2 * b + core) for a, b in...  5.45 us
    ppermute x1, waiting for transfers between devices, owned_per_device(): lax.ppermute(turn, ('seq', 'mp'), [(2 * a + 1, 2 * a + 0) for a in range(...  4.1 us
    ppermute x3, starting transfers between devices, owned_per_device(): go = lambda x, pairs: lax.ppermute(x, 'seq', pairs)  3.25 us
    ppermute x1, starting transfers between devices, owned_per_device(): lax.ppermute(turn, ('seq', 'mp'), [(2 * a + 1, 2 * a + 0) for a in range(...  1.29 us
    pallas_call x1, Pallas kernels, owned_per_device(): pl.pallas_call(pack_kernel, out_shape=in_vmem(*(stack,) * 7, ((16, HEAD_D...  1.18 us
    pallas_call x1, Pallas kernels, owned_per_device(): pl.pallas_call(unpack_kernel, out_shape=(jax.ShapeDtypeStruct(queries.sha...  0.85 us
  transfers between devices with their start and end apart: 10, of which 4 were waited for; matrix products, arithmetic and copies ran while one was open for 0% of the time, Pallas kernels for 0%

profile of v10, /device:TPU:0, one launch (start us, length us, event | category | flops | bytes accessed | tf_op | source)
XLA Modules:
  0.0 34.3 jit_solution(10197433051593565520)
XLA Ops:
  0.6 1.2 %pack.1 = (bf16[1024,128]{1,0:T(8,128)(2,1)S(1)}, bf16[1024,128]{1,0:T(8,128)(2,1)S(1)}, bf16[1024,128]{1,0:T(8,128)(2,1)S(1)}, bf16[1024,128]{1,0:T(8,128)(2,1)...) custom-call(s32[8]{0:T(128)} %order.1, ...), custom_call_target="tpu_custom_call" | custom-call | tf_op jit(solution)/shard_map/pack/pallas_call | solution.py:357
  1.8 0.7 %collective-permute-start.1 = (bf16[1024,128]{1,0:T(8,128)(2,1)S(1)}, bf16[1024,128]{1,0:T(8,128)(2,1)S(1)}, u32[]{:S(2)}, u32[]{:S(2)}) collective-permute-start(bf16[1024,128]{1,0:T(8,128)(2,1)S(1)} %get-tuple-element.28), channel_id=1, source_target_pairs={{1,9},{13,5},{3,11},{15,7},{17,25},{29,21},{19,27},{31,23}} | collective-permute-start | bytes 786440 | tf_op jit(solution)/shard_map/ppermute | solution.py:368
  2.5 1.3 %collective-permute-start = (bf16[16,128]{1,0:T(8,128)(2,1)S(1)}, bf16[16,128]{1,0:T(8,128)(2,1)S(1)}, u32[]{:S(2)}, u32[]{:S(2)}) collective-permute-start(bf16[16,128]{1,0:T(8,128)(2,1)S(1)} %get-tuple-element.25), channel_id=1, source_target_pairs={{1,0},{5,4},{9,8},{13,12},{3,2},{7,6},{11,10},{15,14},{17,16},{21,... | collective-permute-start | bytes 12296 | tf_op jit(solution)/shard_map/ppermute | solution.py:373
  3.8 0.7 %collective-permute-start.2 = (bf16[1024,128]{1,0:T(8,128)(2,1)S(1)}, bf16[1024,128]{1,0:T(8,128)(2,1)S(1)}, u32[]{:S(2)}, u32[]{:S(2)}) collective-permute-start(bf16[1024,128]{1,0:T(8,128)(2,1)S(1)} %get-tuple-element.29), channel_id=1, source_target_pairs={{1,5},{13,9},{3,7},{15,11},{17,21},{29,25},{19,23},{31,27}} | collective-permute-start | bytes 786440 | tf_op jit(solution)/shard_map/ppermute | solution.py:368
  4.5 0.7 %collective-permute-start.3 = (bf16[1024,128]{1,0:T(8,128)(2,1)S(1)}, bf16[1024,128]{1,0:T(8,128)(2,1)S(1)}, u32[]{:S(2)}, u32[]{:S(2)}) collective-permute-start(bf16[1024,128]{1,0:T(8,128)(2,1)S(1)} %get-tuple-element.30), channel_id=1, source_target_pairs={{5,9},{9,5},{7,11},{11,7},{21,25},{25,21},{23,27},{27,23}} | collective-permute-start | bytes 786440 | tf_op jit(solution)/shard_map/ppermute | solution.py:368
  5.2 4.1 %collective-permute-done.turn = bf16[16,128]{1,0:T(8,128)(2,1)S(1)} collective-permute-done((bf16[16,128]{1,0:T(8,128)(2,1)S(1)}, bf16[16,128]{1,0:T(8,128)(2,1)S(1)}, u32[]{:S(2)}, u32[]{:S(2)}) %collective-permute-start) | collective-permute-done | bytes 4128 | tf_op jit(solution)/shard_map/ppermute | solution.py:373
  9.3 1.3 %collective-permute-start.4 = (bf16[1024,128]{1,0:T(8,128)(2,1)S(1)}, bf16[1024,128]{1,0:T(8,128)(2,1)S(1)}, u32[]{:S(2)}, u32[]{:S(2)}) collective-permute-start(bf16[1024,128]{1,0:T(8,128)(2,1)S(1)} %get-tuple-element.31), channel_id=1, source_target_pairs={{0,4},{12,8},{2,6},{14,10},{16,20},{28,24},{18,22},{30,26}} | collective-permute-start | bytes 786440 | tf_op jit(solution)/shard_map/ppermute | solution.py:368
  10.6 2.2 %collective-permute-start.5 = (bf16[1024,128]{1,0:T(8,128)(2,1)S(1)}, bf16[1024,128]{1,0:T(8,128)(2,1)S(1)}, u32[]{:S(2)}, u32[]{:S(2)}) collective-permute-start(bf16[1024,128]{1,0:T(8,128)(2,1)S(1)} %get-tuple-element.32), channel_id=1, source_target_pairs={{0,8},{12,4},{2,10},{14,6},{16,24},{28,20},{18,26},{30,22}} | collective-permute-start | bytes 786440 | tf_op jit(solution)/shard_map/ppermute | solution.py:368
  12.8 0.0 collective-permute-done.1.s_c1
  12.8 0.7 %collective-permute-start.6 = (bf16[1024,128]{1,0:T(8,128)(2,1)S(1)}, bf16[1024,128]{1,0:T(8,128)(2,1)S(1)}, u32[]{:S(2)}, u32[]{:S(2)}) collective-permute-start(bf16[1024,128]{1,0:T(8,128)(2,1)S(1)} %get-tuple-element.33), channel_id=1, source_target_pairs={{4,8},{8,4},{6,10},{10,6},{20,24},{24,20},{22,26},{26,22}} | collective-permute-start | bytes 786440 | tf_op jit(solution)/shard_map/ppermute | solution.py:368
  13.5 0.0 collective-permute-done.2.s_a1
  13.5 0.0 collective-permute-done.3.s_b1
  13.5 2.6 %collective-permute-done.4.s_a0 = bf16[1024,128]{1,0:T(8,128)(2,1)S(1)} collective-permute-done((bf16[1024,128]{1,0:T(8,128)(2,1)S(1)}, bf16[1024,128]{1,0:T(8,128)(2,1)S(1)}, u32[]{:S(2)}, u32[]{:S(2)}) %collective-permute-start.4) | collective-permute-done | bytes 262176 | tf_op jit(solution)/shard_map/ppermute | solution.py:368
  16.1 2.9 %collective-permute-done.5.s_c0 = bf16[1024,128]{1,0:T(8,128)(2,1)S(1)} collective-permute-done((bf16[1024,128]{1,0:T(8,128)(2,1)S(1)}, bf16[1024,128]{1,0:T(8,128)(2,1)S(1)}, u32[]{:S(2)}, u32[]{:S(2)}) %collective-permute-start.5) | collective-permute-done | bytes 262176 | tf_op jit(solution)/shard_map/ppermute | solution.py:368
  19.0 0.0 collective-permute-done.6.s_b0
  19.0 1.3 %collective-permute-start.7 = (bf16[1024,128]{1,0:T(8,128)(2,1)S(1)}, bf16[1024,128]{1,0:T(8,128)(2,1)S(1)}, u32[]{:S(2)}, u32[]{:S(2)}) collective-permute-start(bf16[1024,128]{1,0:T(8,128)(2,1)S(1)} %get-tuple-element.35), channel_id=1, source_target_pairs={{4,0},{8,12},{5,1},{9,13},{6,2},{10,14},{7,3},{11,15},{20,16},{24,... | collective-permute-start | bytes 786440 | tf_op jit(solution)/shard_map/ppermute | solution.py:365
  20.3 1.3 %collective-permute-start.8 = (bf16[1024,128]{1,0:T(8,128)(2,1)S(1)}, bf16[1024,128]{1,0:T(8,128)(2,1)S(1)}, u32[]{:S(2)}, u32[]{:S(2)}) collective-permute-start(bf16[1024,128]{1,0:T(8,128)(2,1)S(1)} %get-tuple-element.36), channel_id=1, source_target_pairs={{4,12},{8,0},{5,13},{9,1},{6,14},{10,2},{7,15},{11,3},{20,28},{24,... | collective-permute-start | bytes 786440 | tf_op jit(solution)/shard_map/ppermute | solution.py:365
  21.6 0.7 %collective-permute-start.9 = (bf16[1024,128]{1,0:T(8,128)(2,1)S(1)}, bf16[1024,128]{1,0:T(8,128)(2,1)S(1)}, u32[]{:S(2)}, u32[]{:S(2)}) collective-permute-start(bf16[1024,128]{1,0:T(8,128)(2,1)S(1)} %get-tuple-element.37), channel_id=1, source_target_pairs={{4,8},{8,4},{5,9},{9,5},{6,10},{10,6},{7,11},{11,7},{20,24},{24,20... | collective-permute-start | bytes 786440 | tf_op jit(solution)/shard_map/ppermute | solution.py:365
  22.3 11.2 %collective-permute-done.7.r_a = bf16[1024,128]{1,0:T(8,128)(2,1)S(1)} collective-permute-done((bf16[1024,128]{1,0:T(8,128)(2,1)S(1)}, bf16[1024,128]{1,0:T(8,128)(2,1)S(1)}, u32[]{:S(2)}, u32[]{:S(2)}) %collective-permute-start.7) | collective-permute-done | bytes 262176 | tf_op jit(solution)/shard_map/ppermute | solution.py:365
  33.4 0.0 collective-permute-done.8.r_c
  33.4 0.0 collective-permute-done.9.r_b
  33.4 0.8 %unpack.1 = (bf16[256,256]{1,0:T(8,128)(2,1)}, bf16[256,256]{1,0:T(8,128)(2,1)}, bf16[256,256]{1,0:T(8,128)(2,1)}, bf16[256,256]{1,0:T(8,128)(2,1)}) custom-call(bf16[1024,128]{1,0:T(8,128)(2,1)S(1)} %get-tuple-element.34.own, bf16[1024,128]{1,0:T(8,128)(2,1)S(1)} %collective-permute-done.7.r_a, bf16[1024,128]{1,0:T(8,128)(2,1)S(1)} %collective-permute-done.8.r_c, ...), custom_call_target="tpu_custom_call" | custom-call | tf_op jit(solution)/shard_map/unpack/pallas_call | solution.py:392
  (1 shorter events, 0.0 us)
Async XLA Ops:
  1.8 11.0 %collective-permute-start.1 = (bf16[1024,128]{1,0:T(8,128)(2,1)S(1)}, bf16[1024,128]{1,0:T(8,128)(2,1)S(1)}, u32[]{:S(2)}, u32[]{:S(2)}) collective-permute-start(bf16[1024,128]{1,0:T(8,128)(2,1)S(1)} %get-tuple-element.28), channel_id=1, source_target_pairs={{1,9},{13,5},{3,11},{15,7},{17,25},{29,21},{19,27},{31,23}} | collective-permute-start | bytes 786440 | tf_op jit(solution)/shard_map/ppermute | solution.py:368
  2.5 6.8 %collective-permute-start = (bf16[16,128]{1,0:T(8,128)(2,1)S(1)}, bf16[16,128]{1,0:T(8,128)(2,1)S(1)}, u32[]{:S(2)}, u32[]{:S(2)}) collective-permute-start(bf16[16,128]{1,0:T(8,128)(2,1)S(1)} %get-tuple-element.25), channel_id=1, source_target_pairs={{1,0},{5,4},{9,8},{13,12},{3,2},{7,6},{11,10},{15,14},{17,16},{21,... | collective-permute-start | bytes 12296 | tf_op jit(solution)/shard_map/ppermute | solution.py:373
  3.8 9.7 %collective-permute-start.2 = (bf16[1024,128]{1,0:T(8,128)(2,1)S(1)}, bf16[1024,128]{1,0:T(8,128)(2,1)S(1)}, u32[]{:S(2)}, u32[]{:S(2)}) collective-permute-start(bf16[1024,128]{1,0:T(8,128)(2,1)S(1)} %get-tuple-element.29), channel_id=1, source_target_pairs={{1,5},{13,9},{3,7},{15,11},{17,21},{29,25},{19,23},{31,27}} | collective-permute-start | bytes 786440 | tf_op jit(solution)/shard_map/ppermute | solution.py:368
  4.5 9.0 %collective-permute-start.3 = (bf16[1024,128]{1,0:T(8,128)(2,1)S(1)}, bf16[1024,128]{1,0:T(8,128)(2,1)S(1)}, u32[]{:S(2)}, u32[]{:S(2)}) collective-permute-start(bf16[1024,128]{1,0:T(8,128)(2,1)S(1)} %get-tuple-element.30), channel_id=1, source_target_pairs={{5,9},{9,5},{7,11},{11,7},{21,25},{25,21},{23,27},{27,23}} | collective-permute-start | bytes 786440 | tf_op jit(solution)/shard_map/ppermute | solution.py:368
  9.3 6.8 %collective-permute-start.4 = (bf16[1024,128]{1,0:T(8,128)(2,1)S(1)}, bf16[1024,128]{1,0:T(8,128)(2,1)S(1)}, u32[]{:S(2)}, u32[]{:S(2)}) collective-permute-start(bf16[1024,128]{1,0:T(8,128)(2,1)S(1)} %get-tuple-element.31), channel_id=1, source_target_pairs={{0,4},{12,8},{2,6},{14,10},{16,20},{28,24},{18,22},{30,26}} | collective-permute-start | bytes 786440 | tf_op jit(solution)/shard_map/ppermute | solution.py:368
  10.6 8.4 %collective-permute-start.5 = (bf16[1024,128]{1,0:T(8,128)(2,1)S(1)}, bf16[1024,128]{1,0:T(8,128)(2,1)S(1)}, u32[]{:S(2)}, u32[]{:S(2)}) collective-permute-start(bf16[1024,128]{1,0:T(8,128)(2,1)S(1)} %get-tuple-element.32), channel_id=1, source_target_pairs={{0,8},{12,4},{2,10},{14,6},{16,24},{28,20},{18,26},{30,22}} | collective-permute-start | bytes 786440 | tf_op jit(solution)/shard_map/ppermute | solution.py:368
  12.8 6.2 %collective-permute-start.6 = (bf16[1024,128]{1,0:T(8,128)(2,1)S(1)}, bf16[1024,128]{1,0:T(8,128)(2,1)S(1)}, u32[]{:S(2)}, u32[]{:S(2)}) collective-permute-start(bf16[1024,128]{1,0:T(8,128)(2,1)S(1)} %get-tuple-element.33), channel_id=1, source_target_pairs={{4,8},{8,4},{6,10},{10,6},{20,24},{24,20},{22,26},{26,22}} | collective-permute-start | bytes 786440 | tf_op jit(solution)/shard_map/ppermute | solution.py:368
  19.0 14.4 %collective-permute-start.7 = (bf16[1024,128]{1,0:T(8,128)(2,1)S(1)}, bf16[1024,128]{1,0:T(8,128)(2,1)S(1)}, u32[]{:S(2)}, u32[]{:S(2)}) collective-permute-start(bf16[1024,128]{1,0:T(8,128)(2,1)S(1)} %get-tuple-element.35), channel_id=1, source_target_pairs={{4,0},{8,12},{5,1},{9,13},{6,2},{10,14},{7,3},{11,15},{20,16},{24,... | collective-permute-start | bytes 786440 | tf_op jit(solution)/shard_map/ppermute | solution.py:365
  20.3 13.1 %collective-permute-start.8 = (bf16[1024,128]{1,0:T(8,128)(2,1)S(1)}, bf16[1024,128]{1,0:T(8,128)(2,1)S(1)}, u32[]{:S(2)}, u32[]{:S(2)}) collective-permute-start(bf16[1024,128]{1,0:T(8,128)(2,1)S(1)} %get-tuple-element.36), channel_id=1, source_target_pairs={{4,12},{8,0},{5,13},{9,1},{6,14},{10,2},{7,15},{11,3},{20,28},{24,... | collective-permute-start | bytes 786440 | tf_op jit(solution)/shard_map/ppermute | solution.py:365
  21.6 11.8 %collective-permute-start.9 = (bf16[1024,128]{1,0:T(8,128)(2,1)S(1)}, bf16[1024,128]{1,0:T(8,128)(2,1)S(1)}, u32[]{:S(2)}, u32[]{:S(2)}) collective-permute-start(bf16[1024,128]{1,0:T(8,128)(2,1)S(1)} %get-tuple-element.37), channel_id=1, source_target_pairs={{4,8},{8,4},{5,9},{9,5},{6,10},{10,6},{7,11},{11,7},{20,24},{24,20... | collective-permute-start | bytes 786440 | tf_op jit(solution)/shard_map/ppermute | solution.py:365
